TPU v7x, 32 devices: a whole 2x2x4 slice. The times are simulated.
32 devices in a mesh: ens: 2 (over y), row: 4 (over z), col: 2 (over x), chan: 2 (over core).
Axes of the slice: x: 2, y: 2, z: 4, core: 2. Of those that a mesh axis runs over, the one named last changes fastest.
Arguments:
- latent: float32 [4, 12, 32, 256], P('ens', None, 'row', 'col'), parts along dimension 0, may hold values from -6 to 6
- fresh_noise: float32 [4, 12, 32, 256], P('ens', None, 'row', 'col'), parts along dimension 0, may hold values from -6 to 6
- step_index: int32 [4], P('ens'), parts along dimension 0, may hold values from 0 to 11
- coarse: float32 [24, 4, 32], P('ens', None, 'col'), parts along dimension 0, may hold values from -6 to 6
- weight_in: bfloat16 [9, 256, 24], replicated, may hold values from -0.4375 to 0.4375
- bias_in: float32 [256], replicated, may hold values from -4 to 4
- weight_noise: float32 [256], replicated, may hold values from -4 to 4
- weight_mid: bfloat16 [9, 256, 256], P(None, 'chan'), may hold values from -0.125 to 0.125
- bias_mid: float32 [256], P('chan'), may hold values from -4 to 4
- weight_out: bfloat16 [12, 256], P(None, 'chan'), may hold values from -0.375 to 0.375
Outputs:
- fine_field: float32 [4, 12, 32, 256], P('ens', None, 'row', 'col'), parts along dimension 0
- next_latent: float32 [4, 12, 32, 256], P('ens', None, 'row', 'col'), parts along dimension 0
There are 2 independent parts, one for each index of `ens`. A program takes and returns all parts, laid end to end along the dimension named above; an argument that names none is the same for every part. Nothing has to cross between parts.
Inputs may be any that keep to these rules, and one draw needn't show every extreme that they name: `step_index`: each sample's position in the noise plan of 18 steps.
All inputs are finite; a program needn't handle non-finite values.
Results may differ from a plain program's by a relative error of at most 0.0024.
Values may be sent and summed in bfloat16 or wider, within the bound.
No kernel may reach another device: no remote copies, remote signals or barrier semaphores. Data moves between devices by JAX's collectives and lax.ppermute only.
A program may use at most 64 MiB of HBM per device.

v0:
```python
import jax
import jax.numpy as jnp
from jax import lax
from jax.sharding import PartitionSpec as P

STEPS = 18
FACTOR = 8


sigma_data = 0.5
sigma_high = 80.0
sigma_low = 0.002
rho_power = 7.0


def extended_2(value, sides, width):
    for axis, dim in sides:
        count, length = (lax.axis_size(axis), value.shape[dim])
        up = [(i, (i + 1) % count) for i in range(count - 1)]
        down = [(j, i) for i, j in up]
        last = lax.slice_in_dim(value, length - width, length, axis=dim)
        initial = lax.slice_in_dim(value, 0, width, axis=dim)
        before = lax.ppermute(last, axis, up)
        after = lax.ppermute(initial, axis, down)
        value = jnp.concatenate([before, value, after], axis=dim)
    return value


def blend_matrix(fine_index, coarse_index, coarse_count, factor):
    twice_pos = 2 * fine_index + 1 - factor
    lower_cell = twice_pos // (2 * factor)
    fraction = (twice_pos - lower_cell * 2 * factor).astype(jnp.float32) / (2.0 * factor)
    before = lower_cell < 0
    fraction = jnp.where(before, 0.0, fraction)
    lower_clip = jnp.clip(lower_cell, 0, coarse_count - 1)
    upper_clip = jnp.clip(lower_cell + 1, 0, coarse_count - 1)
    lower_hit = (lower_clip[:, None] == coarse_index[None, :]).astype(jnp.float32)
    upper_hit = (upper_clip[:, None] == coarse_index[None, :]).astype(jnp.float32)
    return (1.0 - fraction)[:, None] * lower_hit + fraction[:, None] * upper_hit


def noise_level(position):
    top_root = sigma_high ** (1.0 / rho_power)
    bottom_root = sigma_low ** (1.0 / rho_power)
    along = position.astype(jnp.float32) / (STEPS - 1)
    return (top_root + along * (bottom_root - top_root)) ** rho_power


def conv_valid(source, weight, out_rows, out_cols):
    total = None
    for offset_row in range(3):
        for offset_col in range(3):
            window = source[
                :, :, offset_row : offset_row + out_rows, offset_col : offset_col + out_cols
            ]
            term = jnp.einsum(
                "oi,siyx->soyx",
                weight[3 * offset_row + offset_col],
                window,
                preferred_element_type=jnp.float32,
            )
            total = term if total is None else total + term
    return total


def on_device(
    latent,
    fresh_noise,
    step_index,
    coarse,
    weight_in,
    bias_in,
    weight_noise,
    weight_mid,
    bias_mid,
    weight_out,
):
    samples, channels, rows_here, cols_here = latent.shape
    row_place = lax.axis_index("row")
    col_place = lax.axis_index("col")
    height = lax.axis_size("row") * rows_here
    width = lax.axis_size("col") * cols_here
    coarse_rows = coarse.shape[1]
    local_cols = coarse.shape[2]
    coarse_cols = lax.axis_size("col") * local_cols
    widened = extended_2(coarse, (("col", 2),), 1)
    rows_matrix = blend_matrix(
        row_place * rows_here + jnp.arange(rows_here, dtype=jnp.int32),
        jnp.arange(coarse_rows, dtype=jnp.int32),
        coarse_rows,
        FACTOR,
    )
    cols_matrix = blend_matrix(
        col_place * cols_here + jnp.arange(cols_here, dtype=jnp.int32),
        col_place * local_cols - 1 + jnp.arange(local_cols + 2, dtype=jnp.int32),
        coarse_cols,
        FACTOR,
    )
    mean_up = jnp.einsum(
        "yh,khw,xw->kyx", rows_matrix, widened, cols_matrix, precision=lax.Precision.HIGHEST
    )
    noise_now = noise_level(step_index)
    noise_next = noise_level(step_index + 1)
    inputs = jnp.concatenate(
        [latent, jnp.broadcast_to(mean_up[None], (samples,) + mean_up.shape)], axis=1
    ).astype(jnp.bfloat16)
    conditioning = (
        bias_in[None, :, None, None]
        + (jnp.log(noise_now) / 4.0)[:, None, None, None] * weight_noise[None, :, None, None]
    )
    mid_full, out_full = (
        lax.all_gather(weight_mid, "chan", axis=1, tiled=True),
        lax.all_gather(weight_out, "chan", axis=1, tiled=True),
    )
    bias_full = lax.all_gather(bias_mid, "chan", axis=0, tiled=True)
    half_cols = cols_here // lax.axis_size("chan")
    chan_place = lax.axis_index("chan")
    extended = extended_2(inputs, (("row", 2), ("col", 3)), 2)
    source = lax.dynamic_slice_in_dim(extended, chan_place * half_cols, half_cols + 4, 3)
    hidden = jax.nn.silu(conv_valid(source, weight_in, rows_here + 2, half_cols + 2) + conditioning)
    global_rows = row_place * rows_here - 1 + jnp.arange(rows_here + 2, dtype=jnp.int32)
    global_cols = (
        col_place * cols_here
        + chan_place * half_cols
        - 1
        + jnp.arange(half_cols + 2, dtype=jnp.int32)
    )
    inside = ((global_rows >= 0) & (global_rows < height))[:, None] & (
        (global_cols >= 0) & (global_cols < width)
    )[None, :]
    hidden_wide = jnp.where(inside, hidden, 0.0).astype(jnp.bfloat16)
    middle = jax.nn.silu(
        conv_valid(hidden_wide, mid_full, rows_here, half_cols) + bias_full[None, :, None, None]
    ).astype(jnp.bfloat16)
    half_network = jnp.einsum("ko,soyx->skyx", out_full, middle, preferred_element_type=jnp.float32)
    network = lax.all_gather(half_network, "chan", axis=3, tiled=True)
    scale_now = jnp.sqrt(noise_now * noise_now + sigma_data * sigma_data)
    skip_coef = sigma_data * sigma_data / (noise_now * noise_now + sigma_data * sigma_data)
    out_coef = sigma_data * noise_now / scale_now
    denoised = (skip_coef * scale_now)[:, None, None, None] * latent + out_coef[
        :, None, None, None
    ] * network
    fine_field = mean_up[None] + denoised
    scale_next = jnp.sqrt(noise_next * noise_next + sigma_data * sigma_data)
    next_latent = (denoised + noise_next[:, None, None, None] * fresh_noise) / scale_next[
        :, None, None, None
    ]
    return (fine_field, next_latent)


def solution(mesh):
    in_specs = (
        P("ens", None, "row", "col"),
        P("ens", None, "row", "col"),
        P("ens"),
        P("ens", None, "col"),
        P(),
        P(),
        P(),
        P(None, "chan", None),
        P("chan"),
        P(None, "chan"),
    )
    out_specs = (P("ens", None, "row", "col"), P("ens", None, "row", "col"))
    return jax.shard_map(
        on_device, mesh=mesh, in_specs=in_specs, out_specs=out_specs, check_vma=False
    )
```

profile of v0, /device:TPU:0, one launch (start us, length us, event | category | flops | bytes accessed | tf_op | source)
XLA Modules:
  0.0 60.4 jit_solution(1089614030091482770)
XLA Ops:
  7.2 0.0 copy-start.5
  7.2 0.0 copy-start.4
  7.2 0.0 all-gather.3.cloned.1.call-start
  7.2 0.7 %copy.29 = f32[12,4,16]{2,0,1:T(8,128)S(1)} copy(f32[12,4,16]{2,1,0:T(4,128)} %param.13) | data formatting | bytes 6144 | tf_op args[3]
  8.0 0.1 fusion.95
  8.0 4.9 %collective-permute-start = (f32[12,4,1]{2,0,1:T(8,128)S(1)}, f32[12,4,1]{2,0,1:T(8,128)S(1)}, u32[]{:S(2)}, u32[]{:S(2)}) collective-permute-start(f32[12,4,1]{2,0,1:T(8,128)S(1)} %get-tuple-element.23), channel_id=1, source_target_pairs={{0,2},{1,3},{4,6},{5,7},{8,10},{9,11},{12,14},{13,15},{16,18},{17,... | collective-permute-start | bytes 584 | tf_op jit(solution)/shard_map/ppermute | solution.py:23
  12.9 1.3 %collective-permute-start.1 = (f32[12,4,1]{2,0,1:T(8,128)S(1)}, f32[12,4,1]{2,0,1:T(8,128)S(1)}, u32[]{:S(2)}, u32[]{:S(2)}) collective-permute-start(f32[12,4,1]{2,0,1:T(8,128)S(1)} %get-tuple-element.24), channel_id=1, source_target_pairs={{2,0},{3,1},{6,4},{7,5},{10,8},{11,9},{14,12},{15,13},{18,16},{19,... | collective-permute-start | bytes 584 | tf_op jit(solution)/shard_map/ppermute | solution.py:24
  14.2 0.0 all-gather.3.cloned.1.call-update
  14.4 0.8 %add_sqrt_fusion = (f32[2]{0:T(128)S(1)}, f32[2]{0:T(128)S(1)}, f32[2]{0:T(128)S(1)}, f32[2]{0:T(128)S(1)}, f32[2]{0:T(128)S(1)}) fusion(s32[2]{0:T(128)} %param.12), kind=kLoop, calls=%fused_computation.139 | loop fusion | flops 34 | bytes 48 | tf_op jit(solution)/shard_map/sqrt | solution.py:144
  15.1 0.8 %multiply_add_fusion.1 = f32[2,256]{1,0:T(2,128)S(1)} fusion(f32[256]{0:T(256)} %param.16, f32[256]{0:T(256)} %param.15, f32[2]{0:T(128)S(1)} %get-tuple-element.25), kind=kLoop, calls=%fused_computation.115 | loop fusion | flops 1024 | bytes 4104 | tf_op jit(solution)/shard_map/add | solution.py:108
  15.9 0.9 %convert.7 = bf16[2,12,8,128]{3,2,1,0:T(8,128)(2,1)S(1)} convert(f32[2,12,8,128]{3,2,1,0:T(8,128)} %param.10) | non-fusion elementwise | flops 24576 | bytes 147456 | tf_op jit(solution)/shard_map/convert
  16.8 0.0 collective-permute-done
  16.8 1.9 %collective-permute-done.1 = f32[12,4,1]{2,0,1:T(8,128)S(1)} collective-permute-done((f32[12,4,1]{2,0,1:T(8,128)S(1)}, f32[12,4,1]{2,0,1:T(8,128)S(1)}, u32[]{:S(2)}, u32[]{:S(2)}) %collective-permute-start.1) | collective-permute-done | bytes 224 | tf_op jit(solution)/shard_map/ppermute | solution.py:24
  18.7 0.2 fusion.42
  19.0 0.2 fusion.96
  19.3 3.5 %collective-permute-start.2 = (bf16[2,24,2,128]{3,2,1,0:T(2,128)(2,1)S(1)}, bf16[2,24,2,128]{3,2,1,0:T(2,128)(2,1)S(1)}, u32[]{:S(2)}, u32[]{:S(2)}) collective-permute-start(bf16[2,24,2,128]{3,2,1,0:T(2,128)(2,1)S(1)} %get-tuple-element.21), channel_id=1, source_target_pairs={{0,4},{4,8},{8,12},{1,5},{5,9},{9,13},{2,6},{6,10},{10,14},{3,7},{... | collective-permute-start | bytes 73736 | tf_op jit(solution)/shard_map/ppermute | solution.py:23
  22.8 1.3 %collective-permute-start.3 = (bf16[2,24,2,128]{3,2,1,0:T(2,128)(2,1)S(1)}, bf16[2,24,2,128]{3,2,1,0:T(2,128)(2,1)S(1)}, u32[]{:S(2)}, u32[]{:S(2)}) collective-permute-start(bf16[2,24,2,128]{3,2,1,0:T(2,128)(2,1)S(1)} %get-tuple-element.22), channel_id=1, source_target_pairs={{4,0},{8,4},{12,8},{5,1},{9,5},{13,9},{6,2},{10,6},{14,10},{7,3},{... | collective-permute-start | bytes 73736 | tf_op jit(solution)/shard_map/ppermute | solution.py:24
  24.1 0.2 collective-permute-done.2
  24.3 4.2 %collective-permute-done.3 = bf16[2,24,2,128]{3,2,1,0:T(2,128)(2,1)S(1)} collective-permute-done((bf16[2,24,2,128]{3,2,1,0:T(2,128)(2,1)S(1)}, bf16[2,24,2,128]{3,2,1,0:T(2,128)(2,1)S(1)}, u32[]{:S(2)}, u32[]{:S(2)}) %collective-permute-start.3) | collective-permute-done | bytes 24608 | tf_op jit(solution)/shard_map/ppermute | solution.py:24
  28.5 0.1 pad_maximum_fusion
  28.6 0.1 fusion.94
  28.7 2.6 %collective-permute-start.4 = (bf16[2,24,12,2]{3,2,1,0:T(8,128)(2,1)S(1)}, bf16[2,24,12,2]{3,2,1,0:T(8,128)(2,1)S(1)}, u32[]{:S(2)}, u32[]{:S(2)}) collective-permute-start(bf16[2,24,12,2]{3,2,1,0:T(8,128)(2,1)S(1)} %get-tuple-element.20), channel_id=1, source_target_pairs={{0,2},{1,3},{4,6},{5,7},{8,10},{9,11},{12,14},{13,15},{16,18},{17,... | collective-permute-start | bytes 6920 | tf_op jit(solution)/shard_map/ppermute | solution.py:23
  31.4 1.3 %collective-permute-start.5 = (bf16[2,24,12,2]{3,2,1,0:T(8,128)(2,1)S(1)}, bf16[2,24,12,2]{3,2,1,0:T(8,128)(2,1)S(1)}, u32[]{:S(2)}, u32[]{:S(2)}) collective-permute-start(bf16[2,24,12,2]{3,2,1,0:T(8,128)(2,1)S(1)} %get-tuple-element.19), channel_id=1, source_target_pairs={{2,0},{3,1},{6,4},{7,5},{10,8},{11,9},{14,12},{15,13},{18,16},{19,... | collective-permute-start | bytes 6920 | tf_op jit(solution)/shard_map/ppermute | solution.py:24
  32.7 0.1 broadcast_and_fusion
  32.8 0.0 copy-done.5
  32.8 1.8 %all-gather = f32[2,1,128]{2,1,0:T(1,128)S(1)} all-gather(f32[1,1,128]{2,1,0:T(1,128)S(1)} %bitcast.167), channel_id=1, replica_groups=mesh['ens'=2,'row'=4,'col'=2,'chan'=2] {'chan'}, dimensions={0}, use_global_device_ids=true | all-gather | bytes 1536 | tf_op jit(solution)/shard_map/all_gather | solution.py:115
  34.6 0.0 copy-done.4
  34.6 1.8 %all_gather.14 = bf16[12,256]{1,0:T(8,128)(2,1)S(1)} all-gather(bf16[12,128]{1,0:T(8,128)(2,1)S(1)} %copy-done.4), channel_id=1, replica_groups=mesh['ens'=2,'row'=4,'col'=2,'chan'=2] {'chan'}, dimensions={1}, use_global_device_ids=true | all-gather | bytes 9216 | tf_op jit(solution)/shard_map/all_gather | solution.py:113
  36.4 0.0 collective-permute-done.4
  36.4 2.6 %collective-permute-done.5 = bf16[2,24,12,2]{3,2,1,0:T(8,128)(2,1)S(1)} collective-permute-done((bf16[2,24,12,2]{3,2,1,0:T(8,128)(2,1)S(1)}, bf16[2,24,12,2]{3,2,1,0:T(8,128)(2,1)S(1)}, u32[]{:S(2)}, u32[]{:S(2)}) %collective-permute-start.5) | collective-permute-done | bytes 2336 | tf_op jit(solution)/shard_map/ppermute | solution.py:24
  39.0 0.6 %fusion.21 = bf16[2,24,12,68]{3,2,1,0:T(8,128)(2,1)S(1)} fusion(s32[]{:T(128)S(6)} %select_n.69, bf16[2,24,12,2]{3,2,1,0:T(8,128)(2,1)S(1)} %collective-permute-done.4, bf16[2,24,2,128]{3,2,1,0:T(2,128)(2,1)S(1)} %collective-permute-done.2, bf16[2,12,8,128]{3,2,1,0:T(8,128)(2,1)S(1)} %convert.7, bf16[2,12,8,128]{3,2,1,0:T(8,128)(2,1)S(1)} %add.314, ...), kind=kLoop, calls=%fused_computation.39 | loop fusion | flops 470016 | bytes 230404 | tf_op jit(solution)/shard_map/concatenate | solution.py:25
  39.6 0.0 copy-start.2
  39.6 0.5 fusion.93
  40.1 0.4 copy-done.2
  40.5 0.4 fusion.26
  40.9 0.4 fusion.28
  41.3 0.4 fusion.30
  41.7 0.4 fusion.32
  42.1 0.4 fusion.34
  42.5 0.4 fusion.36
  42.9 0.4 fusion.38
  43.3 0.4 fusion.40
  43.7 1.0 %fusion.4 = bf16[2,256,10,66]{1,3,2,0:T(8,128)(2,1)S(1)} fusion(f32[2,10,66,256]{3,2,1,0:T(8,128)S(1)} %fusion.26, f32[2,10,66,256]{3,2,1,0:T(8,128)S(1)} %fusion.28, f32[2,10,66,256]{3,2,1,0:T(8,128)S(1)} %fusion.30, f32[2,10,66,256]{3,2,1,0:T(8,128)S(1)} %fusion.32, f32[2,10,66,256]{3,2,1,0:T(8,128)S(1)} %fusion.34, f32[2,10,66,256]{3,2,1,0:T(8,128)S(1)} %fusion.36, ...), kind=kOutput, calls=%fused_computation.6 | convolution fusion | flops 21288960 | bytes 12685312 | tf_op jit(solution)/shard_map/oi,siyx->soyx/dot_general | solution.py:56
  44.8 0.0 all-gather.3.cloned.1.call-done
  44.8 0.0 copy-start
  44.8 1.3 %fusion.16 = f32[2,8,64,256]{3,2,1,0:T(8,128)S(1)} fusion(bf16[2,256,10,66]{1,3,2,0:T(8,128)(2,1)S(1)} %fusion.4, bf16[9,256,256]{2,1,0:T(8,128)(2,1)} %all-gather.3.cloned.1.call-done), kind=kOutput, calls=%fused_computation.28 | convolution fusion | flops 134217728 | bytes 1703936 | tf_op jit(solution)/shard_map/oi,siyx->soyx/dot_general | solution.py:56
  46.2 0.0 copy-done
  46.2 0.3 convolution_add_fusion.7
  46.5 0.4 convolution_add_fusion.6
  46.9 0.3 convolution_add_fusion.5
  47.2 0.4 convolution_add_fusion.4
  47.6 0.3 convolution_add_fusion.3
  47.9 0.3 convolution_add_fusion.2
  48.3 0.4 convolution_add_fusion.1
  48.6 0.7 %convolution_bitcast_fusion = f32[2,12,8,64]{3,1,2,0:T(8,128)S(1)} fusion(f32[2,8,64,256]{3,2,1,0:T(8,128)S(1)} %convolution_add_fusion.1, bf16[2,256,10,66]{1,3,2,0:T(8,128)(2,1)S(1)} %fusion.4, f32[256]{0:T(256)S(1)} %bitcast.168, bf16[9,256,256]{2,1,0:T(8,128)(2,1)S(1)} %copy-done, bf16[12,256]{1,0:T(8,128)(2,1)S(1)} %all_gather.14), kind=kOutput, calls=%fused_computation.17 | convolution fusion | flops 142344192 | bytes 1762304 | tf_op jit(solution)/shard_map/ko,soyx->skyx/dot_general | solution.py:135
  49.3 0.3 copy.42
  49.7 0.0 copy-start.1
  49.7 0.0 copy-start.3
  49.7 2.7 %all_gather.15 = f32[2,12,8,128]{1,2,0,3:T(8,128)S(1)} all-gather(f32[2,12,8,64]{1,2,0,3:T(8,128)S(1)} %copy.42), channel_id=1, replica_groups=mesh['ens'=2,'row'=4,'col'=2,'chan'=2] {'chan'}, dimensions={3}, use_global_device_ids=true | all-gather | bytes 147456 | tf_op jit(solution)/shard_map/all_gather | solution.py:136
  52.4 0.4 copy.43
  52.8 0.0 copy-done.1
  52.8 0.0 copy-done.3
  52.8 0.8 %add_divide_fusion = (f32[2,12,8,128]{3,2,1,0:T(8,128)}, f32[2,12,8,128]{3,2,1,0:T(8,128)}) fusion(f32[2,12,8,128]{3,2,1,0:T(8,128)S(1)} %copy-done.3, f32[2]{0:T(128)S(1)} %get-tuple-element.6, f32[2]{0:T(128)S(1)} %get-tuple-element.7, f32[2,12,8,128]{3,2,1,0:T(8,128)S(1)} %copy.43, f32[2]{0:T(128)S(1)} %get-tuple-element.26, ...), kind=kLoop, calls=%fused_computation.70 | loop fusion | flops 172032 | bytes 540704 | tf_op jit(solution)/shard_map/div | solution.py:145
  (9 shorter events, 0.1 us)
Async XLA Ops:
  7.2 25.6 %copy-start.5 = (f32[128]{0:T(128)S(1)}, f32[128]{0:T(128)}, u32[]{:S(2)}) copy-start(f32[128]{0:T(128)} %param.18) | copy-start | bytes 1540
  7.2 27.4 %copy-start.4 = (bf16[12,128]{1,0:T(8,128)(2,1)S(1)}, bf16[12,128]{1,0:T(8,128)(2,1)}, u32[]{:S(2)}) copy-start(bf16[12,128]{1,0:T(8,128)(2,1)} %param.19) | copy-start | bytes 9220
  7.2 37.6 %all-gather.3.cloned.1.call-start = ((), (), s32[]{:S(2)}) async-start(), calls=%async_computation | async-start | bytes 1769472 | tf_op jit(solution)/shard_map/all_gather | solution.py:112
  8.0 8.8 %collective-permute-start = (f32[12,4,1]{2,0,1:T(8,128)S(1)}, f32[12,4,1]{2,0,1:T(8,128)S(1)}, u32[]{:S(2)}, u32[]{:S(2)}) collective-permute-start(f32[12,4,1]{2,0,1:T(8,128)S(1)} %get-tuple-element.23), channel_id=1, source_target_pairs={{0,2},{1,3},{4,6},{5,7},{8,10},{9,11},{12,14},{13,15},{16,18},{17,... | collective-permute-start | bytes 584 | tf_op jit(solution)/shard_map/ppermute | solution.py:23
  12.9 5.8 %collective-permute-start.1 = (f32[12,4,1]{2,0,1:T(8,128)S(1)}, f32[12,4,1]{2,0,1:T(8,128)S(1)}, u32[]{:S(2)}, u32[]{:S(2)}) collective-permute-start(f32[12,4,1]{2,0,1:T(8,128)S(1)} %get-tuple-element.24), channel_id=1, source_target_pairs={{2,0},{3,1},{6,4},{7,5},{10,8},{11,9},{14,12},{15,13},{18,16},{19,... | collective-permute-start | bytes 584 | tf_op jit(solution)/shard_map/ppermute | solution.py:24
  19.3 5.0 %collective-permute-start.2 = (bf16[2,24,2,128]{3,2,1,0:T(2,128)(2,1)S(1)}, bf16[2,24,2,128]{3,2,1,0:T(2,128)(2,1)S(1)}, u32[]{:S(2)}, u32[]{:S(2)}) collective-permute-start(bf16[2,24,2,128]{3,2,1,0:T(2,128)(2,1)S(1)} %get-tuple-element.21), channel_id=1, source_target_pairs={{0,4},{4,8},{8,12},{1,5},{5,9},{9,13},{2,6},{6,10},{10,14},{3,7},{... | collective-permute-start | bytes 73736 | tf_op jit(solution)/shard_map/ppermute | solution.py:23
  22.8 5.7 %collective-permute-start.3 = (bf16[2,24,2,128]{3,2,1,0:T(2,128)(2,1)S(1)}, bf16[2,24,2,128]{3,2,1,0:T(2,128)(2,1)S(1)}, u32[]{:S(2)}, u32[]{:S(2)}) collective-permute-start(bf16[2,24,2,128]{3,2,1,0:T(2,128)(2,1)S(1)} %get-tuple-element.22), channel_id=1, source_target_pairs={{4,0},{8,4},{12,8},{5,1},{9,5},{13,9},{6,2},{10,6},{14,10},{7,3},{... | collective-permute-start | bytes 73736 | tf_op jit(solution)/shard_map/ppermute | solution.py:24
  28.7 7.7 %collective-permute-start.4 = (bf16[2,24,12,2]{3,2,1,0:T(8,128)(2,1)S(1)}, bf16[2,24,12,2]{3,2,1,0:T(8,128)(2,1)S(1)}, u32[]{:S(2)}, u32[]{:S(2)}) collective-permute-start(bf16[2,24,12,2]{3,2,1,0:T(8,128)(2,1)S(1)} %get-tuple-element.20), channel_id=1, source_target_pairs={{0,2},{1,3},{4,6},{5,7},{8,10},{9,11},{12,14},{13,15},{16,18},{17,... | collective-permute-start | bytes 6920 | tf_op jit(solution)/shard_map/ppermute | solution.py:23
  31.4 7.6 %collective-permute-start.5 = (bf16[2,24,12,2]{3,2,1,0:T(8,128)(2,1)S(1)}, bf16[2,24,12,2]{3,2,1,0:T(8,128)(2,1)S(1)}, u32[]{:S(2)}, u32[]{:S(2)}) collective-permute-start(bf16[2,24,12,2]{3,2,1,0:T(8,128)(2,1)S(1)} %get-tuple-element.19), channel_id=1, source_target_pairs={{2,0},{3,1},{6,4},{7,5},{10,8},{11,9},{14,12},{15,13},{18,16},{19,... | collective-permute-start | bytes 6920 | tf_op jit(solution)/shard_map/ppermute | solution.py:24
  39.6 0.9 %copy-start.2 = (bf16[9,256,24]{1,2,0:T(8,128)(2,1)S(1)}, bf16[9,256,24]{1,2,0:T(8,128)(2,1)}, u32[]{:S(2)}) copy-start(bf16[9,256,24]{1,2,0:T(8,128)(2,1)} %param.14) | copy-start | bytes 331780
  44.8 1.3 %copy-start = (bf16[9,256,256]{2,1,0:T(8,128)(2,1)S(1)}, bf16[9,256,256]{2,1,0:T(8,128)(2,1)}, u32[]{:S(2)}) copy-start(bf16[9,256,256]{2,1,0:T(8,128)(2,1)} %all-gather.3.cloned.1.call-done) | copy-start | bytes 3538948
  49.7 3.2 %copy-start.1 = (f32[2,12,8,128]{3,2,1,0:T(8,128)S(1)}, f32[2,12,8,128]{3,2,1,0:T(8,128)}, u32[]{:S(2)}) copy-start(f32[2,12,8,128]{3,2,1,0:T(8,128)} %param.10) | copy-start | bytes 294916
  49.7 3.1 %copy-start.3 = (f32[2,12,8,128]{3,2,1,0:T(8,128)S(1)}, f32[2,12,8,128]{3,2,1,0:T(8,128)}, u32[]{:S(2)}) copy-start(f32[2,12,8,128]{3,2,1,0:T(8,128)} %param.11) | copy-start | bytes 294916
Sparse Core Ops, SparseCore 0:
  14.4 11.6 all-gather.2
where the time goes:
time: 60.9 us; the launch traced here: 60.4 us
  starting transfers between devices  14.9 us (24%)
  between operations  14.4 us (24%)
  matrix products  9.14 us (15%)
  waiting for transfers between devices  8.92 us (15%)
  blocking collectives  6.31 us (10%)
  other arithmetic  4.14 us (7%)
  local copies, waits for them, and re-layouts  2.63 us (4%)
    ppermute x3, starting transfers between devices, extended_2(): before = lax.ppermute(last, axis, up)  11 us
    ppermute x3, waiting for transfers between devices, extended_2(): after = lax.ppermute(initial, axis, down)  8.69 us
    dot_general x17, matrix products, conv_valid(): jnp.einsum('oi,siyx->soyx', weight[3 * offset_row + offset_col], window,...  7.96 us
    ppermute x3, starting transfers between devices, extended_2(): after = lax.ppermute(initial, axis, down)  3.88 us
    all_gather x1, blocking collectives, on_device(): network = lax.all_gather(half_network, 'chan', axis=3, tiled=True)  2.69 us
    all_gather x1, blocking collectives, on_device(): lax.all_gather(weight_out, 'chan', axis=1, tiled=True)  1.83 us
    all_gather x1, blocking collectives, on_device(): bias_full = lax.all_gather(bias_mid, 'chan', axis=0, tiled=True)  1.8 us
  transfers between devices with their start and end apart: 7, of which 4 were waited for; matrix products, arithmetic and copies ran while one was open for 14% of the time, Pallas kernels for 0%

commit v1 on v0

v1 whole, which is shorter than its diff:
```python
import functools

import jax
import jax.numpy as jnp
from jax import lax
from jax.experimental import pallas as pl
from jax.experimental.pallas import tpu as pltpu
from jax.sharding import PartitionSpec as P

STEPS = 18
FACTOR = 8

sigma_data = 0.5
sigma_high = 80.0
sigma_low = 0.002
rho_power = 7.0

F32 = jnp.float32
BF16 = jnp.bfloat16
LANES = 128
CPAD = 16


def lane_index(rows):
    return lax.broadcasted_iota(jnp.int32, (rows, LANES), 1)


def noise_level(position):
    top_root = sigma_high ** (1.0 / rho_power)
    bottom_root = sigma_low ** (1.0 / rho_power)
    root = top_root + position * (1.0 / (STEPS - 1)) * (bottom_root - top_root)
    square = root * root
    return square * square * square * root


def silu(value):
    half = 0.5 * value
    return half + half * jnp.tanh(half)


def three_terms(value):
    high = value.astype(BF16).astype(F32)
    rest = value - high
    mid = rest.astype(BF16).astype(F32)
    return high, mid, (rest - mid).astype(BF16).astype(F32)


def pack_kernel(dims, latent, coarse, weight_out, bias_mid, rows_out, shared_out, *side_outs):
    samples, channels, rows, cols = latent.shape
    coarse_rows, local_cols = coarse.shape[1:]
    count = dims["col"]
    col_place = lax.axis_index("col")
    lower = lax.axis_index("chan") == 1
    for near in range(2):
        for s in range(samples):
            first = latent[s, :, near, :]
            last = latent[s, :, rows - 2 + near, :]
            rows_out[near * samples + s, 0:channels, :] = jnp.where(lower, first, last).astype(BF16)
            rows_out[near * samples + s, channels:CPAD, :] = jnp.zeros(
                (CPAD - channels, LANES), BF16
            )
    shared_out[0:channels, :] = weight_out[...].astype(F32)
    shared_out[channels : channels + 1, :] = bias_mid[...]
    shared_out[channels + 1 : CPAD, :] = jnp.zeros((CPAD - channels - 1, LANES), F32)
    lane = lane_index(channels)
    sums = [jnp.zeros((channels, LANES), F32) for _ in side_outs]
    for s in range(samples):
        for y in range(rows):
            row = latent[s, :, y, :]
            place = 2 * (s * rows + y)
            right = pltpu.roll(row, (place + 2) % LANES, 1)
            left = row if place == 0 else pltpu.roll(row, place, 1)
            if count > 2:
                values = (right, left)
            else:
                values = (jnp.where(col_place == 0, right, left),)
            hit = (lane == place) | (lane == place + 1)
            sums = [jnp.where(hit, v, t) for v, t in zip(values, sums)]
    base = 2 * samples * rows
    for h in range(coarse_rows):
        line = coarse[:, h, :]
        right = jnp.broadcast_to(line[:, local_cols - 1 : local_cols], (channels, LANES))
        left = jnp.broadcast_to(line[:, 0:1], (channels, LANES))
        if count > 2:
            values = (right, left)
        else:
            values = (jnp.where(col_place == 0, right, left),)
        sums = [jnp.where(lane == base + h, v, t) for v, t in zip(values, sums)]
    for out, total in zip(side_outs, sums):
        out[0:channels, :] = total
        out[channels:CPAD, :] = jnp.zeros((CPAD - channels, LANES), F32)


def blend(target, index, size):
    twice = 2.0 * target + (1.0 - FACTOR)
    lower = jnp.floor(twice * (1.0 / (2 * FACTOR)))
    fraction = (twice - lower * (2.0 * FACTOR)) * (1.0 / (2 * FACTOR))
    fraction = jnp.where(lower < 0.0, 0.0, fraction)
    low = jnp.clip(lower, 0.0, size - 1.0)
    high = jnp.clip(lower + 1.0, 0.0, size - 1.0)
    return jnp.where(low == index, 1.0 - fraction, 0.0) + jnp.where(high == index, fraction, 0.0)


def row_weight(row, h, size):
    twice = 2 * row + 1 - FACTOR
    lower = (twice + 2 * FACTOR) // (2 * FACTOR) - 1
    fraction = (twice - lower * 2 * FACTOR).astype(F32) * (1.0 / (2 * FACTOR))
    fraction = jnp.where(lower < 0, 0.0, fraction)
    low = jnp.clip(lower, 0, size - 1)
    high = jnp.clip(lower + 1, 0, size - 1)
    return jnp.where(low == h, 1.0 - fraction, 0.0) + jnp.where(high == h, fraction, 0.0)


def main_kernel(
    dims,
    steps,
    latent,
    coarse,
    weight_in,
    bias_in,
    weight_noise,
    own_mid,
    other_mid,
    own_shared,
    other_shared,
    rows_in,
    *rest,
):
    sides = rest[: dims["messages"]]
    corners = rest[dims["messages"] : 2 * dims["messages"]]
    net_out, mean_out, xs, zx, w1, ce, hs, tr = rest[2 * dims["messages"] :]
    samples, channels, rows, cols = latent.shape
    coarse_rows, local_cols = coarse.shape[1:]
    taps, hidden, deep = weight_in.shape
    half = rows // 2
    reach = half + 4
    height, width = dims["row"] * rows, dims["col"] * cols
    coarse_cols = dims["col"] * local_cols
    block = 3 * deep + 8
    row_place = lax.axis_index("row")
    col_place = lax.axis_index("col")
    place = lax.axis_index("chan")
    upper = place == 0
    start = row_place * rows + half * place - 2
    lane = lane_index(CPAD)
    even = lane % 2 == 0

    w1[...] = jnp.zeros(w1.shape, F32)
    for i in range(3):
        for j in range(3):
            at = i * block + j * deep
            w1[:, at : at + deep] = weight_in[3 * i + j].astype(F32)
    vectors = jnp.concatenate(
        [bias_in[...], weight_noise[...], jnp.zeros((LANES - 2, hidden), F32)], axis=0
    )
    columns = vectors.T
    bias_terms = three_terms(columns[:, 0:1])
    noise_terms = three_terms(columns[:, 1:2])
    for i in range(3):
        at = i * block + 3 * deep
        w1[:, at : at + 1] = bias_terms[i]
        for j in range(3 - i):
            w1[:, at + 1 + j : at + 2 + j] = noise_terms[i]

    for y in range(rows):
        for s in range(samples):
            xs[2 + y, s, 0:channels, :] = latent[s, :, y, :]
            xs[2 + y, s, channels:CPAD, :] = jnp.zeros((CPAD - channels, LANES), F32)
    for near in range(2):
        for s in range(samples):
            got = rows_in[near * samples + s].astype(F32)
            xs[near, s] = got
            xs[2 + rows + near, s] = got
    tile = {}
    for v in range(reach):
        row = start + v
        inside = (row >= 0) & (row < height)
        for s in range(samples):
            tile[s, v] = jnp.where(inside, xs[half * place + v, s], 0.0)

    lane_v = (lane // 2) % reach
    lane_row = start + lane_v
    row_ok = (lane_row >= 0) & (lane_row < height) & (lane < 2 * samples * reach)
    near_first = jnp.where(upper, 0, reach - 2)
    near_line = (lane_v >= near_first) & (lane_v < near_first + 2)

    def halo(side, corner, ok):
        shift = 2 * (reach - rows)
        from_side = jnp.where(
            upper,
            pltpu.roll(side, 4, 1),
            pltpu.roll(side, (4 - 2 * half) % LANES, 1),
        )
        from_corner = jnp.where(
            upper,
            pltpu.roll(corner, (4 - 2 * rows) % LANES, 1),
            pltpu.roll(corner, 2 * reach - 4, 1),
        )
        return jnp.where(row_ok & ok, jnp.where(near_line, from_corner, from_side), 0.0)

    from_left = halo(sides[0][...], corners[0][...], col_place > 0)
    from_right = halo(sides[-1][...], corners[-1][...], col_place < dims["col"] - 1)
    own = jnp.zeros((CPAD, LANES), F32)
    for s in range(samples):
        for v in range(reach):
            at = 2 * (s * reach + v)
            first = tile[s, v] if at == 0 else pltpu.roll(tile[s, v], at, 1)
            own = jnp.where(lane == at, first, own)
            own = jnp.where(lane == at + 1, pltpu.roll(tile[s, v], (at + 2) % LANES, 1), own)
    edge = (
        jnp.where(even, from_left, own),
        jnp.where(even, pltpu.roll(from_left, LANES - 1, 1), pltpu.roll(from_right, 1, 1)),
        jnp.where(even, own, from_right),
    )

    ce[...] = jnp.zeros(ce.shape, F32)
    base = 2 * samples * rows
    for h in range(coarse_rows):
        at = h * CPAD
        ce[at : at + channels, 0:local_cols] = coarse[:, h, :]
        left = jnp.broadcast_to(sides[0][:, base + h : base + h + 1], (CPAD, 1))
        right = jnp.broadcast_to(sides[-1][:, base + h : base + h + 1], (CPAD, 1))
        ce[at : at + CPAD, local_cols : local_cols + 1] = left
        ce[at : at + CPAD, local_cols + 1 : local_cols + 2] = right
    group = local_cols + 2
    high, mid, low = three_terms(ce[...])
    cells = (high + pltpu.roll(mid, group, 1) + pltpu.roll(low, 2 * group, 1)).astype(BF16)
    depth = lax.broadcasted_iota(jnp.int32, (LANES, LANES), 0)
    spot = depth % group
    index = col_place * local_cols + jnp.where(
        spot < local_cols, spot, jnp.where(spot == local_cols, -1, local_cols)
    )
    index = jnp.where(depth < 3 * group, index, -2).astype(F32)
    wide = lax.broadcasted_iota(jnp.int32, (LANES, LANES), 1)
    targets = [col_place * cols + wide - 1 + j for j in range(3)]
    targets += [
        col_place * cols + jnp.where(wide % 2 == 0, j - 2, cols - 1 + j) for j in range(3)
    ]
    cols_matrix = [
        jnp.where((t >= 0) & (t < width), blend(t.astype(F32), index, coarse_cols), 0.0)
        for t in targets
    ]
    cols_matrix = jnp.concatenate([m.astype(BF16) for m in cols_matrix], axis=1)
    spread = jnp.dot(cells, cols_matrix, preferred_element_type=F32)

    def mean_of(weights, j):
        total = None
        for h in range(coarse_rows):
            term = weights[h] * spread[h * CPAD : (h + 1) * CPAD, j * LANES : (j + 1) * LANES]
            total = term if total is None else total + term
        return total

    ones = jnp.ones((1, LANES), F32)
    level_terms = [
        three_terms(jnp.log(noise_level(ones * steps[s].astype(F32))) * 0.25)
        for s in range(samples)
    ]
    tails = [
        jnp.concatenate([ones, *level_terms[s], jnp.zeros((4, LANES), F32)], axis=0)
        for s in range(samples)
    ]
    means = {}
    for v in range(reach):
        row = start + v
        inside = (row >= 0) & (row < height)
        weights = [
            jnp.where(inside, row_weight(row, h, coarse_rows), 0.0) for h in range(coarse_rows)
        ]
        for j in range(3):
            means[v, j] = mean_of(weights, j)
    for y in range(rows):
        row = row_place * rows + y
        mean_out[y] = mean_of([row_weight(row, h, coarse_rows) for h in range(coarse_rows)], 1)
    lane_weights = [
        jnp.where(
            row_ok, blend(lane_row.astype(F32), float(h), coarse_rows), 0.0
        )
        for h in range(coarse_rows)
    ]
    edge_means = [mean_of(lane_weights, 3 + j) for j in range(3)]

    for s in range(samples):
        for v in range(reach):
            at = 2 * (s * reach + v)
            turned = pltpu.roll(edge[1], LANES - 1 - at, 1)
            here = tile[s, v]
            moved = (
                pltpu.roll(jnp.where(lane == LANES - 1, turned, here), 1, 1),
                here,
                pltpu.roll(jnp.where(lane == 0, turned, here), LANES - 1, 1),
            )
            for j in range(3):
                zx[s, v, j * deep : j * deep + channels, :] = moved[j][0:channels]
                zx[s, v, j * deep + channels : (j + 1) * deep, :] = means[v, j][0:channels]
            zx[s, v, 3 * deep : block, :] = tails[s]
    sample_of = lane_index(8) // (2 * reach)
    edge_tail = tails[0]
    for s in range(1, samples):
        edge_tail = jnp.where(sample_of == s, tails[s], edge_tail)
    edge_block = jnp.concatenate(
        sum([[edge[j][0:channels], edge_means[j][0:channels]] for j in range(3)], []) + [edge_tail],
        axis=0,
    )

    first_weight = w1[...].astype(BF16)
    stacked = jnp.concatenate(
        [edge_block, pltpu.roll(edge_block, LANES - 2, 1), pltpu.roll(edge_block, LANES - 4, 1)],
        axis=0,
    ).astype(BF16)
    edge_hidden = silu(jnp.dot(first_weight, stacked, preferred_element_type=F32))
    lane_h = lane_index(hidden)
    v_h = (lane_h // 2) % reach
    row_h = start + 1 + v_h
    side_h = col_place + lane_h % 2
    side_h = (side_h > 0) & (side_h < dims["col"])
    edge_hidden = jnp.where((row_h >= 0) & (row_h < height) & side_h, edge_hidden, 0.0)
    for s in range(samples):
        for v in range(0, half + 2, 2):
            pair = jnp.concatenate(
                [
                    jnp.concatenate([zx[s, v + e + i] for i in range(3)], axis=0).astype(BF16)
                    for e in range(2)
                ],
                axis=1,
            )
            value = silu(jnp.dot(first_weight, pair, preferred_element_type=F32))
            for e in range(2):
                row = start + 1 + v + e
                inside = (row >= 0) & (row < height)
                here = jnp.where(inside, value[:, e * LANES : (e + 1) * LANES], 0.0)
                at = 2 * (s * reach + v + e)
                turned = pltpu.roll(edge_hidden, LANES - 1 - at, 1)
                left = pltpu.roll(jnp.where(lane_h == LANES - 1, turned, here), 1, 1)
                right = pltpu.roll(jnp.where(lane_h == 0, turned, here), LANES - 1, 1)
                hs[0, s, v + e] = left.astype(BF16)
                hs[1, s, v + e] = here.astype(BF16)
                hs[2, s, v + e] = right.astype(BF16)

    tr[...] = jnp.zeros(tr.shape, F32)
    tr[0:CPAD] = own_shared[...]
    own_bias = tr[...].T[:, channels : channels + 1]
    tr[0:CPAD] = other_shared[...]
    other_bias = tr[...].T[:, channels : channels + 1]
    bias = jnp.concatenate([own_bias, other_bias], axis=0)
    out_weight = jnp.concatenate([own_shared[...], other_shared[...]], axis=1).astype(BF16)
    second_weight = jnp.concatenate(
        [
            jnp.concatenate([own_mid[t] for t in range(taps)], axis=1),
            jnp.concatenate([other_mid[t] for t in range(taps)], axis=1),
        ],
        axis=0,
    )
    for s in range(samples):
        for v in range(0, half, 2):
            stacked = jnp.concatenate(
                [
                    jnp.concatenate([hs[j, s, v + i], hs[j, s, v + 1 + i]], axis=1)
                    for i in range(3)
                    for j in range(3)
                ],
                axis=0,
            )
            value = jnp.dot(second_weight, stacked, preferred_element_type=F32)
            middle = silu(value + bias).astype(BF16)
            net = jnp.dot(out_weight, middle, preferred_element_type=F32)
            for e in range(2):
                net_out[s * half + v + e] = net[:, e * LANES : (e + 1) * LANES]
    del cols, place


def finish_kernel(steps, latent, fresh, own_net, other_net, own_mean, fine, following):
    samples, channels, rows, cols = latent.shape
    half = rows // 2
    upper = lax.axis_index("chan") == 0

    def joined(own, other, at):
        a = jnp.swapaxes(own[at : at + half], 0, 1)
        b = jnp.swapaxes(other[at : at + half], 0, 1)
        return jnp.concatenate([jnp.where(upper, a, b), jnp.where(upper, b, a)], axis=1)

    mean = jnp.swapaxes(own_mean[...], 0, 1)[0:channels]
    for s in range(samples):
        net = joined(own_net[...], other_net[...], s * half)[0:channels]
        step = jnp.full((1, 1, cols), 1.0, F32) * steps[s].astype(F32)
        now = noise_level(step)
        ahead = noise_level(step + 1.0)
        variance = now * now + sigma_data * sigma_data
        scale = jnp.sqrt(variance)
        skip = sigma_data * sigma_data / variance * scale
        gain = sigma_data * now / scale
        denoised = skip * latent[s] + gain * net
        fine[s] = mean + denoised
        inverse = 1.0 / jnp.sqrt(ahead * ahead + sigma_data * sigma_data)
        following[s] = (denoised + ahead * fresh[s]) * inverse


def on_device(
    dims,
    latent,
    fresh_noise,
    step_index,
    coarse,
    weight_in,
    bias_in,
    weight_noise,
    weight_mid,
    bias_mid,
    weight_out,
):
    samples, channels, rows, cols = latent.shape
    taps, hidden, deep = weight_in.shape
    half = rows // 2
    row_count, col_count = dims["row"], dims["col"]
    messages = dims["messages"]
    vmem = pl.BlockSpec(memory_space=pltpu.VMEM)
    smem = pl.BlockSpec(memory_space=pltpu.SMEM)
    struct = jax.ShapeDtypeStruct

    swap = [(0, 1), (1, 0)]
    other_mid = lax.ppermute(weight_mid, "chan", swap)
    packed = pl.pallas_call(
        functools.partial(pack_kernel, dims),
        out_shape=[
            struct((2 * samples, CPAD, cols), BF16),
            struct((CPAD, hidden // 2), F32),
        ]
        + [struct((CPAD, LANES), F32)] * messages,
        in_specs=[vmem] * 4,
        out_specs=[vmem] * (2 + messages),
        name="pack",
    )(latent, coarse, weight_out, bias_mid.reshape(1, -1))
    rows_message, shared, side_messages = packed[0], packed[1], packed[2:]

    down = [(r, 0, r + 1, 0) for r in range(row_count - 1)]
    down += [(r + 1, 1, r, 1) for r in range(row_count - 1)]
    ends = [(row_count - 1, 0, row_count - 1, 1), (0, 1, 0, 0)]
    vertical = [(2 * a + b, 2 * c + d) for a, b, c, d in down + ends]
    rows_in = lax.ppermute(rows_message, ("row", "chan"), vertical)
    sides, corners = [], []
    for n, message in enumerate(side_messages):
        if col_count > 2:
            step = 1 if n == 0 else -1
            columns = [(i, (i + step) % col_count) for i in range(col_count)]
        else:
            columns = [(i, col_count - 1 - i) for i in range(col_count)]
        sides.append(lax.ppermute(message, "col", columns))
        diagonal = [
            (2 * (a * col_count + i) + b, 2 * (c * col_count + k) + d)
            for a, b, c, d in down
            for i, k in columns
        ]
        diagonal += [
            (2 * (a * col_count + i) + b, 2 * (c * col_count + i) + d)
            for a, b, c, d in ends
            for i in range(col_count)
        ]
        corners.append(lax.ppermute(message, ("row", "col", "chan"), diagonal))
    other_shared = lax.ppermute(shared, "chan", swap)

    block = 3 * deep + 8
    net, mean = pl.pallas_call(
        functools.partial(main_kernel, dims),
        out_shape=[
            struct((samples * half, CPAD, cols), F32),
            struct((rows, CPAD, cols), F32),
        ],
        in_specs=[smem] + [vmem] * (10 + 2 * messages),
        out_specs=[vmem] * 2,
        scratch_shapes=[
            pltpu.VMEM((rows + 4, samples, CPAD, cols), F32),
            pltpu.VMEM((samples, half + 4, block, cols), F32),
            pltpu.VMEM((hidden, 3 * block), F32),
            pltpu.VMEM((coarse.shape[1] * CPAD, LANES), F32),
            pltpu.VMEM((3, samples, half + 2, hidden, cols), BF16),
            pltpu.VMEM((LANES, LANES), F32),
        ],
        name="sections",
    )(
        step_index,
        latent,
        coarse,
        weight_in,
        bias_in.reshape(1, -1),
        weight_noise.reshape(1, -1),
        weight_mid,
        other_mid,
        shared,
        other_shared,
        rows_in,
        *sides,
        *corners,
    )
    other_net = lax.ppermute(net, "chan", swap)
    return pl.pallas_call(
        finish_kernel,
        out_shape=[struct(latent.shape, F32)] * 2,
        in_specs=[smem] + [vmem] * 5,
        out_specs=[vmem] * 2,
        name="finish",
    )(step_index, latent, fresh_noise, net, other_net, mean)


def solution(mesh):
    dims = {axis: mesh.shape[axis] for axis in ("row", "col", "chan")}
    dims["messages"] = 2 if dims["col"] > 2 else 1
    tile = P("ens", None, "row", "col")
    in_specs = (
        tile,
        tile,
        P("ens"),
        P("ens", None, "col"),
        P(),
        P(),
        P(),
        P(None, "chan", None),
        P("chan"),
        P(None, "chan"),
    )

    def body(*args):
        return tuple(on_device(dims, *args))

    return jax.shard_map(
        body, mesh=mesh, in_specs=in_specs, out_specs=(tile, tile), check_vma=False
    )
```

time: 60.9 us -> 23.4 us (0.38)
  between operations: 14.4 us -> 0.69 us
  Pallas kernels: 0 us -> 10.1 us
  matrix products: 9.14 us -> 0 us
  starting transfers between devices: 14.9 us -> 6.18 us
  blocking collectives: 6.31 us -> 0 us
  waiting for transfers between devices: 8.92 us -> 3.71 us
  other arithmetic: 4.14 us -> 0 us
    pallas_call x0 -> x3, Pallas kernels: none -> 10.1 us  [the longest x1 6.61 us: on_device(): pl.pallas_call(functools.partial(main_kernel, dims), out_shape=[struct((s...]
    dot_general x20 -> x0, matrix products: 9.14 us -> none  [the longest x17 7.96 us: conv_valid(): jnp.einsum('oi,siyx->soyx', weight[3 * offset_row + offset_col], window,...]
    ppermute x6, starting transfers between devices: 14.9 us -> 6.18 us  [the longest x1 2.58 us: on_device(): rows_in = lax.ppermute(rows_message, ('row', 'chan'), vertical)]
    all_gather x3 -> x0, blocking collectives: 6.31 us -> none  [the longest x1 2.69 us: on_device(): network = lax.all_gather(half_network, 'chan', axis=3, tiled=True)]
    ppermute x6, waiting for transfers between devices: 8.88 us -> 3.71 us  [the longest x1 2.24 us: on_device(): sides.append(lax.ppermute(message, 'col', columns))]
    unnamed x13 -> x15, local copies, waits for them, and re-layouts: 1.2 us -> 2.5 us
    another operation x1 -> x0, other arithmetic: 0.9 us -> none
    add x2 -> x0, other arithmetic: 0.77 us -> none  [the longest x1 0.77 us: on_device(): bias_in[None, :, None, None]]
  transfers between devices with their start and end apart: 7 -> 6, of which waited for: 4 -> 2; matrix products, arithmetic and copies ran while one was open for 14% -> 5% of each run, Pallas kernels for 0% -> 8%
where the time goes in v1:
time: 23.4 us; the launch traced here: 23.2 us
  Pallas kernels  10.1 us (43%)
  starting transfers between devices  6.18 us (26%)
  waiting for transfers between devices  3.71 us (16%)
  local copies, waits for them, and re-layouts  2.5 us (11%)
  between operations  0.69 us (3%)
    pallas_call x1, Pallas kernels, on_device(): pl.pallas_call(functools.partial(main_kernel, dims), out_shape=[struct((s...  6.61 us
    ppermute x1, starting transfers between devices, on_device(): rows_in = lax.ppermute(rows_message, ('row', 'chan'), vertical)  2.58 us
    ppermute x1, starting transfers between devices, on_device(): corners.append(lax.ppermute(message, ('row', 'col', 'chan'), diagonal))  2.5 us
    unnamed x15, local copies, waits for them, and re-layouts  2.5 us
    ppermute x1, waiting for transfers between devices, on_device(): sides.append(lax.ppermute(message, 'col', columns))  2.24 us
    pallas_call x1, Pallas kernels, on_device(): pl.pallas_call(functools.partial(pack_kernel, dims), out_shape=[struct((2...  1.77 us
    pallas_call x1, Pallas kernels, on_device(): pl.pallas_call(finish_kernel, out_shape=[struct(latent.shape, F32)] * 2,...  1.75 us
    ppermute x1, waiting for transfers between devices, on_device(): other_net = lax.ppermute(net, 'chan', swap)  1.46 us
  transfers between devices with their start and end apart: 6, of which 2 were waited for; matrix products, arithmetic and copies ran while one was open for 5% of the time, Pallas kernels for 8%

profile of v1, /device:TPU:0, one launch (start us, length us, event | category | flops | bytes accessed | tf_op | source)
XLA Modules:
  0.0 23.2 jit_solution(6715731439143384174)
XLA Ops:
  0.6 0.0 copy-start.1
  0.6 0.6 %collective-permute-start = (bf16[9,128,256]{2,1,0:T(8,128)(2,1)}, bf16[9,128,256]{2,1,0:T(8,128)(2,1)S(1)}, u32[]{:S(2)}, u32[]{:S(2)}) collective-permute-start(bf16[9,128,256]{2,1,0:T(8,128)(2,1)} %own_mid.1), channel_id=1, source_target_pairs={{0,1},{1,0},{2,3},{3,2},{4,5},{5,4},{6,7},{7,6},{8,9},{9,8},{10,11... | collective-permute-start | bytes 1769480 | tf_op jit(solution)/shard_map/ppermute | solution.py:420
  1.2 1.8 %pack.1 = (bf16[4,16,128]{2,1,0:T(8,128)(2,1)}, f32[16,128]{1,0:T(8,128)}, f32[16,128]{1,0:T(8,128)}) custom-call(f32[2,12,8,128]{3,2,1,0:T(8,128)} %latent.5, f32[12,4,16]{2,1,0:T(4,128)} %coarse.3, bf16[12,128]{1,0:T(8,128)(2,1)} %weight_out.1, f32[1,128]{1,0:T(1,128)} %bitcast.5), custom_call_target="tpu_custom_call" | custom-call | tf_op jit(solution)/shard_map/pack/pallas_call | solution.py:421
  3.0 2.6 %collective-permute-start.2 = (bf16[4,16,128]{2,1,0:T(8,128)(2,1)}, bf16[4,16,128]{2,1,0:T(8,128)(2,1)S(1)}, u32[]{:S(2)}, u32[]{:S(2)}) collective-permute-start(bf16[4,16,128]{2,1,0:T(8,128)(2,1)} %get-tuple-element.8), channel_id=1, source_target_pairs={{0,4},{4,8},{8,12},{5,1},{9,5},{13,9},{12,13},{1,0},{2,6},{6,10},{... | collective-permute-start | bytes 49160 | tf_op jit(solution)/shard_map/ppermute | solution.py:438
  5.5 0.0 collective-permute-start.1
  5.5 2.5 %collective-permute-start.4 = (f32[16,128]{1,0:T(8,128)}, f32[16,128]{1,0:T(8,128)S(1)}, u32[]{:S(2)}, u32[]{:S(2)}) collective-permute-start(f32[16,128]{1,0:T(8,128)} %get-tuple-element.9), channel_id=1, source_target_pairs={{0,6},{2,4},{4,10},{6,8},{8,14},{10,12},{5,3},{7,1},{9,7},{11,5},{... | collective-permute-start | bytes 24584 | tf_op jit(solution)/shard_map/ppermute | solution.py:457
  8.1 0.5 %collective-permute-start.3 = (f32[16,128]{1,0:T(8,128)}, f32[16,128]{1,0:T(8,128)S(1)}, u32[]{:S(2)}, u32[]{:S(2)}) collective-permute-start(f32[16,128]{1,0:T(8,128)} %get-tuple-element.9), channel_id=1, source_target_pairs={{0,2},{2,0},{1,3},{3,1},{4,6},{6,4},{5,7},{7,5},{8,10},{10,8},{9,1... | collective-permute-start | bytes 24584 | tf_op jit(solution)/shard_map/ppermute | solution.py:446
  8.6 0.0 copy-done.1
  8.6 1.1 %copy.12.weight_in = bf16[9,256,24]{2,1,0:T(8,128)(2,1)} copy(bf16[9,256,24]{1,2,0:T(8,128)(2,1)S(1)} %copy-done.1) | data formatting | bytes 221184 | tf_op args[4]
  9.7 0.0 collective-permute-done.1.other_shared
  9.7 0.0 copy-start.4
  9.7 0.0 collective-permute-done.4.rest_1_
  9.7 0.0 copy-start.5
  9.7 2.2 %collective-permute-done.3.rest_0_ = f32[16,128]{1,0:T(8,128)S(1)} collective-permute-done((f32[16,128]{1,0:T(8,128)}, f32[16,128]{1,0:T(8,128)S(1)}, u32[]{:S(2)}, u32[]{:S(2)}) %collective-permute-start.3) | collective-permute-done | bytes 8224 | tf_op jit(solution)/shard_map/ppermute | solution.py:446
  11.9 0.0 copy-start.6
  11.9 0.0 collective-permute-done.2.rows_in
  11.9 0.0 copy-start.3
  11.9 0.0 collective-permute-done.other_mid
  11.9 0.0 copy-start
  11.9 0.0 copy-done.4
  11.9 0.0 copy-done.5
  12.0 0.6 %copy-done.6 = f32[16,128]{1,0:T(8,128)} copy-done((f32[16,128]{1,0:T(8,128)}, f32[16,128]{1,0:T(8,128)S(1)}, u32[]{:S(2)}) %copy-start.6) | copy-done | bytes 8216
  12.5 0.0 copy-done.3
  12.5 0.2 copy-done
  12.8 6.6 %sections.1 = (f32[8,16,128]{2,1,0:T(8,128)}, f32[8,16,128]{2,1,0:T(8,128)}) custom-call(s32[2]{0:T(128)} %steps.3, f32[2,12,8,128]{3,2,1,0:T(8,128)} %latent.5, f32[12,4,16]{2,1,0:T(4,128)} %coarse.3, bf16[9,256,24]{2,1,0:T(8,128)(2,1)} %copy.12.weight_in, f32[1,256]{1,0:T(1,128)} %bitcast.3, f32[1,256]{1,0:T(1,128)} %bitcast.4, ...), custom_call_target="tpu_custom_call" | custom-call | tf_op jit(solution)/shard_map/sections/pallas_call | solution.py:461
  19.4 0.0 collective-permute-start.5
  19.4 1.5 %collective-permute-done.5.other_net = f32[8,16,128]{2,1,0:T(8,128)S(1)} collective-permute-done((f32[8,16,128]{2,1,0:T(8,128)}, f32[8,16,128]{2,1,0:T(8,128)S(1)}, u32[]{:S(2)}, u32[]{:S(2)}) %collective-permute-start.5) | collective-permute-done | bytes 65568 | tf_op jit(solution)/shard_map/ppermute | solution.py:493
  20.8 0.0 copy-start.2
  20.8 0.6 %copy-done.2 = f32[8,16,128]{2,1,0:T(8,128)} copy-done((f32[8,16,128]{2,1,0:T(8,128)}, f32[8,16,128]{2,1,0:T(8,128)S(1)}, u32[]{:S(2)}) %copy-start.2) | copy-done | bytes 65560
  21.4 1.8 %finish.1 = (f32[2,12,8,128]{3,2,1,0:T(8,128)}, f32[2,12,8,128]{3,2,1,0:T(8,128)}) custom-call(s32[2]{0:T(128)} %steps.3, f32[2,12,8,128]{3,2,1,0:T(8,128)} %latent.5, f32[2,12,8,128]{3,2,1,0:T(8,128)} %fresh.1, f32[8,16,128]{2,1,0:T(8,128)} %get-tuple-element.10.own_net, f32[8,16,128]{2,1,0:T(8,128)} %copy-done.2, f32[8,16,128]{2,1,0:T(8,128)} %get-tuple-element.11.own_mean), custom_call_target="tpu_custom_call" | custom-call | tf_op jit(solution)/shard_map/finish/pallas_call | solution.py:494
Async XLA Ops:
  0.6 8.0 %copy-start.1 = (bf16[9,256,24]{1,2,0:T(8,128)(2,1)S(1)}, bf16[9,256,24]{1,2,0:T(8,128)(2,1)}, u32[]{:S(2)}) copy-start(bf16[9,256,24]{1,2,0:T(8,128)(2,1)} %param.14) | copy-start | bytes 331780
  0.6 11.3 %collective-permute-start = (bf16[9,128,256]{2,1,0:T(8,128)(2,1)}, bf16[9,128,256]{2,1,0:T(8,128)(2,1)S(1)}, u32[]{:S(2)}, u32[]{:S(2)}) collective-permute-start(bf16[9,128,256]{2,1,0:T(8,128)(2,1)} %own_mid.1), channel_id=1, source_target_pairs={{0,1},{1,0},{2,3},{3,2},{4,5},{5,4},{6,7},{7,6},{8,9},{9,8},{10,11... | collective-permute-start | bytes 1769480 | tf_op jit(solution)/shard_map/ppermute | solution.py:420
  3.0 9.0 %collective-permute-start.2 = (bf16[4,16,128]{2,1,0:T(8,128)(2,1)}, bf16[4,16,128]{2,1,0:T(8,128)(2,1)S(1)}, u32[]{:S(2)}, u32[]{:S(2)}) collective-permute-start(bf16[4,16,128]{2,1,0:T(8,128)(2,1)} %get-tuple-element.8), channel_id=1, source_target_pairs={{0,4},{4,8},{8,12},{5,1},{9,5},{13,9},{12,13},{1,0},{2,6},{6,10},{... | collective-permute-start | bytes 49160 | tf_op jit(solution)/shard_map/ppermute | solution.py:438
  5.5 4.1 %collective-permute-start.1 = (f32[16,128]{1,0:T(8,128)}, f32[16,128]{1,0:T(8,128)S(1)}, u32[]{:S(2)}, u32[]{:S(2)}) collective-permute-start(f32[16,128]{1,0:T(8,128)} %get-tuple-element.7.own_shared), channel_id=1, source_target_pairs={{0,1},{1,0},{2,3},{3,2},{4,5},{5,4},{6,7},{7,6},{8,9},{9,8},{10,11... | collective-permute-start | bytes 24584 | tf_op jit(solution)/shard_map/ppermute | solution.py:458
  5.5 4.1 %collective-permute-start.4 = (f32[16,128]{1,0:T(8,128)}, f32[16,128]{1,0:T(8,128)S(1)}, u32[]{:S(2)}, u32[]{:S(2)}) collective-permute-start(f32[16,128]{1,0:T(8,128)} %get-tuple-element.9), channel_id=1, source_target_pairs={{0,6},{2,4},{4,10},{6,8},{8,14},{10,12},{5,3},{7,1},{9,7},{11,5},{... | collective-permute-start | bytes 24584 | tf_op jit(solution)/shard_map/ppermute | solution.py:457
  8.1 3.9 %collective-permute-start.3 = (f32[16,128]{1,0:T(8,128)}, f32[16,128]{1,0:T(8,128)S(1)}, u32[]{:S(2)}, u32[]{:S(2)}) collective-permute-start(f32[16,128]{1,0:T(8,128)} %get-tuple-element.9), channel_id=1, source_target_pairs={{0,2},{2,0},{1,3},{3,1},{4,6},{6,4},{5,7},{7,5},{8,10},{10,8},{9,1... | collective-permute-start | bytes 24584 | tf_op jit(solution)/shard_map/ppermute | solution.py:446
  9.7 2.3 %copy-start.4 = (f32[16,128]{1,0:T(8,128)}, f32[16,128]{1,0:T(8,128)S(1)}, u32[]{:S(2)}) copy-start(f32[16,128]{1,0:T(8,128)S(1)} %collective-permute-done.1.other_shared) | copy-start | bytes 24580
  9.7 2.3 %copy-start.5 = (f32[16,128]{1,0:T(8,128)}, f32[16,128]{1,0:T(8,128)S(1)}, u32[]{:S(2)}) copy-start(f32[16,128]{1,0:T(8,128)S(1)} %collective-permute-done.4.rest_1_) | copy-start | bytes 24580
  11.9 0.6 %copy-start.6 = (f32[16,128]{1,0:T(8,128)}, f32[16,128]{1,0:T(8,128)S(1)}, u32[]{:S(2)}) copy-start(f32[16,128]{1,0:T(8,128)S(1)} %collective-permute-done.3.rest_0_) | copy-start | bytes 24580
  11.9 0.6 %copy-start.3 = (bf16[4,16,128]{2,1,0:T(8,128)(2,1)}, bf16[4,16,128]{2,1,0:T(8,128)(2,1)S(1)}, u32[]{:S(2)}) copy-start(bf16[4,16,128]{2,1,0:T(8,128)(2,1)S(1)} %collective-permute-done.2.rows_in) | copy-start | bytes 49156
  11.9 0.8 %copy-start = (bf16[9,128,256]{2,1,0:T(8,128)(2,1)}, bf16[9,128,256]{2,1,0:T(8,128)(2,1)S(1)}, u32[]{:S(2)}) copy-start(bf16[9,128,256]{2,1,0:T(8,128)(2,1)S(1)} %collective-permute-done.other_mid) | copy-start | bytes 1769476
  19.4 1.5 %collective-permute-start.5 = (f32[8,16,128]{2,1,0:T(8,128)}, f32[8,16,128]{2,1,0:T(8,128)S(1)}, u32[]{:S(2)}, u32[]{:S(2)}) collective-permute-start(f32[8,16,128]{2,1,0:T(8,128)} %get-tuple-element.10.own_net), channel_id=1, source_target_pairs={{0,1},{1,0},{2,3},{3,2},{4,5},{5,4},{6,7},{7,6},{8,9},{9,8},{10,11... | collective-permute-start | bytes 196616 | tf_op jit(solution)/shard_map/ppermute | solution.py:493
  20.8 0.6 %copy-start.2 = (f32[8,16,128]{2,1,0:T(8,128)}, f32[8,16,128]{2,1,0:T(8,128)S(1)}, u32[]{:S(2)}) copy-start(f32[8,16,128]{2,1,0:T(8,128)S(1)} %collective-permute-done.5.other_net) | copy-start | bytes 196612

commit v2 on v1

--- a/solution.py
+++ b/solution.py
@@ -45,7 +45,7 @@
     return high, mid, (rest - mid).astype(BF16).astype(F32)
 
 
-def pack_kernel(dims, latent, coarse, weight_out, bias_mid, rows_out, shared_out, *side_outs):
+def pack_kernel(dims, latent, coarse, weight_out, bias_mid, own_out, rows_out, shared_out, *side_outs):
     samples, channels, rows, cols = latent.shape
     coarse_rows, local_cols = coarse.shape[1:]
     count = dims["col"]
@@ -59,9 +59,10 @@
             rows_out[near * samples + s, channels:CPAD, :] = jnp.zeros(
                 (CPAD - channels, LANES), BF16
             )
-    shared_out[0:channels, :] = weight_out[...].astype(F32)
-    shared_out[channels : channels + 1, :] = bias_mid[...]
-    shared_out[channels + 1 : CPAD, :] = jnp.zeros((CPAD - channels - 1, LANES), F32)
+    for out in (own_out, shared_out):
+        out[0:channels, :] = weight_out[...].astype(F32)
+        out[channels : channels + 1, :] = bias_mid[...]
+        out[channels + 1 : CPAD, :] = jnp.zeros((CPAD - channels - 1, LANES), F32)
     lane = lane_index(channels)
     sums = [jnp.zeros((channels, LANES), F32) for _ in side_outs]
     for s in range(samples):
@@ -128,7 +129,7 @@
 ):
     sides = rest[: dims["messages"]]
     corners = rest[dims["messages"] : 2 * dims["messages"]]
-    net_out, mean_out, xs, zx, w1, ce, hs, tr = rest[2 * dims["messages"] :]
+    net_out, own_out, mean_out, xs, zx, w1, ce, hs, tr = rest[2 * dims["messages"] :]
     samples, channels, rows, cols = latent.shape
     coarse_rows, local_cols = coarse.shape[1:]
     taps, hidden, deep = weight_in.shape
@@ -365,6 +366,7 @@
             net = jnp.dot(out_weight, middle, preferred_element_type=F32)
             for e in range(2):
                 net_out[s * half + v + e] = net[:, e * LANES : (e + 1) * LANES]
+                own_out[s * half + v + e] = net[:, e * LANES : (e + 1) * LANES]
     del cols, place
 
 
@@ -415,21 +417,23 @@
     vmem = pl.BlockSpec(memory_space=pltpu.VMEM)
     smem = pl.BlockSpec(memory_space=pltpu.SMEM)
     struct = jax.ShapeDtypeStruct
+    near = functools.partial(pltpu.with_memory_space_constraint, memory_space=pltpu.VMEM)
 
     swap = [(0, 1), (1, 0)]
     other_mid = lax.ppermute(weight_mid, "chan", swap)
     packed = pl.pallas_call(
         functools.partial(pack_kernel, dims),
         out_shape=[
+            pltpu.VMEM((CPAD, hidden // 2), F32),
             struct((2 * samples, CPAD, cols), BF16),
             struct((CPAD, hidden // 2), F32),
         ]
         + [struct((CPAD, LANES), F32)] * messages,
         in_specs=[vmem] * 4,
-        out_specs=[vmem] * (2 + messages),
+        out_specs=[vmem] * (3 + messages),
         name="pack",
     )(latent, coarse, weight_out, bias_mid.reshape(1, -1))
-    rows_message, shared, side_messages = packed[0], packed[1], packed[2:]
+    own_shared, rows_message, shared, side_messages = *packed[:3], packed[3:]
 
     down = [(r, 0, r + 1, 0) for r in range(row_count - 1)]
     down += [(r + 1, 1, r, 1) for r in range(row_count - 1)]
@@ -458,14 +462,15 @@
     other_shared = lax.ppermute(shared, "chan", swap)
 
     block = 3 * deep + 8
-    net, mean = pl.pallas_call(
+    net, own_net, mean = pl.pallas_call(
         functools.partial(main_kernel, dims),
         out_shape=[
             struct((samples * half, CPAD, cols), F32),
-            struct((rows, CPAD, cols), F32),
+            pltpu.VMEM((samples * half, CPAD, cols), F32),
+            pltpu.VMEM((rows, CPAD, cols), F32),
         ],
         in_specs=[smem] + [vmem] * (10 + 2 * messages),
-        out_specs=[vmem] * 2,
+        out_specs=[vmem] * 3,
         scratch_shapes=[
             pltpu.VMEM((rows + 4, samples, CPAD, cols), F32),
             pltpu.VMEM((samples, half + 4, block, cols), F32),
@@ -477,18 +482,18 @@
         name="sections",
     )(
         step_index,
-        latent,
-        coarse,
-        weight_in,
-        bias_in.reshape(1, -1),
-        weight_noise.reshape(1, -1),
-        weight_mid,
-        other_mid,
-        shared,
-        other_shared,
-        rows_in,
-        *sides,
-        *corners,
+        near(latent),
+        near(coarse),
+        near(weight_in),
+        near(bias_in.reshape(1, -1)),
+        near(weight_noise.reshape(1, -1)),
+        near(weight_mid),
+        near(other_mid),
+        near(own_shared),
+        near(other_shared),
+        near(rows_in),
+        *[near(side) for side in sides],
+        *[near(corner) for corner in corners],
     )
     other_net = lax.ppermute(net, "chan", swap)
     return pl.pallas_call(
@@ -497,7 +502,7 @@
         in_specs=[smem] + [vmem] * 5,
         out_specs=[vmem] * 2,
         name="finish",
-    )(step_index, latent, fresh_noise, net, other_net, mean)
+    )(step_index, near(latent), near(fresh_noise), near(own_net), near(other_net), near(mean))
 
 
 def solution(mesh):

time: 23.4 us -> 21.7 us (0.927)
  Pallas kernels: 10.1 us -> 9.12 us
  local copies, waits for them, and re-layouts: 2.5 us -> 1.93 us
    pallas_call x1, Pallas kernels: 6.61 us -> 5.94 us  [on_device(): pl.pallas_call(functools.partial(main_kernel, dims), out_shape=[struct((s...]
    unnamed x15 -> x13, local copies, waits for them, and re-layouts: 2.5 us -> 1.93 us
    pallas_call x1, Pallas kernels: 1.75 us -> 1.41 us  [on_device(): pl.pallas_call(finish_kernel, out_shape=[struct(latent.shape, F32)] * 2,...]
  transfers between devices with their start and end apart: 6 -> 6, of which waited for: 2 -> 2; matrix products, arithmetic and copies ran while one was open for 5% -> 6% of each run, Pallas kernels for 8% -> 8%
where the time goes in v2:
time: 21.7 us; the launch traced here: 21.5 us
  Pallas kernels  9.12 us (42%)
  starting transfers between devices  6.23 us (29%)
  waiting for transfers between devices  3.49 us (16%)
  local copies, waits for them, and re-layouts  1.93 us (9%)
  between operations  0.71 us (3%)
    pallas_call x1, Pallas kernels, on_device(): pl.pallas_call(functools.partial(main_kernel, dims), out_shape=[struct((s...  5.94 us
    ppermute x1, starting transfers between devices, on_device(): rows_in = lax.ppermute(rows_message, ('row', 'chan'), vertical)  2.62 us
    ppermute x1, starting transfers between devices, on_device(): corners.append(lax.ppermute(message, ('row', 'col', 'chan'), diagonal))  2.5 us
    ppermute x1, waiting for transfers between devices, on_device(): sides.append(lax.ppermute(message, 'col', columns))  2.02 us
    unnamed x13, local copies, waits for them, and re-layouts  1.93 us
    pallas_call x1, Pallas kernels, on_device(): pl.pallas_call(functools.partial(pack_kernel, dims), out_shape=[pltpu.VME...  1.77 us
    ppermute x1, waiting for transfers between devices, on_device(): other_net = lax.ppermute(net, 'chan', swap)  1.46 us
    pallas_call x1, Pallas kernels, on_device(): pl.pallas_call(finish_kernel, out_shape=[struct(latent.shape, F32)] * 2,...  1.41 us
  transfers between devices with their start and end apart: 6, of which 2 were waited for; matrix products, arithmetic and copies ran while one was open for 6% of the time, Pallas kernels for 8%

profile of v2, /device:TPU:0, one launch (start us, length us, event | category | flops | bytes accessed | tf_op | source)
XLA Modules:
  0.0 21.5 jit_solution(59308836386123777)
XLA Ops:
  0.6 0.0 copy-start.1
  0.6 0.6 %collective-permute-start = (bf16[9,128,256]{2,1,0:T(8,128)(2,1)}, bf16[9,128,256]{2,1,0:T(8,128)(2,1)S(1)}, u32[]{:S(2)}, u32[]{:S(2)}) collective-permute-start(bf16[9,128,256]{2,1,0:T(8,128)(2,1)} %own_mid.1), channel_id=1, source_target_pairs={{0,1},{1,0},{2,3},{3,2},{4,5},{5,4},{6,7},{7,6},{8,9},{9,8},{10,11... | collective-permute-start | bytes 1769480 | tf_op jit(solution)/shard_map/ppermute | solution.py:423
  1.2 1.8 %pack.1 = (f32[16,128]{1,0:T(8,128)S(1)}, bf16[4,16,128]{2,1,0:T(8,128)(2,1)}, f32[16,128]{1,0:T(8,128)}, f32[16,128]{1,0:T(8,128)}) custom-call(f32[2,12,8,128]{3,2,1,0:T(8,128)} %latent.5, f32[12,4,16]{2,1,0:T(4,128)} %coarse.3, bf16[12,128]{1,0:T(8,128)(2,1)} %weight_out.1, f32[1,128]{1,0:T(1,128)} %bitcast.5), custom_call_target="tpu_custom_call" | custom-call | tf_op jit(solution)/shard_map/pack/pallas_call | solution.py:424
  3.0 2.6 %collective-permute-start.2 = (bf16[4,16,128]{2,1,0:T(8,128)(2,1)}, bf16[4,16,128]{2,1,0:T(8,128)(2,1)S(1)}, u32[]{:S(2)}, u32[]{:S(2)}) collective-permute-start(bf16[4,16,128]{2,1,0:T(8,128)(2,1)} %get-tuple-element.11), channel_id=1, source_target_pairs={{0,4},{4,8},{8,12},{5,1},{9,5},{13,9},{12,13},{1,0},{2,6},{6,10},{... | collective-permute-start | bytes 49160 | tf_op jit(solution)/shard_map/ppermute | solution.py:442
  5.6 0.0 collective-permute-start.1
  5.6 0.0 copy-start
  5.6 0.0 copy-start.2
  5.6 2.5 %collective-permute-start.4 = (f32[16,128]{1,0:T(8,128)}, f32[16,128]{1,0:T(8,128)S(1)}, u32[]{:S(2)}, u32[]{:S(2)}) collective-permute-start(f32[16,128]{1,0:T(8,128)} %get-tuple-element.12), channel_id=1, source_target_pairs={{0,6},{2,4},{4,10},{6,8},{8,14},{10,12},{5,3},{7,1},{9,7},{11,5},{... | collective-permute-start | bytes 24584 | tf_op jit(solution)/shard_map/ppermute | solution.py:461
  8.1 0.5 %collective-permute-start.3 = (f32[16,128]{1,0:T(8,128)}, f32[16,128]{1,0:T(8,128)S(1)}, u32[]{:S(2)}, u32[]{:S(2)}) collective-permute-start(f32[16,128]{1,0:T(8,128)} %get-tuple-element.12), channel_id=1, source_target_pairs={{0,2},{2,0},{1,3},{3,1},{4,6},{6,4},{5,7},{7,5},{8,10},{10,8},{9,1... | collective-permute-start | bytes 24584 | tf_op jit(solution)/shard_map/ppermute | solution.py:450
  8.6 0.0 copy-start.5
  8.6 1.3 %copy.12.weight_in = bf16[9,256,24]{2,1,0:T(8,128)(2,1)S(1)} copy(bf16[9,256,24]{1,2,0:T(8,128)(2,1)} %param.14) | data formatting | bytes 221184 | tf_op args[4]
  9.9 0.0 collective-permute-done.1.other_shared
  9.9 0.0 collective-permute-done.4.rest_1_
  9.9 2.0 %collective-permute-done.3.rest_0_ = f32[16,128]{1,0:T(8,128)S(1)} collective-permute-done((f32[16,128]{1,0:T(8,128)}, f32[16,128]{1,0:T(8,128)S(1)}, u32[]{:S(2)}, u32[]{:S(2)}) %collective-permute-start.3) | collective-permute-done | bytes 8224 | tf_op jit(solution)/shard_map/ppermute | solution.py:450
  12.0 0.0 collective-permute-done.2.rows_in
  12.0 0.0 collective-permute-done.other_mid
  12.0 0.0 copy-start.4
  12.0 0.0 copy-done.1
  12.0 0.0 copy-done
  12.0 0.0 copy-done.2
  12.0 0.0 copy-done.5
  12.0 0.6 %copy-done.4 = f32[256]{0:T(256)S(1)} copy-done((f32[256]{0:T(256)S(1)}, f32[256]{0:T(256)}, u32[]{:S(2)}) %copy-start.4) | copy-done | bytes 1048
  12.7 0.0 copy-start.3
  12.7 5.9 %sections.1 = (f32[8,16,128]{2,1,0:T(8,128)}, f32[8,16,128]{2,1,0:T(8,128)S(1)}, f32[8,16,128]{2,1,0:T(8,128)S(1)}) custom-call(s32[2]{0:T(128)} %steps.3, f32[2,12,8,128]{3,2,1,0:T(8,128)S(1)} %copy-done, f32[12,4,16]{2,1,0:T(4,128)S(1)} %copy-done.2, bf16[9,256,24]{2,1,0:T(8,128)(2,1)S(1)} %copy.12.weight_in, f32[1,256]{1,0:T(1,128)S(1)} %bitcast.3, ...), custom_call_target="tpu_custom_call" | custom-call | tf_op jit(solution)/shard_map/sections/pallas_call | solution.py:465
  18.6 0.0 collective-permute-start.5
  18.6 1.5 %collective-permute-done.5.other_net = f32[8,16,128]{2,1,0:T(8,128)S(1)} collective-permute-done((f32[8,16,128]{2,1,0:T(8,128)}, f32[8,16,128]{2,1,0:T(8,128)S(1)}, u32[]{:S(2)}, u32[]{:S(2)}) %collective-permute-start.5) | collective-permute-done | bytes 65568 | tf_op jit(solution)/shard_map/ppermute | solution.py:498
  20.1 0.0 copy-done.3
  20.1 1.4 %finish.1 = (f32[2,12,8,128]{3,2,1,0:T(8,128)}, f32[2,12,8,128]{3,2,1,0:T(8,128)}) custom-call(s32[2]{0:T(128)} %steps.3, f32[2,12,8,128]{3,2,1,0:T(8,128)S(1)} %copy-done, f32[2,12,8,128]{3,2,1,0:T(8,128)S(1)} %copy-done.3, f32[8,16,128]{2,1,0:T(8,128)S(1)} %get-tuple-element.13.own_net, f32[8,16,128]{2,1,0:T(8,128)S(1)} %collective-permute-done.5.other_net, ...), custom_call_target="tpu_custom_call" | custom-call | tf_op jit(solution)/shard_map/finish/pallas_call | solution.py:499
Async XLA Ops:
  0.6 11.4 %copy-start.1 = (bf16[9,128,256]{2,1,0:T(8,128)(2,1)S(1)}, bf16[9,128,256]{2,1,0:T(8,128)(2,1)}, u32[]{:S(2)}) copy-start(bf16[9,128,256]{2,1,0:T(8,128)(2,1)} %own_mid.1) | copy-start | bytes 1769476
  0.6 11.3 %collective-permute-start = (bf16[9,128,256]{2,1,0:T(8,128)(2,1)}, bf16[9,128,256]{2,1,0:T(8,128)(2,1)S(1)}, u32[]{:S(2)}, u32[]{:S(2)}) collective-permute-start(bf16[9,128,256]{2,1,0:T(8,128)(2,1)} %own_mid.1), channel_id=1, source_target_pairs={{0,1},{1,0},{2,3},{3,2},{4,5},{5,4},{6,7},{7,6},{8,9},{9,8},{10,11... | collective-permute-start | bytes 1769480 | tf_op jit(solution)/shard_map/ppermute | solution.py:423
  3.0 9.0 %collective-permute-start.2 = (bf16[4,16,128]{2,1,0:T(8,128)(2,1)}, bf16[4,16,128]{2,1,0:T(8,128)(2,1)S(1)}, u32[]{:S(2)}, u32[]{:S(2)}) collective-permute-start(bf16[4,16,128]{2,1,0:T(8,128)(2,1)} %get-tuple-element.11), channel_id=1, source_target_pairs={{0,4},{4,8},{8,12},{5,1},{9,5},{13,9},{12,13},{1,0},{2,6},{6,10},{... | collective-permute-start | bytes 49160 | tf_op jit(solution)/shard_map/ppermute | solution.py:442
  5.6 4.3 %collective-permute-start.1 = (f32[16,128]{1,0:T(8,128)}, f32[16,128]{1,0:T(8,128)S(1)}, u32[]{:S(2)}, u32[]{:S(2)}) collective-permute-start(f32[16,128]{1,0:T(8,128)} %get-tuple-element.10), channel_id=1, source_target_pairs={{0,1},{1,0},{2,3},{3,2},{4,5},{5,4},{6,7},{7,6},{8,9},{9,8},{10,11... | collective-permute-start | bytes 24584 | tf_op jit(solution)/shard_map/ppermute | solution.py:462
  5.6 6.4 %copy-start = (f32[2,12,8,128]{3,2,1,0:T(8,128)S(1)}, f32[2,12,8,128]{3,2,1,0:T(8,128)}, u32[]{:S(2)}) copy-start(f32[2,12,8,128]{3,2,1,0:T(8,128)} %latent.5) | copy-start | bytes 294916
  5.6 6.4 %copy-start.2 = (f32[12,4,16]{2,1,0:T(4,128)S(1)}, f32[12,4,16]{2,1,0:T(4,128)}, u32[]{:S(2)}) copy-start(f32[12,4,16]{2,1,0:T(4,128)} %coarse.3) | copy-start | bytes 9220
  5.6 4.3 %collective-permute-start.4 = (f32[16,128]{1,0:T(8,128)}, f32[16,128]{1,0:T(8,128)S(1)}, u32[]{:S(2)}, u32[]{:S(2)}) collective-permute-start(f32[16,128]{1,0:T(8,128)} %get-tuple-element.12), channel_id=1, source_target_pairs={{0,6},{2,4},{4,10},{6,8},{8,14},{10,12},{5,3},{7,1},{9,7},{11,5},{... | collective-permute-start | bytes 24584 | tf_op jit(solution)/shard_map/ppermute | solution.py:461
  8.1 3.9 %collective-permute-start.3 = (f32[16,128]{1,0:T(8,128)}, f32[16,128]{1,0:T(8,128)S(1)}, u32[]{:S(2)}, u32[]{:S(2)}) collective-permute-start(f32[16,128]{1,0:T(8,128)} %get-tuple-element.12), channel_id=1, source_target_pairs={{0,2},{2,0},{1,3},{3,1},{4,6},{6,4},{5,7},{7,5},{8,10},{10,8},{9,1... | collective-permute-start | bytes 24584 | tf_op jit(solution)/shard_map/ppermute | solution.py:450
  8.6 3.4 %copy-start.5 = (f32[256]{0:T(256)S(1)}, f32[256]{0:T(256)}, u32[]{:S(2)}) copy-start(f32[256]{0:T(256)} %param.16) | copy-start | bytes 3076
  12.0 0.7 %copy-start.4 = (f32[256]{0:T(256)S(1)}, f32[256]{0:T(256)}, u32[]{:S(2)}) copy-start(f32[256]{0:T(256)} %param.15) | copy-start | bytes 3076
  12.7 7.4 %copy-start.3 = (f32[2,12,8,128]{3,2,1,0:T(8,128)S(1)}, f32[2,12,8,128]{3,2,1,0:T(8,128)}, u32[]{:S(2)}) copy-start(f32[2,12,8,128]{3,2,1,0:T(8,128)} %fresh.1) | copy-start | bytes 294916
  18.6 1.5 %collective-permute-start.5 = (f32[8,16,128]{2,1,0:T(8,128)}, f32[8,16,128]{2,1,0:T(8,128)S(1)}, u32[]{:S(2)}, u32[]{:S(2)}) collective-permute-start(f32[8,16,128]{2,1,0:T(8,128)} %get-tuple-element.14), channel_id=1, source_target_pairs={{0,1},{1,0},{2,3},{3,2},{4,5},{5,4},{6,7},{7,6},{8,9},{9,8},{10,11... | collective-permute-start | bytes 196616 | tf_op jit(solution)/shard_map/ppermute | solution.py:498

commit v3 on v0

v3 whole, which is shorter than its diff:
```python
import functools

import jax
import jax.numpy as jnp
from jax import lax
from jax.experimental import pallas as pl
from jax.experimental.pallas import tpu as pltpu
from jax.sharding import PartitionSpec as P

STEPS = 18
FACTOR = 8

sigma_data = 0.5
sigma_high = 80.0
sigma_low = 0.002
rho_power = 7.0

F32 = jnp.float32
BF16 = jnp.bfloat16
LANES = 128
CPAD = 16
LIMIT = pltpu.CompilerParams(vmem_limit_bytes=12 * 1024 * 1024)


def lane_index(rows):
    return lax.broadcasted_iota(jnp.int32, (rows, LANES), 1)


def tile_row(w, rows):
    return jnp.where(lax.axis_index("chan") == 0, w - 2, rows + 1 - w)


def tap_row(i):
    return jnp.where(lax.axis_index("chan") == 0, i, 2 - i)


def noise_level(position):
    top_root = sigma_high ** (1.0 / rho_power)
    bottom_root = sigma_low ** (1.0 / rho_power)
    root = top_root + position * (1.0 / (STEPS - 1)) * (bottom_root - top_root)
    square = root * root
    return square * square * square * root


def silu_of_half(half):
    return half + half * jnp.tanh(half)


def three_terms(value):
    high = value.astype(BF16).astype(F32)
    rest = value - high
    mid = rest.astype(BF16).astype(F32)
    return high, mid, (rest - mid).astype(BF16).astype(F32)


def channel_rows(ref, s, y, channels, rows):
    return ref[s, pl.ds(y, channels, stride=rows), :]


def pack_kernel(
    dims,
    latent_far,
    coarse_far,
    weight_out_far,
    bias_mid_far,
    weight_in_far,
    bias_in_far,
    weight_noise_far,
    steps_far,
    latent,
    coarse,
    weight_in,
    bias_in,
    weight_noise,
    steps_out,
    cols_matrix,
    rows_out,
    shared_out,
    *rest,
):
    sides = rest[: dims["messages"]]
    weight_out, bias_mid, steps, sem = rest[dims["messages"] :]
    pairs = (
        (latent_far, latent),
        (coarse_far, coarse),
        (weight_out_far, weight_out),
        (bias_mid_far, bias_mid),
        (steps_far, steps),
        (weight_in_far, weight_in),
        (bias_in_far, bias_in),
        (weight_noise_far, weight_noise),
    )
    copies = [pltpu.make_async_copy(a, b, sem.at[n]) for n, (a, b) in enumerate(pairs)]
    for copy in copies:
        copy.start()
    samples = latent.shape[0]
    channels, coarse_rows, local_cols = coarse.shape
    rows = latent.shape[1] // channels
    count = dims["col"]
    col_place = lax.axis_index("col")
    upper = lax.axis_index("chan") == 0

    cols = latent.shape[2]
    width = count * cols
    coarse_cols = count * local_cols
    group = local_cols + 2
    depth = lax.broadcasted_iota(jnp.int32, (cols_matrix.shape[0], LANES), 0)
    spot = depth % group
    index = col_place * local_cols + jnp.where(
        spot < local_cols, spot, jnp.where(spot == local_cols, -1, local_cols)
    )
    index = jnp.where(depth < 3 * group, index, -2).astype(F32)
    wide = lax.broadcasted_iota(jnp.int32, (1, LANES), 1)
    targets = [col_place * cols + wide - 1 + j for j in range(3)]
    targets += [
        col_place * cols + jnp.where(wide % 2 == 0, j - 2, cols - 1 + j) for j in range(3)
    ]
    for n, target in enumerate(targets):
        low, high, fraction = blend(target.astype(F32), coarse_cols)
        outside = (target < 0) | (target >= width)
        low = jnp.where(outside, -3.0, low)
        high = jnp.where(outside, -3.0, high)
        weights = jnp.where(low == index, 1.0 - fraction, 0.0)
        weights += jnp.where(high == index, fraction, 0.0)
        cols_matrix[:, n * LANES : (n + 1) * LANES] = weights.astype(BF16)

    copies[0].wait()
    for near in range(2):
        y = jnp.where(upper, rows - 2 + near, 1 - near)
        for s in range(samples):
            got = channel_rows(latent, s, y, channels, rows).astype(BF16)
            rows_out[near * samples + s, 0:channels, :] = got
            rows_out[near * samples + s, channels:CPAD, :] = jnp.zeros(
                (CPAD - channels, LANES), BF16
            )
    lane = lane_index(channels)
    sums = [jnp.zeros((channels, LANES), F32) for _ in sides]
    if count > 2:
        shifts = (2, 0)
    else:
        shifts = (jnp.where(col_place == 0, 2, 0),)
    for s in range(samples):
        for q in range(rows):
            y = jnp.where(upper, q, rows - 1 - q)
            row = channel_rows(latent, s, y, channels, rows)
            place = 2 * (s * rows + q)
            hit = (lane == place) | (lane == place + 1)
            sums = [
                jnp.where(hit, pltpu.roll(row, place + shift, 1), total)
                for shift, total in zip(shifts, sums)
            ]
    for copy in copies[1:5]:
        copy.wait()
    base = 2 * samples * rows
    for h in range(coarse_rows):
        line = coarse[:, h, :]
        right = jnp.broadcast_to(line[:, local_cols - 1 : local_cols], (channels, LANES))
        left = jnp.broadcast_to(line[:, 0:1], (channels, LANES))
        if count > 2:
            values = (right, left)
        else:
            values = (jnp.where(col_place == 0, right, left),)
        sums = [jnp.where(lane == base + h, v, t) for v, t in zip(values, sums)]
    for out, total in zip(sides, sums):
        out[0:channels, :] = total
        out[channels:CPAD, :] = jnp.zeros((CPAD - channels, LANES), F32)
    shared_out[0:channels, :] = weight_out[...].astype(F32)
    shared_out[channels : channels + 1, :] = bias_mid[...]
    shared_out[channels + 1 : CPAD, :] = jnp.zeros((CPAD - channels - 1, LANES), F32)
    for s in range(samples):
        steps_out[s : s + 1, :] = jnp.ones((1, LANES), F32) * steps[s].astype(F32)
    for copy in copies[5:]:
        copy.wait()


def blend(target, size):
    twice = 2.0 * target + (1.0 - FACTOR)
    lower = jnp.floor(twice * (1.0 / (2 * FACTOR)))
    fraction = (twice - lower * (2.0 * FACTOR)) * (1.0 / (2 * FACTOR))
    fraction = jnp.where(lower < 0.0, 0.0, fraction)
    return jnp.clip(lower, 0.0, size - 1.0), jnp.clip(lower + 1.0, 0.0, size - 1.0), fraction


def edge_parts(from_left, from_right, own, even):
    return (
        jnp.where(even, from_left, own),
        jnp.where(even, pltpu.roll(from_left, LANES - 1, 1), pltpu.roll(from_right, 1, 1)),
        jnp.where(even, own, from_right),
    )


def own_columns(lines, lane, samples, rows):
    own = jnp.zeros(lane.shape, F32)
    for (s, w), line in lines.items():
        at = 2 * (s * rows + w)
        first = line if at == 0 else pltpu.roll(line, at, 1)
        own = jnp.where(lane == at, first, own)
        own = jnp.where(lane == at + 1, pltpu.roll(line, (at + 2) % LANES, 1), own)
    return own


def shifted_lines(line, turned, lane):
    return (
        pltpu.roll(jnp.where(lane == LANES - 1, turned, line), 1, 1),
        line,
        pltpu.roll(jnp.where(lane == 0, turned, line), LANES - 1, 1),
    )


def stack_taps(lat, mean):
    parts = sum([[lat[i], mean[i]] for i in range(3)], [])
    return jnp.concatenate(parts, axis=0).astype(BF16)


def edge_first(weight, lat, mean, dims):
    col_place = lax.axis_index("col")
    stacked = stack_taps(
        [pltpu.roll(lat, LANES - 2 * i, 1) if i else lat for i in range(3)],
        [pltpu.roll(mean, LANES - 2 * i, 1) if i else mean for i in range(3)],
    )
    hidden = silu_of_half(jnp.dot(weight, stacked, preferred_element_type=F32))
    lane = lane_index(hidden.shape[0])
    side = col_place + lane % 2
    return jnp.where((side > 0) & (side < dims["col"]), hidden, 0.0).astype(BF16)


def store_hidden(hs, at, here, edge, turn, lane):
    turned = pltpu.roll(edge, (LANES - 1 - turn) % LANES, 1)
    left, middle, right = shifted_lines(here, turned, lane)
    hs[0, at] = left
    hs[1, at] = middle
    hs[2, at] = right


def second(own_mid, other_mid, bias, out_weight, lines):
    taps = [(tap_row(i), j) for i in range(3) for j in range(3)]
    weight = jnp.concatenate(
        [
            jnp.concatenate([ref[3 * i + j] for i, j in taps], axis=1)
            for ref in (own_mid, other_mid)
        ],
        axis=0,
    )
    stacked = jnp.concatenate(
        [
            jnp.concatenate([line(i, j) for line in lines], axis=1)
            for i in range(3)
            for j in range(3)
        ],
        axis=0,
    )
    value = jnp.dot(weight, stacked, preferred_element_type=F32)
    middle = silu_of_half(0.5 * value + bias).astype(BF16)
    return jnp.dot(out_weight, middle, preferred_element_type=F32)


def inner_kernel(
    dims,
    weight_mid,
    latent,
    coarse,
    weight_in,
    bias_in,
    weight_noise,
    steps,
    cols_matrix,
    other_mid,
    own_shared,
    other_shared,
    *rest,
):
    sides = rest[: dims["messages"]]
    (
        w1_out,
        lat_out,
        mean_lines,
        edge_lat_out,
        edge_mean_out,
        hs_out,
        bias_out,
        weight_out,
        net_out,
        mean_out,
        coef_out,
        own_mid,
        zl,
        zm,
        w1t,
        ce,
        hs,
        tr,
        ez,
        weight_sem,
    ) = rest[dims["messages"] :]
    fetch_weight = pltpu.make_async_copy(weight_mid, own_mid, weight_sem)
    fetch_weight.start()
    samples = latent.shape[0]
    channels, coarse_rows, local_cols = coarse.shape
    rows = latent.shape[1] // channels
    taps, deep, hidden = weight_in.shape
    half = rows // 2
    lat_rows = 3 * channels
    block = 2 * (lat_rows + 4)
    height = dims["row"] * rows
    row_place = lax.axis_index("row")
    col_place = lax.axis_index("col")
    lane = lane_index(CPAD)
    even = lane % 2 == 0

    w1t[...] = jnp.zeros(w1t.shape, F32)
    bias_terms = three_terms(0.5 * bias_in[...])
    noise_terms = three_terms(0.5 * weight_noise[...])
    for i in range(3):
        for j in range(3):
            tap = 0.5 * weight_in[3 * tap_row(i) + j].astype(F32)
            at = i * block + j * channels
            w1t[at : at + channels, :] = tap[0:channels]
            at += lat_rows + 4
            w1t[at : at + channels, :] = tap[channels:deep]
        at = i * block + lat_rows
        w1t[at : at + 1, :] = bias_terms[i]
        for j in range(3 - i):
            w1t[at + 1 + j : at + 2 + j, :] = noise_terms[i]
    first_weight = w1t[...].T.astype(BF16)
    w1_out[...] = first_weight

    lane_w = (lane // 2) % rows
    used = lane < 2 * samples * rows
    inside = used & (lane_w >= 2)

    def halo(side, ok):
        return jnp.where(inside & ok, pltpu.roll(side, 4, 1), 0.0)

    from_left = halo(sides[0][...], col_place > 0)
    from_right = halo(sides[-1][...], col_place < dims["col"] - 1)
    pad = jnp.zeros((CPAD - channels, LANES), F32)
    lines = {}
    for s in range(samples):
        for w in range(2, rows):
            line = channel_rows(latent, s, tile_row(w, rows), channels, rows)
            lines[s, w] = jnp.concatenate([line, pad], axis=0)
    own = own_columns(lines, lane, samples, rows)
    edge = edge_parts(from_left, from_right, own, even)

    ce[...] = jnp.zeros(ce.shape, F32)
    base = 2 * samples * rows
    for h in range(coarse_rows):
        at = h * CPAD
        ce[at : at + channels, 0:local_cols] = coarse[:, h, :]
        ce[at : at + CPAD, local_cols : local_cols + 1] = sides[0][:, base + h : base + h + 1]
        ce[at : at + CPAD, local_cols + 1 : local_cols + 2] = sides[-1][:, base + h : base + h + 1]
    blended = []
    for w in range(rows + 2):
        row = row_place * rows + tile_row(w, rows)
        first, following, fraction = blend(jnp.full((1, LANES), row.astype(F32)), coarse_rows)
        total = None
        for h in range(coarse_rows):
            weight = jnp.where(first == h, 1.0 - fraction, 0.0)
            weight += jnp.where(following == h, fraction, 0.0)
            if w < 2:
                weight = jnp.where((row >= 0) & (row < height), weight, 0.0)
            term = weight * ce[h * CPAD : (h + 1) * CPAD, :]
            total = term if total is None else total + term
        blended.append(total)
    group = local_cols + 2
    high, mid, low = three_terms(jnp.concatenate(blended, axis=0))
    cells = (high + pltpu.roll(mid, group, 1) + pltpu.roll(low, 2 * group, 1)).astype(BF16)
    cells = cells[:, 0 : cols_matrix.shape[0]]
    spread = jnp.dot(cells, cols_matrix[...], preferred_element_type=F32)

    def mean_line(w, j):
        return spread[w * CPAD : (w + 1) * CPAD, j * LANES : (j + 1) * LANES]

    zero_rows = jnp.zeros((4, LANES), F32)
    for w in range(rows + 2):
        if w >= 2:
            mean_out[w - 2] = mean_line(w, 1)
        if w < rows:
            for j in range(3):
                zm[w, j * channels : (j + 1) * channels, :] = mean_line(w, j)[0:channels]
            zm[w, lat_rows : lat_rows + 4, :] = zero_rows
    for j in range(3):
        at = j * channels
        total = jnp.zeros((CPAD, LANES), F32)
        for w in range(rows):
            total = jnp.where(used & (lane_w == w), mean_line(w, 3 + j), total)
        ez[1, at : at + channels, :] = total[0:channels]
        ez[0, at : at + channels, :] = edge[j][0:channels]
    ez[1, lat_rows : lat_rows + 4, :] = zero_rows

    ones = jnp.ones((1, LANES), F32)
    tails = []
    for s in range(samples):
        step = steps[s : s + 1, :]
        now = noise_level(step)
        ahead = noise_level(step + 1.0)
        tails.append(jnp.concatenate([ones, *three_terms(jnp.log(now) * 0.25)], axis=0))
        variance = now * now + sigma_data * sigma_data
        scale = jnp.sqrt(variance)
        inverse = 1.0 / jnp.sqrt(ahead * ahead + sigma_data * sigma_data)
        coef_out[s] = jnp.concatenate(
            [
                sigma_data * sigma_data / variance * scale,
                sigma_data * now / scale,
                ahead * inverse,
                inverse,
                jnp.zeros((4, LANES), F32),
            ],
            axis=0,
        )
    sample_of = lane_index(4) // (2 * rows)
    edge_tail = tails[0]
    for s in range(1, samples):
        edge_tail = jnp.where(sample_of == s, tails[s], edge_tail)
    ez[0, lat_rows : lat_rows + 4, :] = edge_tail

    for s in range(samples):
        for w in range(2, rows):
            turned = pltpu.roll(edge[1], (LANES - 1 - 2 * (s * rows + w)) % LANES, 1)
            moved = shifted_lines(lines[s, w], turned, lane)
            for j in range(3):
                zl[s, w - 2, j * channels : (j + 1) * channels, :] = moved[j][0:channels]
            zl[s, w - 2, lat_rows : lat_rows + 4, :] = tails[s]
    for s in range(samples):
        for w in range(2):
            lat_out[s, w] = zl[s, w]
    for w in range(4):
        mean_lines[w] = zm[w]
    edge_lat, edge_mean = ez[0], ez[1]
    edge_lat_out[...] = edge_lat
    edge_mean_out[...] = edge_mean

    edge_hidden = edge_first(first_weight, edge_lat, edge_mean, dims)
    lane_h = lane_index(hidden)
    for s in range(samples):
        stacked = jnp.concatenate(
            [
                stack_taps([zl[s, w - 2 + i] for i in range(3)], [zm[w + i] for i in range(3)])
                for w in range(2, half + 2)
            ],
            axis=1,
        )
        value = silu_of_half(jnp.dot(first_weight, stacked, preferred_element_type=F32))
        value = value.astype(BF16)
        for n in range(half):
            here = value[:, n * LANES : (n + 1) * LANES]
            turn = 2 * (s * rows + n + 2)
            store_hidden(hs, s * half + n, here, edge_hidden, turn, lane_h)
    for s in range(samples):
        for n in range(2):
            for j in range(3):
                hs_out[j, 2 * s + n] = hs[j, s * half + n]

    tr[...] = jnp.zeros(tr.shape, F32)
    tr[0:CPAD, 0:LANES] = own_shared[...]
    tr[0:CPAD, LANES:] = other_shared[...]
    bias = 0.5 * tr[...].T[:, channels : channels + 1]
    bias_out[...] = bias
    out_weight = tr[0:CPAD, :].astype(BF16)
    weight_out[...] = out_weight
    fetch_weight.wait()
    net = second(
        own_mid,
        other_mid,
        bias,
        out_weight,
        [
            functools.partial(lambda s, n, i, j: hs[j, s * half + n + i], s, n)
            for s in range(samples)
            for n in range(half - 2)
        ],
    )
    for n in range(samples * (half - 2)):
        net_out[n] = net[:, n * LANES : (n + 1) * LANES]


def outer_kernel(
    dims,
    rows_in,
    own_mid,
    other_mid,
    first_weight,
    lat_in,
    mean_lines,
    edge_lat_in,
    edge_mean_in,
    hs_in,
    bias,
    out_weight,
    net_in,
    *rest,
):
    corners = rest[: dims["messages"]]
    net_out, zl, hs, ez = rest[dims["messages"] :]
    samples = rows_in.shape[0] // 2
    rows = 8
    lat_rows = lat_in.shape[2] - 4
    channels = lat_rows // 3
    half = rows // 2
    height = dims["row"] * rows
    row_place = lax.axis_index("row")
    col_place = lax.axis_index("col")
    lane = lane_index(CPAD)
    even = lane % 2 == 0
    valid = []
    for w in range(2):
        row = row_place * rows + tile_row(w, rows)
        valid.append((row >= 0) & (row < height))
    lines = {}
    for s in range(samples):
        for w in range(2):
            lines[s, w] = jnp.where(valid[w], rows_in[w * samples + s].astype(F32), 0.0)
    lane_w = (lane // 2) % rows
    lane_row = row_place * rows + tile_row(lane_w, rows)
    inside = (lane < 2 * samples * rows) & (lane_w < 2) & (lane_row >= 0) & (lane_row < height)

    def halo(corner, ok):
        return jnp.where(inside & ok, pltpu.roll(corner, LANES - 2 * (rows - 2), 1), 0.0)

    from_left = halo(corners[0][...], col_place > 0)
    from_right = halo(corners[-1][...], col_place < dims["col"] - 1)
    own = own_columns(lines, lane, samples, rows)
    edge = edge_parts(from_left, from_right, own, even)
    for j in range(3):
        at = j * channels
        ez[at : at + channels, :] = edge[j][0:channels] + edge_lat_in[at : at + channels, :]
    ez[lat_rows : lat_rows + 4, :] = edge_lat_in[lat_rows : lat_rows + 4, :]
    for s in range(samples):
        for w in range(2):
            turned = pltpu.roll(edge[1], (LANES - 1 - 2 * (s * rows + w)) % LANES, 1)
            moved = shifted_lines(lines[s, w], turned, lane)
            for j in range(3):
                zl[s, w, j * channels : (j + 1) * channels, :] = moved[j][0:channels]
            zl[s, w, lat_rows : lat_rows + 4, :] = lat_in[s, 0, lat_rows : lat_rows + 4, :]

    weight = first_weight[...]
    edge_hidden = edge_first(weight, ez[...], edge_mean_in[...], dims)
    stacked = []
    for s in range(samples):
        lat = [zl[s, 0], zl[s, 1], lat_in[s, 0], lat_in[s, 1]]
        for w in range(2):
            stacked.append(stack_taps(lat[w : w + 3], [mean_lines[w + i] for i in range(3)]))
    value = jnp.dot(weight, jnp.concatenate(stacked, axis=1), preferred_element_type=F32)
    value = silu_of_half(value)
    lane_h = lane_index(value.shape[0])
    edge_row = ((lane_h // 2) % rows > 0) | valid[1]
    edge_hidden = jnp.where(edge_row, edge_hidden.astype(F32), 0.0).astype(BF16)
    for s in range(samples):
        for w in range(2):
            here = value[:, (2 * s + w) * LANES : (2 * s + w + 1) * LANES]
            if w == 0:
                here = jnp.where(valid[1], here, 0.0)
            store_hidden(
                hs, 2 * s + w, here.astype(BF16), edge_hidden, 2 * (s * rows + w), lane_h
            )

    def line(s, n, i, j):
        return hs[j, 2 * s + n + i] if n + i < 2 else hs_in[j, 2 * s + n + i - 2]

    net = second(
        own_mid,
        other_mid,
        bias[...],
        out_weight[...],
        [functools.partial(line, s, n) for s in range(samples) for n in range(2)],
    )
    rest_lines = half - 2
    for s in range(samples):
        for n in range(2):
            at = 2 * s + n
            net_out[s * half + n] = net[:, at * LANES : (at + 1) * LANES]
        for n in range(rest_lines):
            net_out[s * half + 2 + n] = net_in[s * rest_lines + n]


def finish_kernel(latent, fresh, own_net, other_net, mean, coef, fine, following):
    samples = latent.shape[0]
    rows = mean.shape[0]
    channels = latent.shape[1] // rows
    half = rows // 2
    upper = lax.axis_index("chan") == 0
    for s in range(samples):
        keep, gain, noise, inverse = (coef[s, n : n + 1, :] for n in range(4))
        for y in range(rows):
            place = s * half + (y if y < half else rows - 1 - y)
            own, other = own_net[place], other_net[place]
            net = jnp.where(upper, own, other) if y < half else jnp.where(upper, other, own)
            denoised = keep * channel_rows(latent, s, y, channels, rows) + gain * net[0:channels]
            at = pl.ds(y, channels, stride=rows)
            line = jnp.where(upper, y, rows - 1 - y)
            fine[s, at, :] = mean[line, 0:channels, :] + denoised
            following[s, at, :] = denoised * inverse + noise * channel_rows(
                fresh, s, y, channels, rows
            )


def on_device(
    dims,
    latent,
    fresh_noise,
    step_index,
    coarse,
    weight_in,
    bias_in,
    weight_noise,
    weight_mid,
    bias_mid,
    weight_out,
):
    samples, channels, rows, cols = latent.shape
    taps, hidden, deep = weight_in.shape
    half = rows // 2
    row_count, col_count = dims["row"], dims["col"]
    messages = dims["messages"]
    vmem = pl.BlockSpec(memory_space=pltpu.VMEM)
    struct = jax.ShapeDtypeStruct
    place = functools.partial(pltpu.with_memory_space_constraint, memory_space=pltpu.VMEM)

    far = functools.partial(pltpu.with_memory_space_constraint, memory_space=pltpu.HBM)
    anywhere = pl.BlockSpec(memory_space=pltpu.HBM)

    flat = latent.reshape(samples, channels * rows, cols)
    swap = [(0, 1), (1, 0)]
    other_mid = lax.ppermute(weight_mid, "chan", swap)
    group = coarse.shape[2] + 2
    depth = CPAD * ((3 * group + CPAD - 1) // CPAD)
    packed = pl.pallas_call(
        functools.partial(pack_kernel, dims),
        out_shape=[
            pltpu.VMEM(flat.shape, F32),
            pltpu.VMEM(coarse.shape, F32),
            pltpu.VMEM((taps, deep, hidden), BF16),
            pltpu.VMEM((1, hidden), F32),
            pltpu.VMEM((1, hidden), F32),
            pltpu.VMEM((8, LANES), F32),
            pltpu.VMEM((depth, 6 * LANES), BF16),
            pltpu.VMEM((2 * samples, CPAD, cols), BF16),
            pltpu.VMEM((CPAD, hidden // 2), F32),
        ]
        + [pltpu.VMEM((CPAD, LANES), F32)] * messages,
        in_specs=[anywhere] * 8,
        out_specs=[vmem] * (9 + messages),
        scratch_shapes=[
            pltpu.VMEM(weight_out.shape, BF16),
            pltpu.VMEM((1, hidden // 2), F32),
            pltpu.SMEM((samples,), jnp.int32),
            pltpu.SemaphoreType.DMA((8,)),
        ],
        compiler_params=LIMIT,
        name="pack",
    )(
        far(flat),
        far(coarse),
        far(weight_out),
        far(bias_mid.reshape(1, -1)),
        far(jnp.transpose(weight_in, (0, 2, 1))),
        far(bias_in.reshape(1, -1)),
        far(weight_noise.reshape(1, -1)),
        far(step_index),
    )
    prepared = [place(value) for value in packed[:7]]
    flat_near = prepared[0]
    rows_message, shared, side_messages = packed[7], packed[8], packed[9:]

    down = [(r, 0, r + 1, 0) for r in range(row_count - 1)]
    down += [(r + 1, 1, r, 1) for r in range(row_count - 1)]
    ends = [(row_count - 1, 0, row_count - 1, 1), (0, 1, 0, 0)]
    vertical = [(2 * a + b, 2 * c + d) for a, b, c, d in down + ends]
    sides, corners = [], []
    for n, message in enumerate(side_messages):
        if col_count > 2:
            step = 1 if n == 0 else -1
            columns = [(i, (i + step) % col_count) for i in range(col_count)]
        else:
            columns = [(i, col_count - 1 - i) for i in range(col_count)]
        sides.append(lax.ppermute(message, "col", columns))
        diagonal = [
            (2 * (a * col_count + i) + b, 2 * (c * col_count + k) + d)
            for a, b, c, d in down
            for i, k in columns
        ]
        diagonal += [
            (2 * (a * col_count + i) + b, 2 * (c * col_count + i) + d)
            for a, b, c, d in ends
            for i in range(col_count)
        ]
        corners.append(lax.ppermute(message, ("row", "col", "chan"), diagonal))
    rows_in = lax.ppermute(rows_message, ("row", "chan"), vertical)
    other_shared = lax.ppermute(shared, "chan", swap)

    other_mid = place(other_mid)
    lat_rows = 3 * channels + 4
    inner_lines = samples * (half - 2)
    inner = pl.pallas_call(
        functools.partial(inner_kernel, dims),
        out_shape=[
            pltpu.VMEM((hidden, 6 * lat_rows), BF16),
            pltpu.VMEM((samples, 2, lat_rows, cols), F32),
            pltpu.VMEM((4, lat_rows, cols), F32),
            pltpu.VMEM((lat_rows, cols), F32),
            pltpu.VMEM((lat_rows, cols), F32),
            pltpu.VMEM((3, 2 * samples, hidden, cols), BF16),
            pltpu.VMEM((hidden, 1), F32),
            pltpu.VMEM((CPAD, hidden), BF16),
            pltpu.VMEM((inner_lines, CPAD, cols), F32),
            pltpu.VMEM((rows, CPAD, cols), F32),
            pltpu.VMEM((samples, 8, cols), F32),
            pltpu.VMEM(weight_mid.shape, BF16),
        ],
        in_specs=[anywhere] + [vmem] * (10 + messages),
        out_specs=[vmem] * 12,
        scratch_shapes=[
            pltpu.VMEM((samples, rows - 2, lat_rows, cols), F32),
            pltpu.VMEM((rows, lat_rows, cols), F32),
            pltpu.VMEM((6 * lat_rows, hidden), F32),
            pltpu.VMEM((coarse.shape[1] * CPAD, LANES), F32),
            pltpu.VMEM((3, samples * half, hidden, cols), BF16),
            pltpu.VMEM((LANES, 2 * LANES), F32),
            pltpu.VMEM((2, lat_rows, cols), F32),
            pltpu.SemaphoreType.DMA,
        ],
        compiler_params=LIMIT,
        name="inner",
    )(
        far(weight_mid),
        *prepared,
        other_mid,
        place(shared),
        place(other_shared),
        *[place(side) for side in sides],
    )
    inner = [place(value) for value in inner]
    net = pl.pallas_call(
        functools.partial(outer_kernel, dims),
        out_shape=pltpu.VMEM((samples * half, CPAD, cols), F32),
        in_specs=[vmem] * (12 + messages),
        out_specs=vmem,
        scratch_shapes=[
            pltpu.VMEM((samples, 2, lat_rows, cols), F32),
            pltpu.VMEM((3, 2 * samples, hidden, cols), BF16),
            pltpu.VMEM((lat_rows, cols), F32),
        ],
        compiler_params=LIMIT,
        name="outer",
    )(
        place(rows_in),
        inner[11],
        other_mid,
        *inner[:9],
        *[place(corner) for corner in corners],
    )
    other_net = lax.ppermute(net, "chan", swap)
    results = pl.pallas_call(
        finish_kernel,
        out_shape=[struct(flat.shape, F32)] * 2,
        in_specs=[vmem] * 6,
        out_specs=[vmem] * 2,
        compiler_params=LIMIT,
        name="finish",
    )(
        flat_near,
        place(fresh_noise.reshape(flat.shape)),
        place(net),
        place(other_net),
        inner[9],
        inner[10],
    )
    return tuple(value.reshape(latent.shape) for value in results)


def solution(mesh):
    dims = {axis: mesh.shape[axis] for axis in ("row", "col", "chan")}
    dims["messages"] = 2 if dims["col"] > 2 else 1
    tile = P("ens", None, "row", "col")
    in_specs = (
        tile,
        tile,
        P("ens"),
        P("ens", None, "col"),
        P(),
        P(),
        P(),
        P(None, "chan", None),
        P("chan"),
        P(None, "chan"),
    )
    return jax.shard_map(
        functools.partial(on_device, dims),
        mesh=mesh,
        in_specs=in_specs,
        out_specs=(tile, tile),
        check_vma=False,
    )
```

time: 60.9 us -> 15.5 us (0.25)
  between operations: 14.4 us -> 0.68 us
  matrix products: 9.14 us -> 0 us
  starting transfers between devices: 14.9 us -> 6.2 us
  waiting for transfers between devices: 8.92 us -> 1.88 us
  Pallas kernels: 0 us -> 6.55 us
  blocking collectives: 6.31 us -> 0 us
  other arithmetic: 4.14 us -> 0 us
  local copies, waits for them, and re-layouts: 2.63 us -> 0.01 us
    dot_general x20 -> x0, matrix products: 9.14 us -> none  [the longest x17 7.96 us: conv_valid(): jnp.einsum('oi,siyx->soyx', weight[3 * offset_row + offset_col], window,...]
    ppermute x6, starting transfers between devices: 14.9 us -> 6.2 us  [the longest x1 2.59 us: on_device(): rows_in = lax.ppermute(rows_message, ('row', 'chan'), vertical)]
    ppermute x6, waiting for transfers between devices: 8.88 us -> 1.88 us  [the longest x1 1.26 us: on_device(): other_net = lax.ppermute(net, 'chan', swap)]
    pallas_call x0 -> x4, Pallas kernels: none -> 6.55 us  [the longest x1 2.99 us: on_device(): pl.pallas_call(functools.partial(inner_kernel, dims), out_shape=[pltpu.VM...]
    all_gather x3 -> x0, blocking collectives: 6.31 us -> none  [the longest x1 2.69 us: on_device(): network = lax.all_gather(half_network, 'chan', axis=3, tiled=True)]
    unnamed x13 -> x2, local copies, waits for them, and re-layouts: 1.2 us -> 0.01 us
    another operation x1 -> x0, other arithmetic: 0.9 us -> none
    add x2 -> x0, other arithmetic: 0.77 us -> none  [the longest x1 0.77 us: on_device(): bias_in[None, :, None, None]]
  transfers between devices with their start and end apart: 7 -> 6, of which waited for: 4 -> 2; matrix products, arithmetic and copies ran while one was open for 14% -> 0% of each run, Pallas kernels for 0% -> 28%
where the time goes in v3:
time: 15.5 us; the launch traced here: 15.3 us
  Pallas kernels  6.55 us (42%)
  starting transfers between devices  6.2 us (40%)
  waiting for transfers between devices  1.88 us (12%)
  between operations  0.68 us (4%)
    pallas_call x1, Pallas kernels, on_device(): pl.pallas_call(functools.partial(inner_kernel, dims), out_shape=[pltpu.VM...  2.99 us
    ppermute x1, starting transfers between devices, on_device(): rows_in = lax.ppermute(rows_message, ('row', 'chan'), vertical)  2.59 us
    ppermute x1, starting transfers between devices, on_device(): corners.append(lax.ppermute(message, ('row', 'col', 'chan'), diagonal))  1.55 us
    pallas_call x1, Pallas kernels, on_device(): pl.pallas_call(functools.partial(outer_kernel, dims), out_shape=pltpu.VME...  1.54 us
    ppermute x1, starting transfers between devices, on_device(): sides.append(lax.ppermute(message, 'col', columns))  1.49 us
    pallas_call x1, Pallas kernels, on_device(): pl.pallas_call(functools.partial(pack_kernel, dims), out_shape=[pltpu.VME...  1.28 us
    ppermute x1, waiting for transfers between devices, on_device(): other_net = lax.ppermute(net, 'chan', swap)  1.26 us
    pallas_call x1, Pallas kernels, on_device(): pl.pallas_call(finish_kernel, out_shape=[struct(flat.shape, F32)] * 2, in...  0.74 us
  transfers between devices with their start and end apart: 6, of which 2 were waited for; matrix products, arithmetic and copies ran while one was open for 0% of the time, Pallas kernels for 28%

profile of v3, /device:TPU:0, one launch (start us, length us, event | category | flops | bytes accessed | tf_op | source)
XLA Modules:
  0.0 15.3 jit_solution(8413016221619996591)
XLA Ops:
  0.6 0.6 %collective-permute-start.1 = (bf16[9,128,256]{2,1,0:T(8,128)(2,1)}, bf16[9,128,256]{2,1,0:T(8,128)(2,1)S(1)}, u32[]{:S(2)}, u32[]{:S(2)}) collective-permute-start(bf16[9,128,256]{2,1,0:T(8,128)(2,1)} %weight_mid.1), channel_id=1, source_target_pairs={{0,1},{1,0},{2,3},{3,2},{4,5},{5,4},{6,7},{7,6},{8,9},{9,8},{10,11... | collective-permute-start | bytes 1769480 | tf_op jit(solution)/shard_map/ppermute | solution.py:624
  1.2 1.3 %pack.1 = (f32[2,96,128]{2,1,0:T(8,128)S(1)}, f32[12,4,16]{2,1,0:T(4,128)S(1)}, bf16[9,24,256]{2,1,0:T(8,128)(2,1)S(1)}, f32[1,256]{1,0:T(1,128)S(1)}, f32[1,256...) custom-call(f32[2,96,128]{2,1,0:T(8,128)} %bitcast.10, ...), custom_call_target="tpu_custom_call" | custom-call | tf_op jit(solution)/shard_map/pack/pallas_call | solution.py:627
  2.5 2.6 %collective-permute-start = (bf16[4,16,128]{2,1,0:T(8,128)(2,1)S(1)}, bf16[4,16,128]{2,1,0:T(8,128)(2,1)S(1)}, u32[]{:S(2)}, u32[]{:S(2)}) collective-permute-start(bf16[4,16,128]{2,1,0:T(8,128)(2,1)S(1)} %get-tuple-element.27), channel_id=1, source_target_pairs={{0,4},{4,8},{8,12},{5,1},{9,5},{13,9},{12,13},{1,0},{2,6},{6,10},{... | collective-permute-start | bytes 49160 | tf_op jit(solution)/shard_map/ppermute | solution.py:688
  5.1 0.0 collective-permute-start.2
  5.1 1.5 %collective-permute-start.3 = (f32[16,128]{1,0:T(8,128)S(1)}, f32[16,128]{1,0:T(8,128)S(1)}, u32[]{:S(2)}, u32[]{:S(2)}) collective-permute-start(f32[16,128]{1,0:T(8,128)S(1)} %get-tuple-element.35), channel_id=1, source_target_pairs={{0,2},{2,0},{1,3},{3,1},{4,6},{6,4},{5,7},{7,5},{8,10},{10,8},{9,1... | collective-permute-start | bytes 24584 | tf_op jit(solution)/shard_map/ppermute | solution.py:676
  6.6 1.5 %collective-permute-start.4 = (f32[16,128]{1,0:T(8,128)S(1)}, f32[16,128]{1,0:T(8,128)S(1)}, u32[]{:S(2)}, u32[]{:S(2)}) collective-permute-start(f32[16,128]{1,0:T(8,128)S(1)} %get-tuple-element.35), channel_id=1, source_target_pairs={{0,6},{2,4},{4,10},{6,8},{8,14},{10,12},{5,3},{7,1},{9,7},{11,5},{... | collective-permute-start | bytes 24584 | tf_op jit(solution)/shard_map/ppermute | solution.py:687
  8.1 0.0 collective-permute-done.2.other_shared
  8.1 0.6 %collective-permute-done.3.rest_0_ = f32[16,128]{1,0:T(8,128)S(1)} collective-permute-done((f32[16,128]{1,0:T(8,128)S(1)}, f32[16,128]{1,0:T(8,128)S(1)}, u32[]{:S(2)}, u32[]{:S(2)}) %collective-permute-start.3) | collective-permute-done | bytes 8224 | tf_op jit(solution)/shard_map/ppermute | solution.py:676
  8.7 0.0 collective-permute-done.1.other_mid
  8.7 3.0 %inner.1 = (bf16[256,240]{1,0:T(8,128)(2,1)S(1)}, f32[2,2,40,128]{3,2,1,0:T(8,128)S(1)}, f32[4,40,128]{2,1,0:T(8,128)S(1)}, f32[40,128]{1,0:T(8,128)S(1)}, f32[4...) custom-call(bf16[9,128,256]{2,1,0:T(8,128)(2,1)} %weight_mid.1, ...), custom_call_target="tpu_custom_call" | custom-call | tf_op jit(solution)/shard_map/inner/pallas_call | solution.py:694
  11.7 0.0 collective-permute-done.4.rest_0_
  11.7 0.0 collective-permute-done.rows_in
  11.8 0.0 copy-start
  11.8 1.5 %outer.1.own_net = f32[8,16,128]{2,1,0:T(8,128)S(1)} custom-call(bf16[4,16,128]{2,1,0:T(8,128)(2,1)S(1)} %collective-permute-done.rows_in, bf16[9,128,256]{2,1,0:T(8,128)(2,1)S(1)} %get-tuple-element.36.own_mid, bf16[9,128,256]{2,1,0:T(8,128)(2,1)S(1)} %collective-permute-done.1.other_mid, bf16[256,240]{1,0:T(8,128)(2,1)S(1)} %get-tuple-element.37.first_weight, ...), custom_call_target="tpu_custom_call" | custom-call | tf_op jit(solution)/shard_map/outer/pallas_call | solution.py:733
  13.3 0.0 collective-permute-start.5
  13.3 1.3 %collective-permute-done.5.other_net = f32[8,16,128]{2,1,0:T(8,128)S(1)} collective-permute-done((f32[8,16,128]{2,1,0:T(8,128)S(1)}, f32[8,16,128]{2,1,0:T(8,128)S(1)}, u32[]{:S(2)}, u32[]{:S(2)}) %collective-permute-start.5) | collective-permute-done | bytes 65568 | tf_op jit(solution)/shard_map/ppermute | solution.py:752
  14.6 0.0 copy-done
  14.6 0.7 %finish.1 = (f32[2,96,128]{2,1,0:T(8,128)}, f32[2,96,128]{2,1,0:T(8,128)}) custom-call(f32[2,96,128]{2,1,0:T(8,128)S(1)} %get-tuple-element.26.latent, f32[2,96,128]{2,1,0:T(8,128)S(1)} %bitcast.8, f32[8,16,128]{2,1,0:T(8,128)S(1)} %outer.1.own_net, f32[8,16,128]{2,1,0:T(8,128)S(1)} %collective-permute-done.5.other_net, ...), custom_call_target="tpu_custom_call" | custom-call | tf_op jit(solution)/shard_map/finish/pallas_call | solution.py:753
Async XLA Ops:
  0.6 8.1 %collective-permute-start.1 = (bf16[9,128,256]{2,1,0:T(8,128)(2,1)}, bf16[9,128,256]{2,1,0:T(8,128)(2,1)S(1)}, u32[]{:S(2)}, u32[]{:S(2)}) collective-permute-start(bf16[9,128,256]{2,1,0:T(8,128)(2,1)} %weight_mid.1), channel_id=1, source_target_pairs={{0,1},{1,0},{2,3},{3,2},{4,5},{5,4},{6,7},{7,6},{8,9},{9,8},{10,11... | collective-permute-start | bytes 1769480 | tf_op jit(solution)/shard_map/ppermute | solution.py:624
  2.5 9.3 %collective-permute-start = (bf16[4,16,128]{2,1,0:T(8,128)(2,1)S(1)}, bf16[4,16,128]{2,1,0:T(8,128)(2,1)S(1)}, u32[]{:S(2)}, u32[]{:S(2)}) collective-permute-start(bf16[4,16,128]{2,1,0:T(8,128)(2,1)S(1)} %get-tuple-element.27), channel_id=1, source_target_pairs={{0,4},{4,8},{8,12},{5,1},{9,5},{13,9},{12,13},{1,0},{2,6},{6,10},{... | collective-permute-start | bytes 49160 | tf_op jit(solution)/shard_map/ppermute | solution.py:688
  5.1 3.0 %collective-permute-start.2 = (f32[16,128]{1,0:T(8,128)S(1)}, f32[16,128]{1,0:T(8,128)S(1)}, u32[]{:S(2)}, u32[]{:S(2)}) collective-permute-start(f32[16,128]{1,0:T(8,128)S(1)} %get-tuple-element.34.own_shared), channel_id=1, source_target_pairs={{0,1},{1,0},{2,3},{3,2},{4,5},{5,4},{6,7},{7,6},{8,9},{9,8},{10,11... | collective-permute-start | bytes 24584 | tf_op jit(solution)/shard_map/ppermute | solution.py:689
  5.1 3.7 %collective-permute-start.3 = (f32[16,128]{1,0:T(8,128)S(1)}, f32[16,128]{1,0:T(8,128)S(1)}, u32[]{:S(2)}, u32[]{:S(2)}) collective-permute-start(f32[16,128]{1,0:T(8,128)S(1)} %get-tuple-element.35), channel_id=1, source_target_pairs={{0,2},{2,0},{1,3},{3,1},{4,6},{6,4},{5,7},{7,5},{8,10},{10,8},{9,1... | collective-permute-start | bytes 24584 | tf_op jit(solution)/shard_map/ppermute | solution.py:676
  6.6 5.2 %collective-permute-start.4 = (f32[16,128]{1,0:T(8,128)S(1)}, f32[16,128]{1,0:T(8,128)S(1)}, u32[]{:S(2)}, u32[]{:S(2)}) collective-permute-start(f32[16,128]{1,0:T(8,128)S(1)} %get-tuple-element.35), channel_id=1, source_target_pairs={{0,6},{2,4},{4,10},{6,8},{8,14},{10,12},{5,3},{7,1},{9,7},{11,5},{... | collective-permute-start | bytes 24584 | tf_op jit(solution)/shard_map/ppermute | solution.py:687
  11.8 2.8 %copy-start = (f32[2,12,8,128]{3,2,1,0:T(8,128)S(1)}, f32[2,12,8,128]{3,2,1,0:T(8,128)}, u32[]{:S(2)}) copy-start(f32[2,12,8,128]{3,2,1,0:T(8,128)} %param.11) | copy-start | bytes 294916
  13.3 1.3 %collective-permute-start.5 = (f32[8,16,128]{2,1,0:T(8,128)S(1)}, f32[8,16,128]{2,1,0:T(8,128)S(1)}, u32[]{:S(2)}, u32[]{:S(2)}) collective-permute-start(f32[8,16,128]{2,1,0:T(8,128)S(1)} %outer.1.own_net), channel_id=1, source_target_pairs={{0,1},{1,0},{2,3},{3,2},{4,5},{5,4},{6,7},{7,6},{8,9},{9,8},{10,11... | collective-permute-start | bytes 196616 | tf_op jit(solution)/shard_map/ppermute | solution.py:752

commit v4 on v3

--- a/solution.py
+++ b/solution.py
@@ -7,6 +7,7 @@
 from jax.experimental.pallas import tpu as pltpu
 from jax.sharding import PartitionSpec as P
 
+
 STEPS = 18
 FACTOR = 8
 
@@ -19,6 +20,7 @@
 BF16 = jnp.bfloat16
 LANES = 128
 CPAD = 16
+ORDER = (1, 0, 2)
 LIMIT = pltpu.CompilerParams(vmem_limit_bytes=12 * 1024 * 1024)
 
 
@@ -67,6 +69,7 @@
     bias_in_far,
     weight_noise_far,
     steps_far,
+    weight_mid_far,
     latent,
     coarse,
     weight_in,
@@ -74,6 +77,7 @@
     weight_noise,
     steps_out,
     cols_matrix,
+    own_mid,
     rows_out,
     shared_out,
     *rest,
@@ -89,6 +93,7 @@
         (weight_in_far, weight_in),
         (bias_in_far, bias_in),
         (weight_noise_far, weight_noise),
+        (weight_mid_far, own_mid),
     )
     copies = [pltpu.make_async_copy(a, b, sem.at[n]) for n, (a, b) in enumerate(pairs)]
     for copy in copies:
@@ -189,7 +194,7 @@
     )
 
 
-def own_columns(lines, lane, samples, rows):
+def own_columns(lines, lane, rows):
     own = jnp.zeros(lane.shape, F32)
     for (s, w), line in lines.items():
         at = 2 * (s * rows + w)
@@ -224,16 +229,17 @@
     return jnp.where((side > 0) & (side < dims["col"]), hidden, 0.0).astype(BF16)
 
 
-def store_hidden(hs, at, here, edge, turn, lane):
-    turned = pltpu.roll(edge, (LANES - 1 - turn) % LANES, 1)
-    left, middle, right = shifted_lines(here, turned, lane)
-    hs[0, at] = left
-    hs[1, at] = middle
-    hs[2, at] = right
+def store_hidden(hs, lines, edge, lane):
+    for at, turn, here in lines:
+        hs[1, at] = here
+    for at, turn, here in lines:
+        turned = pltpu.roll(edge, (LANES - 1 - turn) % LANES, 1)
+        hs[0, at] = pltpu.roll(jnp.where(lane == LANES - 1, turned, here), 1, 1)
+        hs[2, at] = pltpu.roll(jnp.where(lane == 0, turned, here), LANES - 1, 1)
 
 
 def second(own_mid, other_mid, bias, out_weight, lines):
-    taps = [(tap_row(i), j) for i in range(3) for j in range(3)]
+    taps = [(tap_row(i), j) for j in ORDER for i in range(3)]
     weight = jnp.concatenate(
         [
             jnp.concatenate([ref[3 * i + j] for i, j in taps], axis=1)
@@ -244,8 +250,8 @@
     stacked = jnp.concatenate(
         [
             jnp.concatenate([line(i, j) for line in lines], axis=1)
+            for j in ORDER
             for i in range(3)
-            for j in range(3)
         ],
         axis=0,
     )
@@ -256,7 +262,6 @@
 
 def inner_kernel(
     dims,
-    weight_mid,
     latent,
     coarse,
     weight_in,
@@ -264,6 +269,7 @@
     weight_noise,
     steps,
     cols_matrix,
+    own_mid,
     other_mid,
     own_shared,
     other_shared,
@@ -282,7 +288,6 @@
         net_out,
         mean_out,
         coef_out,
-        own_mid,
         zl,
         zm,
         w1t,
@@ -290,14 +295,11 @@
         hs,
         tr,
         ez,
-        weight_sem,
     ) = rest[dims["messages"] :]
-    fetch_weight = pltpu.make_async_copy(weight_mid, own_mid, weight_sem)
-    fetch_weight.start()
     samples = latent.shape[0]
     channels, coarse_rows, local_cols = coarse.shape
     rows = latent.shape[1] // channels
-    taps, deep, hidden = weight_in.shape
+    _, deep, hidden = weight_in.shape
     half = rows // 2
     lat_rows = 3 * channels
     block = 2 * (lat_rows + 4)
@@ -306,6 +308,14 @@
     col_place = lax.axis_index("col")
     lane = lane_index(CPAD)
     even = lane % 2 == 0
+
+    tr[...] = jnp.zeros(tr.shape, F32)
+    tr[0:CPAD, 0:LANES] = own_shared[...]
+    tr[0:CPAD, LANES:] = other_shared[...]
+    bias = 0.5 * tr[...].T[:, channels : channels + 1]
+    bias_out[...] = bias
+    out_weight = tr[0:CPAD, :].astype(BF16)
+    weight_out[...] = out_weight
 
     w1t[...] = jnp.zeros(w1t.shape, F32)
     bias_terms = three_terms(0.5 * bias_in[...])
@@ -339,7 +349,7 @@
         for w in range(2, rows):
             line = channel_rows(latent, s, tile_row(w, rows), channels, rows)
             lines[s, w] = jnp.concatenate([line, pad], axis=0)
-    own = own_columns(lines, lane, samples, rows)
+    own = own_columns(lines, lane, rows)
     edge = edge_parts(from_left, from_right, own, even)
 
     ce[...] = jnp.zeros(ce.shape, F32)
@@ -432,6 +442,7 @@
 
     edge_hidden = edge_first(first_weight, edge_lat, edge_mean, dims)
     lane_h = lane_index(hidden)
+    hidden_lines = []
     for s in range(samples):
         stacked = jnp.concatenate(
             [
@@ -444,21 +455,13 @@
         value = value.astype(BF16)
         for n in range(half):
             here = value[:, n * LANES : (n + 1) * LANES]
-            turn = 2 * (s * rows + n + 2)
-            store_hidden(hs, s * half + n, here, edge_hidden, turn, lane_h)
+            hidden_lines.append((s * half + n, 2 * (s * rows + n + 2), here))
+    store_hidden(hs, hidden_lines, edge_hidden, lane_h)
     for s in range(samples):
         for n in range(2):
             for j in range(3):
                 hs_out[j, 2 * s + n] = hs[j, s * half + n]
 
-    tr[...] = jnp.zeros(tr.shape, F32)
-    tr[0:CPAD, 0:LANES] = own_shared[...]
-    tr[0:CPAD, LANES:] = other_shared[...]
-    bias = 0.5 * tr[...].T[:, channels : channels + 1]
-    bias_out[...] = bias
-    out_weight = tr[0:CPAD, :].astype(BF16)
-    weight_out[...] = out_weight
-    fetch_weight.wait()
     net = second(
         own_mid,
         other_mid,
@@ -519,7 +522,7 @@
 
     from_left = halo(corners[0][...], col_place > 0)
     from_right = halo(corners[-1][...], col_place < dims["col"] - 1)
-    own = own_columns(lines, lane, samples, rows)
+    own = own_columns(lines, lane, rows)
     edge = edge_parts(from_left, from_right, own, even)
     for j in range(3):
         at = j * channels
@@ -545,14 +548,14 @@
     lane_h = lane_index(value.shape[0])
     edge_row = ((lane_h // 2) % rows > 0) | valid[1]
     edge_hidden = jnp.where(edge_row, edge_hidden.astype(F32), 0.0).astype(BF16)
+    hidden_lines = []
     for s in range(samples):
         for w in range(2):
             here = value[:, (2 * s + w) * LANES : (2 * s + w + 1) * LANES]
             if w == 0:
                 here = jnp.where(valid[1], here, 0.0)
-            store_hidden(
-                hs, 2 * s + w, here.astype(BF16), edge_hidden, 2 * (s * rows + w), lane_h
-            )
+            hidden_lines.append((2 * s + w, 2 * (s * rows + w), here.astype(BF16)))
+    store_hidden(hs, hidden_lines, edge_hidden, lane_h)
 
     def line(s, n, i, j):
         return hs[j, 2 * s + n + i] if n + i < 2 else hs_in[j, 2 * s + n + i - 2]
@@ -634,17 +637,18 @@
             pltpu.VMEM((1, hidden), F32),
             pltpu.VMEM((8, LANES), F32),
             pltpu.VMEM((depth, 6 * LANES), BF16),
+            pltpu.VMEM(weight_mid.shape, BF16),
             pltpu.VMEM((2 * samples, CPAD, cols), BF16),
             pltpu.VMEM((CPAD, hidden // 2), F32),
         ]
         + [pltpu.VMEM((CPAD, LANES), F32)] * messages,
-        in_specs=[anywhere] * 8,
-        out_specs=[vmem] * (9 + messages),
+        in_specs=[anywhere] * 9,
+        out_specs=[vmem] * (10 + messages),
         scratch_shapes=[
             pltpu.VMEM(weight_out.shape, BF16),
             pltpu.VMEM((1, hidden // 2), F32),
             pltpu.SMEM((samples,), jnp.int32),
-            pltpu.SemaphoreType.DMA((8,)),
+            pltpu.SemaphoreType.DMA((9,)),
         ],
         compiler_params=LIMIT,
         name="pack",
@@ -657,10 +661,11 @@
         far(bias_in.reshape(1, -1)),
         far(weight_noise.reshape(1, -1)),
         far(step_index),
-    )
-    prepared = [place(value) for value in packed[:7]]
+        far(weight_mid),
+    )
+    prepared = [place(value) for value in packed[:8]]
     flat_near = prepared[0]
-    rows_message, shared, side_messages = packed[7], packed[8], packed[9:]
+    rows_message, shared, side_messages = packed[8], packed[9], packed[10:]
 
     down = [(r, 0, r + 1, 0) for r in range(row_count - 1)]
     down += [(r + 1, 1, r, 1) for r in range(row_count - 1)]
@@ -705,10 +710,9 @@
             pltpu.VMEM((inner_lines, CPAD, cols), F32),
             pltpu.VMEM((rows, CPAD, cols), F32),
             pltpu.VMEM((samples, 8, cols), F32),
-            pltpu.VMEM(weight_mid.shape, BF16),
         ],
-        in_specs=[anywhere] + [vmem] * (10 + messages),
-        out_specs=[vmem] * 12,
+        in_specs=[vmem] * (11 + messages),
+        out_specs=[vmem] * 11,
         scratch_shapes=[
             pltpu.VMEM((samples, rows - 2, lat_rows, cols), F32),
             pltpu.VMEM((rows, lat_rows, cols), F32),
@@ -717,12 +721,10 @@
             pltpu.VMEM((3, samples * half, hidden, cols), BF16),
             pltpu.VMEM((LANES, 2 * LANES), F32),
             pltpu.VMEM((2, lat_rows, cols), F32),
-            pltpu.SemaphoreType.DMA,
         ],
         compiler_params=LIMIT,
         name="inner",
     )(
-        far(weight_mid),
         *prepared,
         other_mid,
         place(shared),
@@ -744,7 +746,7 @@
         name="outer",
     )(
         place(rows_in),
-        inner[11],
+        prepared[7],
         other_mid,
         *inner[:9],
         *[place(corner) for corner in corners],
@@ -784,10 +786,10 @@
         P("chan"),
         P(None, "chan"),
     )
+
+    def body(*args):
+        return on_device(dims, *args)
+
     return jax.shard_map(
-        functools.partial(on_device, dims),
-        mesh=mesh,
-        in_specs=in_specs,
-        out_specs=(tile, tile),
-        check_vma=False,
-    )
+        body, mesh=mesh, in_specs=in_specs, out_specs=(tile, tile), check_vma=False
+    )

time: 15.5 us -> 14.4 us (0.929)
  Pallas kernels: 6.55 us -> 5.5 us
    pallas_call x1, Pallas kernels: 2.99 us -> 1.93 us  [on_device(): pl.pallas_call(functools.partial(inner_kernel, dims), out_shape=[pltpu.VM...]
  transfers between devices with their start and end apart: 6 -> 6, of which waited for: 2 -> 2; matrix products, arithmetic and copies ran while one was open for 0% -> 0% of each run, Pallas kernels for 28% -> 23%
where the time goes in v4:
time: 14.4 us; the launch traced here: 14.2 us
  starting transfers between devices  6.19 us (43%)
  Pallas kernels  5.5 us (38%)
  waiting for transfers between devices  1.88 us (13%)
  between operations  0.66 us (5%)
    ppermute x1, starting transfers between devices, on_device(): rows_in = lax.ppermute(rows_message, ('row', 'chan'), vertical)  2.59 us
    pallas_call x1, Pallas kernels, on_device(): pl.pallas_call(functools.partial(inner_kernel, dims), out_shape=[pltpu.VM...  1.93 us
    ppermute x1, starting transfers between devices, on_device(): corners.append(lax.ppermute(message, ('row', 'col', 'chan'), diagonal))  1.55 us
    ppermute x1, starting transfers between devices, on_device(): sides.append(lax.ppermute(message, 'col', columns))  1.49 us
    pallas_call x1, Pallas kernels, on_device(): pl.pallas_call(functools.partial(outer_kernel, dims), out_shape=pltpu.VME...  1.48 us
    pallas_call x1, Pallas kernels, on_device(): pl.pallas_call(functools.partial(pack_kernel, dims), out_shape=[pltpu.VME...  1.34 us
    ppermute x1, waiting for transfers between devices, on_device(): other_net = lax.ppermute(net, 'chan', swap)  1.26 us
    pallas_call x1, Pallas kernels, on_device(): pl.pallas_call(finish_kernel, out_shape=[struct(flat.shape, F32)] * 2, in...  0.74 us
  transfers between devices with their start and end apart: 6, of which 2 were waited for; matrix products, arithmetic and copies ran while one was open for 0% of the time, Pallas kernels for 23%

profile of v4, /device:TPU:0, one launch (start us, length us, event | category | flops | bytes accessed | tf_op | source)
XLA Modules:
  0.0 14.2 jit_solution(14487664229545399222)
XLA Ops:
  0.6 0.6 %collective-permute-start.1 = (bf16[9,128,256]{2,1,0:T(8,128)(2,1)}, bf16[9,128,256]{2,1,0:T(8,128)(2,1)S(1)}, u32[]{:S(2)}, u32[]{:S(2)}) collective-permute-start(bf16[9,128,256]{2,1,0:T(8,128)(2,1)} %weight_mid_far.1), channel_id=1, source_target_pairs={{0,1},{1,0},{2,3},{3,2},{4,5},{5,4},{6,7},{7,6},{8,9},{9,8},{10,11... | collective-permute-start | bytes 1769480 | tf_op jit(solution)/shard_map/ppermute | solution.py:627
  1.2 1.3 %pack.1 = (f32[2,96,128]{2,1,0:T(8,128)S(1)}, f32[12,4,16]{2,1,0:T(4,128)S(1)}, bf16[9,24,256]{2,1,0:T(8,128)(2,1)S(1)}, f32[1,256]{1,0:T(1,128)S(1)}, f32[1,256...) custom-call(f32[2,96,128]{2,1,0:T(8,128)} %bitcast.10, ...), custom_call_target="tpu_custom_call" | custom-call | tf_op jit(solution)/shard_map/pack/pallas_call | solution.py:630
  2.5 2.6 %collective-permute-start = (bf16[4,16,128]{2,1,0:T(8,128)(2,1)S(1)}, bf16[4,16,128]{2,1,0:T(8,128)(2,1)S(1)}, u32[]{:S(2)}, u32[]{:S(2)}) collective-permute-start(bf16[4,16,128]{2,1,0:T(8,128)(2,1)S(1)} %get-tuple-element.27), channel_id=1, source_target_pairs={{0,4},{4,8},{8,12},{5,1},{9,5},{13,9},{12,13},{1,0},{2,6},{6,10},{... | collective-permute-start | bytes 49160 | tf_op jit(solution)/shard_map/ppermute | solution.py:693
  5.1 0.0 collective-permute-start.2
  5.1 1.5 %collective-permute-start.3 = (f32[16,128]{1,0:T(8,128)S(1)}, f32[16,128]{1,0:T(8,128)S(1)}, u32[]{:S(2)}, u32[]{:S(2)}) collective-permute-start(f32[16,128]{1,0:T(8,128)S(1)} %get-tuple-element.36), channel_id=1, source_target_pairs={{0,2},{2,0},{1,3},{3,1},{4,6},{6,4},{5,7},{7,5},{8,10},{10,8},{9,1... | collective-permute-start | bytes 24584 | tf_op jit(solution)/shard_map/ppermute | solution.py:681
  6.6 1.5 %collective-permute-start.4 = (f32[16,128]{1,0:T(8,128)S(1)}, f32[16,128]{1,0:T(8,128)S(1)}, u32[]{:S(2)}, u32[]{:S(2)}) collective-permute-start(f32[16,128]{1,0:T(8,128)S(1)} %get-tuple-element.36), channel_id=1, source_target_pairs={{0,6},{2,4},{4,10},{6,8},{8,14},{10,12},{5,3},{7,1},{9,7},{11,5},{... | collective-permute-start | bytes 24584 | tf_op jit(solution)/shard_map/ppermute | solution.py:692
  8.2 0.0 collective-permute-done.2.other_shared
  8.2 0.6 %collective-permute-done.3.rest_0_ = f32[16,128]{1,0:T(8,128)S(1)} collective-permute-done((f32[16,128]{1,0:T(8,128)S(1)}, f32[16,128]{1,0:T(8,128)S(1)}, u32[]{:S(2)}, u32[]{:S(2)}) %collective-permute-start.3) | collective-permute-done | bytes 8224 | tf_op jit(solution)/shard_map/ppermute | solution.py:681
  8.8 0.0 collective-permute-done.1.other_mid
  8.8 1.9 %inner.1 = (bf16[256,240]{1,0:T(8,128)(2,1)S(1)}, f32[2,2,40,128]{3,2,1,0:T(8,128)S(1)}, f32[4,40,128]{2,1,0:T(8,128)S(1)}, f32[40,128]{1,0:T(8,128)S(1)}, f32[4...) custom-call(f32[2,96,128]{2,1,0:T(8,128)S(1)} %get-tuple-element.26., ...), custom_call_target="tpu_custom_call" | custom-call | tf_op jit(solution)/shard_map/inner/pallas_call | solution.py:699
  10.7 0.0 collective-permute-done.4.rest_0_
  10.7 0.0 collective-permute-done.rows_in
  10.7 0.0 copy-start
  10.7 1.5 %outer.1.own_net = f32[8,16,128]{2,1,0:T(8,128)S(1)} custom-call(bf16[4,16,128]{2,1,0:T(8,128)(2,1)S(1)} %collective-permute-done.rows_in, bf16[9,128,256]{2,1,0:T(8,128)(2,1)S(1)} %get-tuple-element.28.own_mid, bf16[9,128,256]{2,1,0:T(8,128)(2,1)S(1)} %collective-permute-done.1.other_mid, bf16[256,240]{1,0:T(8,128)(2,1)S(1)} %get-tuple-element.37.first_weight, ...), custom_call_target="tpu_custom_call" | custom-call | tf_op jit(solution)/shard_map/outer/pallas_call | solution.py:735
  12.2 0.0 collective-permute-start.5
  12.2 1.3 %collective-permute-done.5.other_net = f32[8,16,128]{2,1,0:T(8,128)S(1)} collective-permute-done((f32[8,16,128]{2,1,0:T(8,128)S(1)}, f32[8,16,128]{2,1,0:T(8,128)S(1)}, u32[]{:S(2)}, u32[]{:S(2)}) %collective-permute-start.5) | collective-permute-done | bytes 65568 | tf_op jit(solution)/shard_map/ppermute | solution.py:754
  13.5 0.0 copy-done
  13.5 0.7 %finish.1 = (f32[2,96,128]{2,1,0:T(8,128)}, f32[2,96,128]{2,1,0:T(8,128)}) custom-call(f32[2,96,128]{2,1,0:T(8,128)S(1)} %get-tuple-element.26.latent, f32[2,96,128]{2,1,0:T(8,128)S(1)} %bitcast.8, f32[8,16,128]{2,1,0:T(8,128)S(1)} %outer.1.own_net, f32[8,16,128]{2,1,0:T(8,128)S(1)} %collective-permute-done.5.other_net, ...), custom_call_target="tpu_custom_call" | custom-call | tf_op jit(solution)/shard_map/finish/pallas_call | solution.py:755
Async XLA Ops:
  0.6 8.2 %collective-permute-start.1 = (bf16[9,128,256]{2,1,0:T(8,128)(2,1)}, bf16[9,128,256]{2,1,0:T(8,128)(2,1)S(1)}, u32[]{:S(2)}, u32[]{:S(2)}) collective-permute-start(bf16[9,128,256]{2,1,0:T(8,128)(2,1)} %weight_mid_far.1), channel_id=1, source_target_pairs={{0,1},{1,0},{2,3},{3,2},{4,5},{5,4},{6,7},{7,6},{8,9},{9,8},{10,11... | collective-permute-start | bytes 1769480 | tf_op jit(solution)/shard_map/ppermute | solution.py:627
  2.5 8.2 %collective-permute-start = (bf16[4,16,128]{2,1,0:T(8,128)(2,1)S(1)}, bf16[4,16,128]{2,1,0:T(8,128)(2,1)S(1)}, u32[]{:S(2)}, u32[]{:S(2)}) collective-permute-start(bf16[4,16,128]{2,1,0:T(8,128)(2,1)S(1)} %get-tuple-element.27), channel_id=1, source_target_pairs={{0,4},{4,8},{8,12},{5,1},{9,5},{13,9},{12,13},{1,0},{2,6},{6,10},{... | collective-permute-start | bytes 49160 | tf_op jit(solution)/shard_map/ppermute | solution.py:693
  5.1 3.0 %collective-permute-start.2 = (f32[16,128]{1,0:T(8,128)S(1)}, f32[16,128]{1,0:T(8,128)S(1)}, u32[]{:S(2)}, u32[]{:S(2)}) collective-permute-start(f32[16,128]{1,0:T(8,128)S(1)} %get-tuple-element.35.own_shared), channel_id=1, source_target_pairs={{0,1},{1,0},{2,3},{3,2},{4,5},{5,4},{6,7},{7,6},{8,9},{9,8},{10,11... | collective-permute-start | bytes 24584 | tf_op jit(solution)/shard_map/ppermute | solution.py:694
  5.1 3.7 %collective-permute-start.3 = (f32[16,128]{1,0:T(8,128)S(1)}, f32[16,128]{1,0:T(8,128)S(1)}, u32[]{:S(2)}, u32[]{:S(2)}) collective-permute-start(f32[16,128]{1,0:T(8,128)S(1)} %get-tuple-element.36), channel_id=1, source_target_pairs={{0,2},{2,0},{1,3},{3,1},{4,6},{6,4},{5,7},{7,5},{8,10},{10,8},{9,1... | collective-permute-start | bytes 24584 | tf_op jit(solution)/shard_map/ppermute | solution.py:681
  6.6 4.1 %collective-permute-start.4 = (f32[16,128]{1,0:T(8,128)S(1)}, f32[16,128]{1,0:T(8,128)S(1)}, u32[]{:S(2)}, u32[]{:S(2)}) collective-permute-start(f32[16,128]{1,0:T(8,128)S(1)} %get-tuple-element.36), channel_id=1, source_target_pairs={{0,6},{2,4},{4,10},{6,8},{8,14},{10,12},{5,3},{7,1},{9,7},{11,5},{... | collective-permute-start | bytes 24584 | tf_op jit(solution)/shard_map/ppermute | solution.py:692
  10.7 2.8 %copy-start = (f32[2,12,8,128]{3,2,1,0:T(8,128)S(1)}, f32[2,12,8,128]{3,2,1,0:T(8,128)}, u32[]{:S(2)}) copy-start(f32[2,12,8,128]{3,2,1,0:T(8,128)} %param.11) | copy-start | bytes 294916
  12.2 1.3 %collective-permute-start.5 = (f32[8,16,128]{2,1,0:T(8,128)S(1)}, f32[8,16,128]{2,1,0:T(8,128)S(1)}, u32[]{:S(2)}, u32[]{:S(2)}) collective-permute-start(f32[8,16,128]{2,1,0:T(8,128)S(1)} %outer.1.own_net), channel_id=1, source_target_pairs={{0,1},{1,0},{2,3},{3,2},{4,5},{5,4},{6,7},{7,6},{8,9},{9,8},{10,11... | collective-permute-start | bytes 196616 | tf_op jit(solution)/shard_map/ppermute | solution.py:754

commit v5 on v4

--- a/solution.py
+++ b/solution.py
@@ -84,8 +84,15 @@
 ):
     sides = rest[: dims["messages"]]
     weight_out, bias_mid, steps, sem = rest[dims["messages"] :]
-    pairs = (
-        (latent_far, latent),
+    samples = latent.shape[0]
+    middle = latent.shape[1] // 2
+    pairs = [
+        (latent_far.at[s, pl.ds(p * middle, middle)], latent.at[s, pl.ds(p * middle, middle)])
+        for s in range(samples)
+        for p in range(2)
+    ]
+    first = len(pairs)
+    pairs += [
         (coarse_far, coarse),
         (weight_out_far, weight_out),
         (bias_mid_far, bias_mid),
@@ -94,11 +101,10 @@
         (bias_in_far, bias_in),
         (weight_noise_far, weight_noise),
         (weight_mid_far, own_mid),
-    )
+    ]
     copies = [pltpu.make_async_copy(a, b, sem.at[n]) for n, (a, b) in enumerate(pairs)]
     for copy in copies:
         copy.start()
-    samples = latent.shape[0]
     channels, coarse_rows, local_cols = coarse.shape
     rows = latent.shape[1] // channels
     count = dims["col"]
@@ -129,7 +135,8 @@
         weights += jnp.where(high == index, fraction, 0.0)
         cols_matrix[:, n * LANES : (n + 1) * LANES] = weights.astype(BF16)
 
-    copies[0].wait()
+    for copy in copies[:first]:
+        copy.wait()
     for near in range(2):
         y = jnp.where(upper, rows - 2 + near, 1 - near)
         for s in range(samples):
@@ -154,7 +161,7 @@
                 jnp.where(hit, pltpu.roll(row, place + shift, 1), total)
                 for shift, total in zip(shifts, sums)
             ]
-    for copy in copies[1:5]:
+    for copy in copies[first : first + 4]:
         copy.wait()
     base = 2 * samples * rows
     for h in range(coarse_rows):
@@ -174,7 +181,7 @@
     shared_out[channels + 1 : CPAD, :] = jnp.zeros((CPAD - channels - 1, LANES), F32)
     for s in range(samples):
         steps_out[s : s + 1, :] = jnp.ones((1, LANES), F32) * steps[s].astype(F32)
-    for copy in copies[5:]:
+    for copy in copies[first + 4 :]:
         copy.wait()
 
 
@@ -238,24 +245,31 @@
         hs[2, at] = pltpu.roll(jnp.where(lane == 0, turned, here), LANES - 1, 1)
 
 
-def second(own_mid, other_mid, bias, out_weight, lines):
-    taps = [(tap_row(i), j) for j in ORDER for i in range(3)]
-    weight = jnp.concatenate(
+def tap_weight(own_mid, other_mid, tap_rows):
+    taps = [(tap_row(i), j) for j in ORDER for i in tap_rows]
+    return jnp.concatenate(
         [
             jnp.concatenate([ref[3 * i + j] for i, j in taps], axis=1)
             for ref in (own_mid, other_mid)
         ],
         axis=0,
     )
+
+
+def section(own_mid, other_mid, tap_rows, lines):
     stacked = jnp.concatenate(
         [
             jnp.concatenate([line(i, j) for line in lines], axis=1)
             for j in ORDER
-            for i in range(3)
+            for i in tap_rows
         ],
         axis=0,
     )
-    value = jnp.dot(weight, stacked, preferred_element_type=F32)
+    weight = tap_weight(own_mid, other_mid, tap_rows)
+    return jnp.dot(weight, stacked, preferred_element_type=F32)
+
+
+def project(value, bias, out_weight):
     middle = silu_of_half(0.5 * value + bias).astype(BF16)
     return jnp.dot(out_weight, middle, preferred_element_type=F32)
 
@@ -462,17 +476,12 @@
             for j in range(3):
                 hs_out[j, 2 * s + n] = hs[j, s * half + n]
 
-    net = second(
-        own_mid,
-        other_mid,
-        bias,
-        out_weight,
-        [
-            functools.partial(lambda s, n, i, j: hs[j, s * half + n + i], s, n)
-            for s in range(samples)
-            for n in range(half - 2)
-        ],
-    )
+    lines = [
+        functools.partial(lambda s, n, i, j: hs[j, s * half + n + i], s, n)
+        for s in range(samples)
+        for n in range(half - 2)
+    ]
+    net = project(section(own_mid, other_mid, range(3), lines), bias, out_weight)
     for n in range(samples * (half - 2)):
         net_out[n] = net[:, n * LANES : (n + 1) * LANES]
 
@@ -494,7 +503,7 @@
     *rest,
 ):
     corners = rest[: dims["messages"]]
-    net_out, zl, hs, ez = rest[dims["messages"] :]
+    net_out, zl, hs, ez, part = rest[dims["messages"] :]
     samples = rows_in.shape[0] // 2
     rows = 8
     lat_rows = lat_in.shape[2] - 4
@@ -505,6 +514,17 @@
     col_place = lax.axis_index("col")
     lane = lane_index(CPAD)
     even = lane % 2 == 0
+
+    def known(n, s, i, j):
+        return hs_in[j, 2 * s + n + i - 2]
+
+    lower = [functools.partial(known, n, s) for n in range(2) for s in range(samples)]
+    early = section(own_mid, other_mid, (2,), lower)
+    wide = samples * LANES
+    later = early[:, wide:] + section(own_mid, other_mid, (1,), lower[samples:])
+    early = jnp.concatenate([early[:, 0:wide], later], axis=1)
+    part[...] = early
+
     valid = []
     for w in range(2):
         row = row_place * rows + tile_row(w, rows)
@@ -557,20 +577,19 @@
             hidden_lines.append((2 * s + w, 2 * (s * rows + w), here.astype(BF16)))
     store_hidden(hs, hidden_lines, edge_hidden, lane_h)
 
-    def line(s, n, i, j):
-        return hs[j, 2 * s + n + i] if n + i < 2 else hs_in[j, 2 * s + n + i - 2]
-
-    net = second(
-        own_mid,
-        other_mid,
-        bias[...],
-        out_weight[...],
-        [functools.partial(line, s, n) for s in range(samples) for n in range(2)],
-    )
+    def line(n, s, i, j):
+        return hs[j, 2 * s + n + i]
+
+    every = range(samples)
+    upper = [functools.partial(line, n, s) for n in range(2) for s in every]
+    value = part[...] + section(own_mid, other_mid, (0,), upper)
+    first = value[:, 0:wide] + section(own_mid, other_mid, (1,), upper[0:samples])
+    value = jnp.concatenate([first, value[:, wide:]], axis=1)
+    net = project(value, bias[...], out_weight[...])
     rest_lines = half - 2
     for s in range(samples):
         for n in range(2):
-            at = 2 * s + n
+            at = samples * n + s
             net_out[s * half + n] = net[:, at * LANES : (at + 1) * LANES]
         for n in range(rest_lines):
             net_out[s * half + 2 + n] = net_in[s * rest_lines + n]
@@ -648,7 +667,7 @@
             pltpu.VMEM(weight_out.shape, BF16),
             pltpu.VMEM((1, hidden // 2), F32),
             pltpu.SMEM((samples,), jnp.int32),
-            pltpu.SemaphoreType.DMA((9,)),
+            pltpu.SemaphoreType.DMA((8 + 2 * samples,)),
         ],
         compiler_params=LIMIT,
         name="pack",
@@ -741,6 +760,7 @@
             pltpu.VMEM((samples, 2, lat_rows, cols), F32),
             pltpu.VMEM((3, 2 * samples, hidden, cols), BF16),
             pltpu.VMEM((lat_rows, cols), F32),
+            pltpu.VMEM((hidden, 2 * samples * cols), F32),
         ],
         compiler_params=LIMIT,
         name="outer",

time: 14.4 us -> 14.3 us (level)
  no operation moved by 1% of the time
where the time goes in v5:
time: 14.3 us; the launch traced here: 14.2 us
  starting transfers between devices  6.19 us (43%)
  Pallas kernels  5.45 us (38%)
  waiting for transfers between devices  1.88 us (13%)
  between operations  0.66 us (5%)
    ppermute x1, starting transfers between devices, on_device(): rows_in = lax.ppermute(rows_message, ('row', 'chan'), vertical)  2.59 us
    pallas_call x1, Pallas kernels, on_device(): pl.pallas_call(functools.partial(inner_kernel, dims), out_shape=[pltpu.VM...  1.93 us
    ppermute x1, starting transfers between devices, on_device(): corners.append(lax.ppermute(message, ('row', 'col', 'chan'), diagonal))  1.55 us
    ppermute x1, starting transfers between devices, on_device(): sides.append(lax.ppermute(message, 'col', columns))  1.49 us
    pallas_call x1, Pallas kernels, on_device(): pl.pallas_call(functools.partial(outer_kernel, dims), out_shape=pltpu.VME...  1.42 us
    pallas_call x1, Pallas kernels, on_device(): pl.pallas_call(functools.partial(pack_kernel, dims), out_shape=[pltpu.VME...  1.36 us
    ppermute x1, waiting for transfers between devices, on_device(): other_net = lax.ppermute(net, 'chan', swap)  1.27 us
    pallas_call x1, Pallas kernels, on_device(): pl.pallas_call(finish_kernel, out_shape=[struct(flat.shape, F32)] * 2, in...  0.74 us
  transfers between devices with their start and end apart: 6, of which 2 were waited for; matrix products, arithmetic and copies ran while one was open for 0% of the time, Pallas kernels for 23%

profile of v5, /device:TPU:0, one launch (start us, length us, event | category | flops | bytes accessed | tf_op | source)
XLA Modules:
  0.0 14.2 jit_solution(890957265356036188)
XLA Ops:
  0.6 0.6 %collective-permute-start.1 = (bf16[9,128,256]{2,1,0:T(8,128)(2,1)}, bf16[9,128,256]{2,1,0:T(8,128)(2,1)S(1)}, u32[]{:S(2)}, u32[]{:S(2)}) collective-permute-start(bf16[9,128,256]{2,1,0:T(8,128)(2,1)} %weight_mid_far.1), channel_id=1, source_target_pairs={{0,1},{1,0},{2,3},{3,2},{4,5},{5,4},{6,7},{7,6},{8,9},{9,8},{10,11... | collective-permute-start | bytes 1769480 | tf_op jit(solution)/shard_map/ppermute | solution.py:646
  1.2 1.4 %pack.1 = (f32[2,96,128]{2,1,0:T(8,128)S(1)}, f32[12,4,16]{2,1,0:T(4,128)S(1)}, bf16[9,24,256]{2,1,0:T(8,128)(2,1)S(1)}, f32[1,256]{1,0:T(1,128)S(1)}, f32[1,256...) custom-call(f32[2,96,128]{2,1,0:T(8,128)} %bitcast.10, ...), custom_call_target="tpu_custom_call" | custom-call | tf_op jit(solution)/shard_map/pack/pallas_call | solution.py:649
  2.6 2.6 %collective-permute-start = (bf16[4,16,128]{2,1,0:T(8,128)(2,1)S(1)}, bf16[4,16,128]{2,1,0:T(8,128)(2,1)S(1)}, u32[]{:S(2)}, u32[]{:S(2)}) collective-permute-start(bf16[4,16,128]{2,1,0:T(8,128)(2,1)S(1)} %get-tuple-element.27), channel_id=1, source_target_pairs={{0,4},{4,8},{8,12},{5,1},{9,5},{13,9},{12,13},{1,0},{2,6},{6,10},{... | collective-permute-start | bytes 49160 | tf_op jit(solution)/shard_map/ppermute | solution.py:712
  5.1 0.0 collective-permute-start.2
  5.2 1.5 %collective-permute-start.3 = (f32[16,128]{1,0:T(8,128)S(1)}, f32[16,128]{1,0:T(8,128)S(1)}, u32[]{:S(2)}, u32[]{:S(2)}) collective-permute-start(f32[16,128]{1,0:T(8,128)S(1)} %get-tuple-element.36), channel_id=1, source_target_pairs={{0,2},{2,0},{1,3},{3,1},{4,6},{6,4},{5,7},{7,5},{8,10},{10,8},{9,1... | collective-permute-start | bytes 24584 | tf_op jit(solution)/shard_map/ppermute | solution.py:700
  6.6 1.5 %collective-permute-start.4 = (f32[16,128]{1,0:T(8,128)S(1)}, f32[16,128]{1,0:T(8,128)S(1)}, u32[]{:S(2)}, u32[]{:S(2)}) collective-permute-start(f32[16,128]{1,0:T(8,128)S(1)} %get-tuple-element.36), channel_id=1, source_target_pairs={{0,6},{2,4},{4,10},{6,8},{8,14},{10,12},{5,3},{7,1},{9,7},{11,5},{... | collective-permute-start | bytes 24584 | tf_op jit(solution)/shard_map/ppermute | solution.py:711
  8.2 0.0 collective-permute-done.2.other_shared
  8.2 0.6 %collective-permute-done.3.rest_0_ = f32[16,128]{1,0:T(8,128)S(1)} collective-permute-done((f32[16,128]{1,0:T(8,128)S(1)}, f32[16,128]{1,0:T(8,128)S(1)}, u32[]{:S(2)}, u32[]{:S(2)}) %collective-permute-start.3) | collective-permute-done | bytes 8224 | tf_op jit(solution)/shard_map/ppermute | solution.py:700
  8.8 0.0 collective-permute-done.1.other_mid
  8.8 1.9 %inner.1 = (bf16[256,240]{1,0:T(8,128)(2,1)S(1)}, f32[2,2,40,128]{3,2,1,0:T(8,128)S(1)}, f32[4,40,128]{2,1,0:T(8,128)S(1)}, f32[40,128]{1,0:T(8,128)S(1)}, f32[4...) custom-call(f32[2,96,128]{2,1,0:T(8,128)S(1)} %get-tuple-element.26., ...), custom_call_target="tpu_custom_call" | custom-call | tf_op jit(solution)/shard_map/inner/pallas_call | solution.py:718
  10.7 0.0 collective-permute-done.4.rest_0_
  10.7 0.0 collective-permute-done.rows_in
  10.7 0.0 copy-start
  10.8 1.4 %outer.1.own_net = f32[8,16,128]{2,1,0:T(8,128)S(1)} custom-call(bf16[4,16,128]{2,1,0:T(8,128)(2,1)S(1)} %collective-permute-done.rows_in, bf16[9,128,256]{2,1,0:T(8,128)(2,1)S(1)} %get-tuple-element.28.own_mid, bf16[9,128,256]{2,1,0:T(8,128)(2,1)S(1)} %collective-permute-done.1.other_mid, bf16[256,240]{1,0:T(8,128)(2,1)S(1)} %get-tuple-element.37.first_weight, ...), custom_call_target="tpu_custom_call" | custom-call | tf_op jit(solution)/shard_map/outer/pallas_call | solution.py:754
  12.2 0.0 collective-permute-start.5
  12.2 1.3 %collective-permute-done.5.other_net = f32[8,16,128]{2,1,0:T(8,128)S(1)} collective-permute-done((f32[8,16,128]{2,1,0:T(8,128)S(1)}, f32[8,16,128]{2,1,0:T(8,128)S(1)}, u32[]{:S(2)}, u32[]{:S(2)}) %collective-permute-start.5) | collective-permute-done | bytes 65568 | tf_op jit(solution)/shard_map/ppermute | solution.py:774
  13.4 0.0 copy-done
  13.4 0.7 %finish.1 = (f32[2,96,128]{2,1,0:T(8,128)}, f32[2,96,128]{2,1,0:T(8,128)}) custom-call(f32[2,96,128]{2,1,0:T(8,128)S(1)} %get-tuple-element.26.latent, f32[2,96,128]{2,1,0:T(8,128)S(1)} %bitcast.8, f32[8,16,128]{2,1,0:T(8,128)S(1)} %outer.1.own_net, f32[8,16,128]{2,1,0:T(8,128)S(1)} %collective-permute-done.5.other_net, ...), custom_call_target="tpu_custom_call" | custom-call | tf_op jit(solution)/shard_map/finish/pallas_call | solution.py:775
Async XLA Ops:
  0.6 8.2 %collective-permute-start.1 = (bf16[9,128,256]{2,1,0:T(8,128)(2,1)}, bf16[9,128,256]{2,1,0:T(8,128)(2,1)S(1)}, u32[]{:S(2)}, u32[]{:S(2)}) collective-permute-start(bf16[9,128,256]{2,1,0:T(8,128)(2,1)} %weight_mid_far.1), channel_id=1, source_target_pairs={{0,1},{1,0},{2,3},{3,2},{4,5},{5,4},{6,7},{7,6},{8,9},{9,8},{10,11... | collective-permute-start | bytes 1769480 | tf_op jit(solution)/shard_map/ppermute | solution.py:646
  2.6 8.2 %collective-permute-start = (bf16[4,16,128]{2,1,0:T(8,128)(2,1)S(1)}, bf16[4,16,128]{2,1,0:T(8,128)(2,1)S(1)}, u32[]{:S(2)}, u32[]{:S(2)}) collective-permute-start(bf16[4,16,128]{2,1,0:T(8,128)(2,1)S(1)} %get-tuple-element.27), channel_id=1, source_target_pairs={{0,4},{4,8},{8,12},{5,1},{9,5},{13,9},{12,13},{1,0},{2,6},{6,10},{... | collective-permute-start | bytes 49160 | tf_op jit(solution)/shard_map/ppermute | solution.py:712
  5.1 3.0 %collective-permute-start.2 = (f32[16,128]{1,0:T(8,128)S(1)}, f32[16,128]{1,0:T(8,128)S(1)}, u32[]{:S(2)}, u32[]{:S(2)}) collective-permute-start(f32[16,128]{1,0:T(8,128)S(1)} %get-tuple-element.35.own_shared), channel_id=1, source_target_pairs={{0,1},{1,0},{2,3},{3,2},{4,5},{5,4},{6,7},{7,6},{8,9},{9,8},{10,11... | collective-permute-start | bytes 24584 | tf_op jit(solution)/shard_map/ppermute | solution.py:713
  5.2 3.7 %collective-permute-start.3 = (f32[16,128]{1,0:T(8,128)S(1)}, f32[16,128]{1,0:T(8,128)S(1)}, u32[]{:S(2)}, u32[]{:S(2)}) collective-permute-start(f32[16,128]{1,0:T(8,128)S(1)} %get-tuple-element.36), channel_id=1, source_target_pairs={{0,2},{2,0},{1,3},{3,1},{4,6},{6,4},{5,7},{7,5},{8,10},{10,8},{9,1... | collective-permute-start | bytes 24584 | tf_op jit(solution)/shard_map/ppermute | solution.py:700
  6.6 4.1 %collective-permute-start.4 = (f32[16,128]{1,0:T(8,128)S(1)}, f32[16,128]{1,0:T(8,128)S(1)}, u32[]{:S(2)}, u32[]{:S(2)}) collective-permute-start(f32[16,128]{1,0:T(8,128)S(1)} %get-tuple-element.36), channel_id=1, source_target_pairs={{0,6},{2,4},{4,10},{6,8},{8,14},{10,12},{5,3},{7,1},{9,7},{11,5},{... | collective-permute-start | bytes 24584 | tf_op jit(solution)/shard_map/ppermute | solution.py:711
  10.7 2.7 %copy-start = (f32[2,12,8,128]{3,2,1,0:T(8,128)S(1)}, f32[2,12,8,128]{3,2,1,0:T(8,128)}, u32[]{:S(2)}) copy-start(f32[2,12,8,128]{3,2,1,0:T(8,128)} %param.11) | copy-start | bytes 294916
  12.2 1.3 %collective-permute-start.5 = (f32[8,16,128]{2,1,0:T(8,128)S(1)}, f32[8,16,128]{2,1,0:T(8,128)S(1)}, u32[]{:S(2)}, u32[]{:S(2)}) collective-permute-start(f32[8,16,128]{2,1,0:T(8,128)S(1)} %outer.1.own_net), channel_id=1, source_target_pairs={{0,1},{1,0},{2,3},{3,2},{4,5},{5,4},{6,7},{7,6},{8,9},{9,8},{10,11... | collective-permute-start | bytes 196616 | tf_op jit(solution)/shard_map/ppermute | solution.py:774

commit v6 on v5

--- a/solution.py
+++ b/solution.py
@@ -296,7 +296,7 @@
         mean_lines,
         edge_lat_out,
         edge_mean_out,
-        hs_out,
+        hs,
         bias_out,
         weight_out,
         net_out,
@@ -306,7 +306,6 @@
         zm,
         w1t,
         ce,
-        hs,
         tr,
         ez,
     ) = rest[dims["messages"] :]
@@ -471,10 +470,6 @@
             here = value[:, n * LANES : (n + 1) * LANES]
             hidden_lines.append((s * half + n, 2 * (s * rows + n + 2), here))
     store_hidden(hs, hidden_lines, edge_hidden, lane_h)
-    for s in range(samples):
-        for n in range(2):
-            for j in range(3):
-                hs_out[j, 2 * s + n] = hs[j, s * half + n]
 
     lines = [
         functools.partial(lambda s, n, i, j: hs[j, s * half + n + i], s, n)
@@ -516,7 +511,7 @@
     even = lane % 2 == 0
 
     def known(n, s, i, j):
-        return hs_in[j, 2 * s + n + i - 2]
+        return hs_in[j, s * half + n + i - 2]
 
     lower = [functools.partial(known, n, s) for n in range(2) for s in range(samples)]
     early = section(own_mid, other_mid, (2,), lower)
@@ -723,7 +718,7 @@
             pltpu.VMEM((4, lat_rows, cols), F32),
             pltpu.VMEM((lat_rows, cols), F32),
             pltpu.VMEM((lat_rows, cols), F32),
-            pltpu.VMEM((3, 2 * samples, hidden, cols), BF16),
+            pltpu.VMEM((3, samples * half, hidden, cols), BF16),
             pltpu.VMEM((hidden, 1), F32),
             pltpu.VMEM((CPAD, hidden), BF16),
             pltpu.VMEM((inner_lines, CPAD, cols), F32),
@@ -737,7 +732,6 @@
             pltpu.VMEM((rows, lat_rows, cols), F32),
             pltpu.VMEM((6 * lat_rows, hidden), F32),
             pltpu.VMEM((coarse.shape[1] * CPAD, LANES), F32),
-            pltpu.VMEM((3, samples * half, hidden, cols), BF16),
             pltpu.VMEM((LANES, 2 * LANES), F32),
             pltpu.VMEM((2, lat_rows, cols), F32),
         ],

time: 14.3 us -> 14.4 us (level)
  no operation moved by 1% of the time
where the time goes in v6:
time: 14.4 us; the launch traced here: 14.2 us
  starting transfers between devices  6.19 us (43%)
  Pallas kernels  5.49 us (38%)
  waiting for transfers between devices  1.88 us (13%)
  between operations  0.66 us (5%)
    ppermute x1, starting transfers between devices, on_device(): rows_in = lax.ppermute(rows_message, ('row', 'chan'), vertical)  2.59 us
    pallas_call x1, Pallas kernels, on_device(): pl.pallas_call(functools.partial(inner_kernel, dims), out_shape=[pltpu.VM...  1.97 us
    ppermute x1, starting transfers between devices, on_device(): corners.append(lax.ppermute(message, ('row', 'col', 'chan'), diagonal))  1.55 us
    ppermute x1, starting transfers between devices, on_device(): sides.append(lax.ppermute(message, 'col', columns))  1.49 us
    pallas_call x1, Pallas kernels, on_device(): pl.pallas_call(functools.partial(outer_kernel, dims), out_shape=pltpu.VME...  1.42 us
    pallas_call x1, Pallas kernels, on_device(): pl.pallas_call(functools.partial(pack_kernel, dims), out_shape=[pltpu.VME...  1.36 us
    ppermute x1, waiting for transfers between devices, on_device(): other_net = lax.ppermute(net, 'chan', swap)  1.27 us
    pallas_call x1, Pallas kernels, on_device(): pl.pallas_call(finish_kernel, out_shape=[struct(flat.shape, F32)] * 2, in...  0.74 us
  transfers between devices with their start and end apart: 6, of which 2 were waited for; matrix products, arithmetic and copies ran while one was open for 0% of the time, Pallas kernels for 23%

profile of v6, /device:TPU:0, one launch (start us, length us, event | category | flops | bytes accessed | tf_op | source)
XLA Modules:
  0.0 14.2 jit_solution(8904954326896283399)
XLA Ops:
  0.6 0.6 %collective-permute-start.1 = (bf16[9,128,256]{2,1,0:T(8,128)(2,1)}, bf16[9,128,256]{2,1,0:T(8,128)(2,1)S(1)}, u32[]{:S(2)}, u32[]{:S(2)}) collective-permute-start(bf16[9,128,256]{2,1,0:T(8,128)(2,1)} %weight_mid_far.1), channel_id=1, source_target_pairs={{0,1},{1,0},{2,3},{3,2},{4,5},{5,4},{6,7},{7,6},{8,9},{9,8},{10,11... | collective-permute-start | bytes 1769480 | tf_op jit(solution)/shard_map/ppermute | solution.py:641
  1.2 1.4 %pack.1 = (f32[2,96,128]{2,1,0:T(8,128)S(1)}, f32[12,4,16]{2,1,0:T(4,128)S(1)}, bf16[9,24,256]{2,1,0:T(8,128)(2,1)S(1)}, f32[1,256]{1,0:T(1,128)S(1)}, f32[1,256...) custom-call(f32[2,96,128]{2,1,0:T(8,128)} %bitcast.10, ...), custom_call_target="tpu_custom_call" | custom-call | tf_op jit(solution)/shard_map/pack/pallas_call | solution.py:644
  2.6 2.6 %collective-permute-start = (bf16[4,16,128]{2,1,0:T(8,128)(2,1)S(1)}, bf16[4,16,128]{2,1,0:T(8,128)(2,1)S(1)}, u32[]{:S(2)}, u32[]{:S(2)}) collective-permute-start(bf16[4,16,128]{2,1,0:T(8,128)(2,1)S(1)} %get-tuple-element.27), channel_id=1, source_target_pairs={{0,4},{4,8},{8,12},{5,1},{9,5},{13,9},{12,13},{1,0},{2,6},{6,10},{... | collective-permute-start | bytes 49160 | tf_op jit(solution)/shard_map/ppermute | solution.py:707
  5.1 0.0 collective-permute-start.2
  5.2 1.5 %collective-permute-start.3 = (f32[16,128]{1,0:T(8,128)S(1)}, f32[16,128]{1,0:T(8,128)S(1)}, u32[]{:S(2)}, u32[]{:S(2)}) collective-permute-start(f32[16,128]{1,0:T(8,128)S(1)} %get-tuple-element.36), channel_id=1, source_target_pairs={{0,2},{2,0},{1,3},{3,1},{4,6},{6,4},{5,7},{7,5},{8,10},{10,8},{9,1... | collective-permute-start | bytes 24584 | tf_op jit(solution)/shard_map/ppermute | solution.py:695
  6.6 1.5 %collective-permute-start.4 = (f32[16,128]{1,0:T(8,128)S(1)}, f32[16,128]{1,0:T(8,128)S(1)}, u32[]{:S(2)}, u32[]{:S(2)}) collective-permute-start(f32[16,128]{1,0:T(8,128)S(1)} %get-tuple-element.36), channel_id=1, source_target_pairs={{0,6},{2,4},{4,10},{6,8},{8,14},{10,12},{5,3},{7,1},{9,7},{11,5},{... | collective-permute-start | bytes 24584 | tf_op jit(solution)/shard_map/ppermute | solution.py:706
  8.2 0.0 collective-permute-done.2.other_shared
  8.2 0.6 %collective-permute-done.3.rest_0_ = f32[16,128]{1,0:T(8,128)S(1)} collective-permute-done((f32[16,128]{1,0:T(8,128)S(1)}, f32[16,128]{1,0:T(8,128)S(1)}, u32[]{:S(2)}, u32[]{:S(2)}) %collective-permute-start.3) | collective-permute-done | bytes 8224 | tf_op jit(solution)/shard_map/ppermute | solution.py:695
  8.8 0.0 collective-permute-done.1.other_mid
  8.8 2.0 %inner.1 = (bf16[256,240]{1,0:T(8,128)(2,1)S(1)}, f32[2,2,40,128]{3,2,1,0:T(8,128)S(1)}, f32[4,40,128]{2,1,0:T(8,128)S(1)}, f32[40,128]{1,0:T(8,128)S(1)}, f32[4...) custom-call(f32[2,96,128]{2,1,0:T(8,128)S(1)} %get-tuple-element.26., ...), custom_call_target="tpu_custom_call" | custom-call | tf_op jit(solution)/shard_map/inner/pallas_call | solution.py:713
  10.8 0.0 collective-permute-done.4.rest_0_
  10.8 0.0 collective-permute-done.rows_in
  10.8 0.0 copy-start
  10.8 1.4 %outer.1.own_net = f32[8,16,128]{2,1,0:T(8,128)S(1)} custom-call(bf16[4,16,128]{2,1,0:T(8,128)(2,1)S(1)} %collective-permute-done.rows_in, bf16[9,128,256]{2,1,0:T(8,128)(2,1)S(1)} %get-tuple-element.28.own_mid, bf16[9,128,256]{2,1,0:T(8,128)(2,1)S(1)} %collective-permute-done.1.other_mid, bf16[256,240]{1,0:T(8,128)(2,1)S(1)} %get-tuple-element.37.first_weight, ...), custom_call_target="tpu_custom_call" | custom-call | tf_op jit(solution)/shard_map/outer/pallas_call | solution.py:748
  12.2 0.0 collective-permute-start.5
  12.2 1.3 %collective-permute-done.5.other_net = f32[8,16,128]{2,1,0:T(8,128)S(1)} collective-permute-done((f32[8,16,128]{2,1,0:T(8,128)S(1)}, f32[8,16,128]{2,1,0:T(8,128)S(1)}, u32[]{:S(2)}, u32[]{:S(2)}) %collective-permute-start.5) | collective-permute-done | bytes 65568 | tf_op jit(solution)/shard_map/ppermute | solution.py:768
  13.5 0.0 copy-done
  13.5 0.7 %finish.1 = (f32[2,96,128]{2,1,0:T(8,128)}, f32[2,96,128]{2,1,0:T(8,128)}) custom-call(f32[2,96,128]{2,1,0:T(8,128)S(1)} %get-tuple-element.26.latent, f32[2,96,128]{2,1,0:T(8,128)S(1)} %bitcast.8, f32[8,16,128]{2,1,0:T(8,128)S(1)} %outer.1.own_net, f32[8,16,128]{2,1,0:T(8,128)S(1)} %collective-permute-done.5.other_net, ...), custom_call_target="tpu_custom_call" | custom-call | tf_op jit(solution)/shard_map/finish/pallas_call | solution.py:769
Async XLA Ops:
  0.6 8.2 %collective-permute-start.1 = (bf16[9,128,256]{2,1,0:T(8,128)(2,1)}, bf16[9,128,256]{2,1,0:T(8,128)(2,1)S(1)}, u32[]{:S(2)}, u32[]{:S(2)}) collective-permute-start(bf16[9,128,256]{2,1,0:T(8,128)(2,1)} %weight_mid_far.1), channel_id=1, source_target_pairs={{0,1},{1,0},{2,3},{3,2},{4,5},{5,4},{6,7},{7,6},{8,9},{9,8},{10,11... | collective-permute-start | bytes 1769480 | tf_op jit(solution)/shard_map/ppermute | solution.py:641
  2.6 8.2 %collective-permute-start = (bf16[4,16,128]{2,1,0:T(8,128)(2,1)S(1)}, bf16[4,16,128]{2,1,0:T(8,128)(2,1)S(1)}, u32[]{:S(2)}, u32[]{:S(2)}) collective-permute-start(bf16[4,16,128]{2,1,0:T(8,128)(2,1)S(1)} %get-tuple-element.27), channel_id=1, source_target_pairs={{0,4},{4,8},{8,12},{5,1},{9,5},{13,9},{12,13},{1,0},{2,6},{6,10},{... | collective-permute-start | bytes 49160 | tf_op jit(solution)/shard_map/ppermute | solution.py:707
  5.1 3.0 %collective-permute-start.2 = (f32[16,128]{1,0:T(8,128)S(1)}, f32[16,128]{1,0:T(8,128)S(1)}, u32[]{:S(2)}, u32[]{:S(2)}) collective-permute-start(f32[16,128]{1,0:T(8,128)S(1)} %get-tuple-element.35.own_shared), channel_id=1, source_target_pairs={{0,1},{1,0},{2,3},{3,2},{4,5},{5,4},{6,7},{7,6},{8,9},{9,8},{10,11... | collective-permute-start | bytes 24584 | tf_op jit(solution)/shard_map/ppermute | solution.py:708
  5.2 3.7 %collective-permute-start.3 = (f32[16,128]{1,0:T(8,128)S(1)}, f32[16,128]{1,0:T(8,128)S(1)}, u32[]{:S(2)}, u32[]{:S(2)}) collective-permute-start(f32[16,128]{1,0:T(8,128)S(1)} %get-tuple-element.36), channel_id=1, source_target_pairs={{0,2},{2,0},{1,3},{3,1},{4,6},{6,4},{5,7},{7,5},{8,10},{10,8},{9,1... | collective-permute-start | bytes 24584 | tf_op jit(solution)/shard_map/ppermute | solution.py:695
  6.6 4.1 %collective-permute-start.4 = (f32[16,128]{1,0:T(8,128)S(1)}, f32[16,128]{1,0:T(8,128)S(1)}, u32[]{:S(2)}, u32[]{:S(2)}) collective-permute-start(f32[16,128]{1,0:T(8,128)S(1)} %get-tuple-element.36), channel_id=1, source_target_pairs={{0,6},{2,4},{4,10},{6,8},{8,14},{10,12},{5,3},{7,1},{9,7},{11,5},{... | collective-permute-start | bytes 24584 | tf_op jit(solution)/shard_map/ppermute | solution.py:706
  10.8 2.7 %copy-start = (f32[2,12,8,128]{3,2,1,0:T(8,128)S(1)}, f32[2,12,8,128]{3,2,1,0:T(8,128)}, u32[]{:S(2)}) copy-start(f32[2,12,8,128]{3,2,1,0:T(8,128)} %param.11) | copy-start | bytes 294916
  12.2 1.3 %collective-permute-start.5 = (f32[8,16,128]{2,1,0:T(8,128)S(1)}, f32[8,16,128]{2,1,0:T(8,128)S(1)}, u32[]{:S(2)}, u32[]{:S(2)}) collective-permute-start(f32[8,16,128]{2,1,0:T(8,128)S(1)} %outer.1.own_net), channel_id=1, source_target_pairs={{0,1},{1,0},{2,3},{3,2},{4,5},{5,4},{6,7},{7,6},{8,9},{9,8},{10,11... | collective-permute-start | bytes 196616 | tf_op jit(solution)/shard_map/ppermute | solution.py:768

commit v7 on v6

--- a/solution.py
+++ b/solution.py
@@ -100,11 +100,12 @@
         (weight_in_far, weight_in),
         (bias_in_far, bias_in),
         (weight_noise_far, weight_noise),
-        (weight_mid_far, own_mid),
     ]
     copies = [pltpu.make_async_copy(a, b, sem.at[n]) for n, (a, b) in enumerate(pairs)]
-    for copy in copies:
+    big = pltpu.make_async_copy(weight_mid_far, own_mid, sem.at[len(pairs)])
+    for copy in copies[:first] + [big] + copies[first:]:
         copy.start()
+    copies.append(big)
     channels, coarse_rows, local_cols = coarse.shape
     rows = latent.shape[1] // channels
     count = dims["col"]

time: 14.4 us -> 14.3 us (level)
  no operation moved by 1% of the time
where the time goes in v7:
time: 14.3 us; the launch traced here: 14.2 us
  starting transfers between devices  6.19 us (43%)
  Pallas kernels  5.44 us (38%)
  waiting for transfers between devices  1.88 us (13%)
  between operations  0.66 us (5%)
    ppermute x1, starting transfers between devices, on_device(): rows_in = lax.ppermute(rows_message, ('row', 'chan'), vertical)  2.59 us
    pallas_call x1, Pallas kernels, on_device(): pl.pallas_call(functools.partial(inner_kernel, dims), out_shape=[pltpu.VM...  1.97 us
    ppermute x1, starting transfers between devices, on_device(): corners.append(lax.ppermute(message, ('row', 'col', 'chan'), diagonal))  1.55 us
    ppermute x1, starting transfers between devices, on_device(): sides.append(lax.ppermute(message, 'col', columns))  1.49 us
    pallas_call x1, Pallas kernels, on_device(): pl.pallas_call(functools.partial(outer_kernel, dims), out_shape=pltpu.VME...  1.42 us
    pallas_call x1, Pallas kernels, on_device(): pl.pallas_call(functools.partial(pack_kernel, dims), out_shape=[pltpu.VME...  1.31 us
    ppermute x1, waiting for transfers between devices, on_device(): other_net = lax.ppermute(net, 'chan', swap)  1.27 us
    pallas_call x1, Pallas kernels, on_device(): pl.pallas_call(finish_kernel, out_shape=[struct(flat.shape, F32)] * 2, in...  0.74 us
  transfers between devices with their start and end apart: 6, of which 2 were waited for; matrix products, arithmetic and copies ran while one was open for 0% of the time, Pallas kernels for 23%

profile of v7, /device:TPU:0, one launch (start us, length us, event | category | flops | bytes accessed | tf_op | source)
XLA Modules:
  0.0 14.2 jit_solution(14152193252918431015)
XLA Ops:
  0.6 0.6 %collective-permute-start.1 = (bf16[9,128,256]{2,1,0:T(8,128)(2,1)}, bf16[9,128,256]{2,1,0:T(8,128)(2,1)S(1)}, u32[]{:S(2)}, u32[]{:S(2)}) collective-permute-start(bf16[9,128,256]{2,1,0:T(8,128)(2,1)} %weight_mid_far.1), channel_id=1, source_target_pairs={{0,1},{1,0},{2,3},{3,2},{4,5},{5,4},{6,7},{7,6},{8,9},{9,8},{10,11... | collective-permute-start | bytes 1769480 | tf_op jit(solution)/shard_map/ppermute | solution.py:642
  1.2 1.3 %pack.1 = (f32[2,96,128]{2,1,0:T(8,128)S(1)}, f32[12,4,16]{2,1,0:T(4,128)S(1)}, bf16[9,24,256]{2,1,0:T(8,128)(2,1)S(1)}, f32[1,256]{1,0:T(1,128)S(1)}, f32[1,256...) custom-call(f32[2,96,128]{2,1,0:T(8,128)} %bitcast.10, ...), custom_call_target="tpu_custom_call" | custom-call | tf_op jit(solution)/shard_map/pack/pallas_call | solution.py:645
  2.5 2.6 %collective-permute-start = (bf16[4,16,128]{2,1,0:T(8,128)(2,1)S(1)}, bf16[4,16,128]{2,1,0:T(8,128)(2,1)S(1)}, u32[]{:S(2)}, u32[]{:S(2)}) collective-permute-start(bf16[4,16,128]{2,1,0:T(8,128)(2,1)S(1)} %get-tuple-element.27), channel_id=1, source_target_pairs={{0,4},{4,8},{8,12},{5,1},{9,5},{13,9},{12,13},{1,0},{2,6},{6,10},{... | collective-permute-start | bytes 49160 | tf_op jit(solution)/shard_map/ppermute | solution.py:708
  5.1 0.0 collective-permute-start.2
  5.1 1.5 %collective-permute-start.3 = (f32[16,128]{1,0:T(8,128)S(1)}, f32[16,128]{1,0:T(8,128)S(1)}, u32[]{:S(2)}, u32[]{:S(2)}) collective-permute-start(f32[16,128]{1,0:T(8,128)S(1)} %get-tuple-element.36), channel_id=1, source_target_pairs={{0,2},{2,0},{1,3},{3,1},{4,6},{6,4},{5,7},{7,5},{8,10},{10,8},{9,1... | collective-permute-start | bytes 24584 | tf_op jit(solution)/shard_map/ppermute | solution.py:696
  6.6 1.5 %collective-permute-start.4 = (f32[16,128]{1,0:T(8,128)S(1)}, f32[16,128]{1,0:T(8,128)S(1)}, u32[]{:S(2)}, u32[]{:S(2)}) collective-permute-start(f32[16,128]{1,0:T(8,128)S(1)} %get-tuple-element.36), channel_id=1, source_target_pairs={{0,6},{2,4},{4,10},{6,8},{8,14},{10,12},{5,3},{7,1},{9,7},{11,5},{... | collective-permute-start | bytes 24584 | tf_op jit(solution)/shard_map/ppermute | solution.py:707
  8.1 0.0 collective-permute-done.2.other_shared
  8.1 0.6 %collective-permute-done.3.rest_0_ = f32[16,128]{1,0:T(8,128)S(1)} collective-permute-done((f32[16,128]{1,0:T(8,128)S(1)}, f32[16,128]{1,0:T(8,128)S(1)}, u32[]{:S(2)}, u32[]{:S(2)}) %collective-permute-start.3) | collective-permute-done | bytes 8224 | tf_op jit(solution)/shard_map/ppermute | solution.py:696
  8.8 0.0 collective-permute-done.1.other_mid
  8.8 2.0 %inner.1 = (bf16[256,240]{1,0:T(8,128)(2,1)S(1)}, f32[2,2,40,128]{3,2,1,0:T(8,128)S(1)}, f32[4,40,128]{2,1,0:T(8,128)S(1)}, f32[40,128]{1,0:T(8,128)S(1)}, f32[4...) custom-call(f32[2,96,128]{2,1,0:T(8,128)S(1)} %get-tuple-element.26., ...), custom_call_target="tpu_custom_call" | custom-call | tf_op jit(solution)/shard_map/inner/pallas_call | solution.py:714
  10.7 0.0 collective-permute-done.4.rest_0_
  10.7 0.0 collective-permute-done.rows_in
  10.7 0.0 copy-start
  10.7 1.4 %outer.1.own_net = f32[8,16,128]{2,1,0:T(8,128)S(1)} custom-call(bf16[4,16,128]{2,1,0:T(8,128)(2,1)S(1)} %collective-permute-done.rows_in, bf16[9,128,256]{2,1,0:T(8,128)(2,1)S(1)} %get-tuple-element.28.own_mid, bf16[9,128,256]{2,1,0:T(8,128)(2,1)S(1)} %collective-permute-done.1.other_mid, bf16[256,240]{1,0:T(8,128)(2,1)S(1)} %get-tuple-element.37.first_weight, ...), custom_call_target="tpu_custom_call" | custom-call | tf_op jit(solution)/shard_map/outer/pallas_call | solution.py:749
  12.2 0.0 collective-permute-start.5
  12.2 1.3 %collective-permute-done.5.other_net = f32[8,16,128]{2,1,0:T(8,128)S(1)} collective-permute-done((f32[8,16,128]{2,1,0:T(8,128)S(1)}, f32[8,16,128]{2,1,0:T(8,128)S(1)}, u32[]{:S(2)}, u32[]{:S(2)}) %collective-permute-start.5) | collective-permute-done | bytes 65568 | tf_op jit(solution)/shard_map/ppermute | solution.py:769
  13.4 0.0 copy-done
  13.4 0.7 %finish.1 = (f32[2,96,128]{2,1,0:T(8,128)}, f32[2,96,128]{2,1,0:T(8,128)}) custom-call(f32[2,96,128]{2,1,0:T(8,128)S(1)} %get-tuple-element.26.latent, f32[2,96,128]{2,1,0:T(8,128)S(1)} %bitcast.8, f32[8,16,128]{2,1,0:T(8,128)S(1)} %outer.1.own_net, f32[8,16,128]{2,1,0:T(8,128)S(1)} %collective-permute-done.5.other_net, ...), custom_call_target="tpu_custom_call" | custom-call | tf_op jit(solution)/shard_map/finish/pallas_call | solution.py:770
Async XLA Ops:
  0.6 8.1 %collective-permute-start.1 = (bf16[9,128,256]{2,1,0:T(8,128)(2,1)}, bf16[9,128,256]{2,1,0:T(8,128)(2,1)S(1)}, u32[]{:S(2)}, u32[]{:S(2)}) collective-permute-start(bf16[9,128,256]{2,1,0:T(8,128)(2,1)} %weight_mid_far.1), channel_id=1, source_target_pairs={{0,1},{1,0},{2,3},{3,2},{4,5},{5,4},{6,7},{7,6},{8,9},{9,8},{10,11... | collective-permute-start | bytes 1769480 | tf_op jit(solution)/shard_map/ppermute | solution.py:642
  2.5 8.2 %collective-permute-start = (bf16[4,16,128]{2,1,0:T(8,128)(2,1)S(1)}, bf16[4,16,128]{2,1,0:T(8,128)(2,1)S(1)}, u32[]{:S(2)}, u32[]{:S(2)}) collective-permute-start(bf16[4,16,128]{2,1,0:T(8,128)(2,1)S(1)} %get-tuple-element.27), channel_id=1, source_target_pairs={{0,4},{4,8},{8,12},{5,1},{9,5},{13,9},{12,13},{1,0},{2,6},{6,10},{... | collective-permute-start | bytes 49160 | tf_op jit(solution)/shard_map/ppermute | solution.py:708
  5.1 3.0 %collective-permute-start.2 = (f32[16,128]{1,0:T(8,128)S(1)}, f32[16,128]{1,0:T(8,128)S(1)}, u32[]{:S(2)}, u32[]{:S(2)}) collective-permute-start(f32[16,128]{1,0:T(8,128)S(1)} %get-tuple-element.35.own_shared), channel_id=1, source_target_pairs={{0,1},{1,0},{2,3},{3,2},{4,5},{5,4},{6,7},{7,6},{8,9},{9,8},{10,11... | collective-permute-start | bytes 24584 | tf_op jit(solution)/shard_map/ppermute | solution.py:709
  5.1 3.7 %collective-permute-start.3 = (f32[16,128]{1,0:T(8,128)S(1)}, f32[16,128]{1,0:T(8,128)S(1)}, u32[]{:S(2)}, u32[]{:S(2)}) collective-permute-start(f32[16,128]{1,0:T(8,128)S(1)} %get-tuple-element.36), channel_id=1, source_target_pairs={{0,2},{2,0},{1,3},{3,1},{4,6},{6,4},{5,7},{7,5},{8,10},{10,8},{9,1... | collective-permute-start | bytes 24584 | tf_op jit(solution)/shard_map/ppermute | solution.py:696
  6.6 4.1 %collective-permute-start.4 = (f32[16,128]{1,0:T(8,128)S(1)}, f32[16,128]{1,0:T(8,128)S(1)}, u32[]{:S(2)}, u32[]{:S(2)}) collective-permute-start(f32[16,128]{1,0:T(8,128)S(1)} %get-tuple-element.36), channel_id=1, source_target_pairs={{0,6},{2,4},{4,10},{6,8},{8,14},{10,12},{5,3},{7,1},{9,7},{11,5},{... | collective-permute-start | bytes 24584 | tf_op jit(solution)/shard_map/ppermute | solution.py:707
  10.7 2.7 %copy-start = (f32[2,12,8,128]{3,2,1,0:T(8,128)S(1)}, f32[2,12,8,128]{3,2,1,0:T(8,128)}, u32[]{:S(2)}) copy-start(f32[2,12,8,128]{3,2,1,0:T(8,128)} %param.11) | copy-start | bytes 294916
  12.2 1.3 %collective-permute-start.5 = (f32[8,16,128]{2,1,0:T(8,128)S(1)}, f32[8,16,128]{2,1,0:T(8,128)S(1)}, u32[]{:S(2)}, u32[]{:S(2)}) collective-permute-start(f32[8,16,128]{2,1,0:T(8,128)S(1)} %outer.1.own_net), channel_id=1, source_target_pairs={{0,1},{1,0},{2,3},{3,2},{4,5},{5,4},{6,7},{7,6},{8,9},{9,8},{10,11... | collective-permute-start | bytes 196616 | tf_op jit(solution)/shard_map/ppermute | solution.py:769
